TPU v7x, 32 devices: a whole 2x2x4 slice. The times are simulated.
32 devices in a mesh: dp: 8 (over z, x), tensor: 4 (over y, core).
Axes of the slice: x: 2, y: 2, z: 4, core: 2. Of those that a mesh axis runs over, the one named last changes fastest.
Arguments:
- tokens: bfloat16 [8192, 768], P('dp'), may hold values from -6 to 6
- row_length: int32 [48], replicated, may hold values from 128 to 256, as said below
- row_group: int32 [48], replicated, may hold values from 0 to 7, as said below
- row_step: int32 [48], replicated, may hold values from 0 to 999
- time_table: bfloat16 [1000, 768], replicated, may hold values from -3 to 3
- norm1_gain: float32 [768], replicated, may hold values from 0.1 to 1.9
- norm1_bias: float32 [768], replicated, may hold values from -1.75 to 1.75
- w_qkv: bfloat16 [768, 3, 768], P(None, None, 'tensor'), may hold values from -0.21875 to 0.21875
- w_out: bfloat16 [768, 768], P('tensor'), may hold values from -2.5 to 2.5
- norm2_gain: float32 [768], replicated, may hold values from 0.1 to 1.9
- norm2_bias: float32 [768], replicated, may hold values from -1.75 to 1.75
- w_up: bfloat16 [768, 3072], P(None, 'tensor'), may hold values from -0.21875 to 0.21875
- up_bias: float32 [3072], P('tensor'), may hold values from -3 to 3
- w_down: bfloat16 [3072, 768], P('tensor'), may hold values from -0.21875 to 0.21875
- down_bias: float32 [768], replicated, may hold values from -1.75 to 1.75
- cotangent: bfloat16 [8192, 768], P('dp'), may hold values from -6 to 6
Outputs:
- block_output: bfloat16 [8192, 768], P('dp')
- input_grad: bfloat16 [8192, 768], P('dp')
- time_grad: float32 [1000, 768], P(None, 'tensor')
- gain1_grad: float32 [768], replicated
- bias1_grad: float32 [768], replicated
- qkv_grad: float32 [768, 3, 768], P(None, None, 'tensor')
- out_proj_grad: float32 [768, 768], P('tensor')
- gain2_grad: float32 [768], replicated
- bias2_grad: float32 [768], replicated
- up_grad: float32 [768, 3072], P(None, 'tensor')
- up_bias_grad: float32 [3072], P('tensor')
- down_grad: float32 [3072, 768], P('tensor')
- down_bias_grad: float32 [768], replicated
Inputs may be any that keep to these rules, and one draw needn't show every extreme that they name: `row_length`: each row holds 128 or 256 tokens. `row_group`: the rows of each group hold 1024 tokens in all, of which 0 to 4 rows have 2 * 128 tokens; both ends of that range are reached.
All inputs are finite; a program needn't handle non-finite values.
Results may differ from a plain program's by a relative error of at most 0.019.
Values may be sent and summed in bfloat16 or wider, within the bound.
No kernel may reach another device: no remote copies, remote signals or barrier semaphores. Data moves between devices by JAX's collectives and lax.ppermute only.
A program may use at most 128 MiB of HBM per device.

v0:
```python
import jax
import jax.numpy as jnp
from jax import lax
from jax.sharding import PartitionSpec as P

HEAD_DIM = 64
SHORT = 128
BLOCK = 512


EPS = 1e-05
NEG = -1000000000.0


def normalize(values, gain, bias):
    row_mean = jnp.mean(values, axis=-1, keepdims=True)
    centred = values - row_mean
    variance = jnp.mean(centred * centred, axis=-1, keepdims=True)
    return centred * lax.rsqrt(variance + EPS) * gain + bias


def exact_gelu(values):
    return jax.nn.gelu(values, approximate=False)


def contract(left, right, left_dim, right_dim):
    return lax.dot_general(
        left, right, (((left_dim,), (right_dim,)), ((), ())), preferred_element_type=jnp.float32
    )


def row_offsets(row_length, row_group):
    row_number = jnp.arange(row_length.shape[0], dtype=jnp.int32)
    order_key = jnp.where(row_length > SHORT, 0, row_length.shape[0]) + row_number
    same_group = row_group[:, None] == row_group[None, :]
    earlier = same_group & (order_key[None, :] < order_key[:, None])
    return jnp.sum(jnp.where(earlier, row_length[None, :], 0), axis=1)


def token_rows(offsets, row_length, row_group, row_step, group_index, count):
    row_number = jnp.arange(row_length.shape[0], dtype=jnp.int32)
    position = jnp.arange(count, dtype=jnp.int32)
    member = (
        (row_group[None, :] == group_index)
        & (position[:, None] >= offsets[None, :])
        & (position[:, None] < (offsets + row_length)[None, :])
    )
    token_row = jnp.sum(jnp.where(member, row_number[None, :], 0), axis=1)
    token_step = jnp.sum(jnp.where(member, row_step[None, :], 0), axis=1)
    return (token_row, token_step)


def shards(
    tokens,
    row_length,
    row_group,
    row_step,
    time_table,
    norm1_gain,
    norm1_bias,
    w_qkv,
    w_out,
    norm2_gain,
    norm2_bias,
    w_up,
    up_bias,
    w_down,
    down_bias,
    cotangent,
):
    count, width = tokens.shape
    blocks = count // BLOCK
    width_local = w_out.shape[0]
    heads_local = width_local // HEAD_DIM
    scale_factor = HEAD_DIM ** (-0.5)
    qkv_weight = w_qkv.reshape(width, 3 * width_local)
    offsets = row_offsets(row_length, row_group)
    token_row, token_step = token_rows(
        offsets, row_length, row_group, row_step, lax.axis_index("dp"), count
    )
    block_rows = token_row.reshape(blocks, BLOCK)
    allowed = block_rows[:, None, :, None] == block_rows[:, None, None, :]
    hidden_in = tokens.astype(jnp.float32) + jnp.take(time_table, token_step, axis=0).astype(
        jnp.float32
    )

    def attend_forward(source):
        normed, norm_back = jax.vjp(normalize, source, norm1_gain, norm1_bias)
        normed_low = normed.astype(jnp.bfloat16)
        projected = jnp.dot(normed_low, qkv_weight, preferred_element_type=jnp.float32).astype(
            jnp.bfloat16
        )
        split = projected.reshape(blocks, BLOCK, 3, heads_local, HEAD_DIM)
        query_block, key_block, value_block = (split[:, :, 0], split[:, :, 1], split[:, :, 2])
        scores = (
            jnp.einsum(
                "bqhd,bkhd->bhqk", query_block, key_block, preferred_element_type=jnp.float32
            )
            * scale_factor
        )
        scores = jnp.where(allowed, scores, NEG)
        log_total = jax.nn.logsumexp(scores, axis=-1, keepdims=True)
        attention = jnp.exp(scores - log_total)
        context = jnp.einsum(
            "bhqk,bkhd->bqhd",
            attention.astype(jnp.bfloat16),
            value_block,
            preferred_element_type=jnp.float32,
        )
        context = context.reshape(count, width_local).astype(jnp.bfloat16)
        return (normed_low, norm_back, query_block, key_block, value_block, attention, context)

    def expand_forward(source):
        normed, norm_back = jax.vjp(normalize, source, norm2_gain, norm2_bias)
        normed_low = normed.astype(jnp.bfloat16)
        pre_act = jnp.dot(normed_low, w_up, preferred_element_type=jnp.float32) + up_bias
        activated, gelu_back = jax.vjp(exact_gelu, pre_act)
        return (normed_low, norm_back, gelu_back, activated.astype(jnp.bfloat16))

    forward_attn = attend_forward(hidden_in)
    attended = lax.psum(
        jnp.dot(forward_attn[6], w_out, preferred_element_type=jnp.float32).astype(jnp.bfloat16),
        "tensor",
    ).astype(jnp.float32)
    residual = hidden_in + attended
    forward_mlp = expand_forward(residual)
    expanded = lax.psum(
        jnp.dot(forward_mlp[3], w_down, preferred_element_type=jnp.float32).astype(jnp.bfloat16),
        "tensor",
    ).astype(jnp.float32)
    block_output = (residual + expanded + down_bias).astype(jnp.bfloat16)
    grad_out = cotangent.astype(jnp.float32)
    residual_again, grad_anchor = lax.optimization_barrier((residual, grad_out))
    saved_mlp = expand_forward(residual_again)
    normed_two, norm2_back, gelu_back, activated = saved_mlp
    grad_down_bias = jnp.sum(grad_out, axis=0)
    grad_w_down = contract(activated, cotangent, 0, 0)
    grad_act = contract(cotangent, w_down, 1, 1)
    (grad_pre,) = gelu_back(grad_act)
    grad_up_bias = jnp.sum(grad_pre, axis=0)
    grad_pre_low = grad_pre.astype(jnp.bfloat16)
    grad_w_up = contract(normed_two, grad_pre_low, 0, 0)
    grad_normed2 = lax.psum(
        contract(grad_pre_low, w_up, 1, 1).astype(jnp.bfloat16), "tensor"
    ).astype(jnp.float32)
    grad_resid_norm, grad_gain2, grad_bias2 = norm2_back(grad_normed2)
    grad_residual = grad_out + grad_resid_norm
    hidden_again, residual_anchor = lax.optimization_barrier((hidden_in, grad_residual))
    saved_attn = attend_forward(hidden_again)
    normed_low, norm1_back, query_block, key_block, value_block, attention, context = saved_attn
    grad_res_low = grad_residual.astype(jnp.bfloat16)
    grad_w_out = contract(context, grad_res_low, 0, 0)
    grad_context = (
        contract(grad_res_low, w_out, 1, 1)
        .astype(jnp.bfloat16)
        .reshape(blocks, BLOCK, heads_local, HEAD_DIM)
    )
    grad_attention = jnp.einsum(
        "bqhd,bkhd->bhqk", grad_context, value_block, preferred_element_type=jnp.float32
    )
    grad_value = jnp.einsum(
        "bhqk,bqhd->bkhd",
        attention.astype(jnp.bfloat16),
        grad_context,
        preferred_element_type=jnp.float32,
    )
    row_dot = jnp.sum(attention * grad_attention, axis=-1, keepdims=True)
    grad_scores = (attention * (grad_attention - row_dot)).astype(jnp.bfloat16)
    grad_query = (
        jnp.einsum("bhqk,bkhd->bqhd", grad_scores, key_block, preferred_element_type=jnp.float32)
        * scale_factor
    )
    grad_key = (
        jnp.einsum("bhqk,bqhd->bkhd", grad_scores, query_block, preferred_element_type=jnp.float32)
        * scale_factor
    )
    grad_proj = (
        jnp.stack([grad_query, grad_key, grad_value], axis=2)
        .astype(jnp.bfloat16)
        .reshape(count, 3 * width_local)
    )
    grad_w_qkv = contract(normed_low, grad_proj, 0, 0).reshape(width, 3, width_local)
    grad_normed1 = lax.psum(
        contract(grad_proj, qkv_weight, 1, 1).astype(jnp.bfloat16), "tensor"
    ).astype(jnp.float32)
    grad_hidden_norm, grad_gain1, grad_bias1 = norm1_back(grad_normed1)
    grad_hidden = grad_residual + grad_hidden_norm
    column_count = width // lax.axis_size("tensor")
    hidden_cols = lax.dynamic_slice_in_dim(
        grad_hidden, lax.axis_index("tensor") * column_count, column_count, 1
    )
    grad_time = jax.ops.segment_sum(hidden_cols, token_step, num_segments=time_table.shape[0])
    input_grad = grad_hidden.astype(jnp.bfloat16)
    summed = lax.psum(
        (
            grad_time,
            grad_gain1,
            grad_bias1,
            grad_w_qkv,
            grad_w_out,
            grad_gain2,
            grad_bias2,
            grad_w_up,
            grad_up_bias,
            grad_w_down,
            grad_down_bias,
        ),
        "dp",
    )
    (
        grad_time,
        grad_gain1,
        grad_bias1,
        grad_w_qkv,
        grad_w_out,
        grad_gain2,
        grad_bias2,
        grad_w_up,
        grad_up_bias,
        grad_w_down,
        grad_down_bias,
    ) = summed
    return (
        block_output,
        input_grad,
        grad_time,
        grad_gain1,
        grad_bias1,
        grad_w_qkv,
        grad_w_out,
        grad_gain2,
        grad_bias2,
        grad_w_up,
        grad_up_bias,
        grad_w_down,
        grad_down_bias,
    )


def solution(mesh):
    in_specs = (
        P("dp", None),
        P(),
        P(),
        P(),
        P(),
        P(),
        P(),
        P(None, None, "tensor"),
        P("tensor", None),
        P(),
        P(),
        P(None, "tensor"),
        P("tensor"),
        P("tensor", None),
        P(),
        P("dp", None),
    )
    out_specs = (
        P("dp", None),
        P("dp", None),
        P(None, "tensor"),
        P(),
        P(),
        P(None, None, "tensor"),
        P("tensor", None),
        P(),
        P(),
        P(None, "tensor"),
        P("tensor"),
        P("tensor", None),
        P(),
    )
    return jax.shard_map(shards, mesh=mesh, in_specs=in_specs, out_specs=out_specs, check_vma=False)
```

profile of v0, /device:TPU:0, one launch (start us, length us, event | category | flops | bytes accessed | tf_op | source)
XLA Modules:
  0.0 560.2 jit_solution(13888479076969562882)
XLA Ops:
  12.3 5.2 gather_fusion
  17.5 2.7 fusion.109
  23.7 4.0 reshape.214
  38.3 45.3 %all-reduce.8.cloned.1.call-done = bf16[1024,768]{1,0:T(8,128)(2,1)} async-done(((bf16[1024,768]{1,0:T(8,128)(2,1)}), bf16[1024,768]{1,0:T(8,128)(2,1)}) %all-reduce.8.cloned.1.call-update) | async-done | bytes 1572880 | tf_op jit(solution)/shard_map/psum | solution.py:121
  83.6 3.4 fusion.108
  94.3 10.2 %fusion.105 = (f32[768]{0:T(1024)}, bf16[1024,768]{1,0:T(8,128)(2,1)S(1)}, f32[1024,768]{1,0:T(8,128)}) fusion(f32[1024,768]{1,0:T(8,128)S(1)} %fusion.112, f32[768]{0:T(1024)S(1)} %copy-done.28, bf16[1024,768]{1,0:T(8,128)(2,1)S(1)} %copy-done.14, bf16[768,768]{1,0:T(8,128)(2,1)S(1)} %copy-done.44), kind=kOutput, calls=%fused_computation.200 | convolution fusion | flops 1266154752 | bytes 10622976 | tf_op jit(solution)/shard_map/dot_general | solution.py:27
  105.6 2.6 convolution_convert_fusion.1
  108.3 12.6 %convolution_convert_fusion.2 = bf16[1024,768]{1,0:T(8,128)(2,1)} fusion(bf16[768,768]{1,0:T(8,128)(2,1)} %param.29, bf16[768,768]{1,0:T(8,128)(2,1)} %param.27, f32[1024,768]{1,0:T(8,128)} %get-tuple-element.15, f32[768]{0:T(1024)S(1)} %copy-done.28, f32[768]{0:T(1024)S(1)} %copy-done.47, f32[768]{0:T(1024)S(1)} %copy-done.29, ...), kind=kOutput, calls=%fused_computation.83 | convolution fusion | flops 2472542208 | bytes 7095296 | tf_op jit(solution)/shard_map/dot_general | solution.py:128
  120.9 6.2 %fusion.30 = f32[768,768]{1,0:T(8,128)} fusion(bf16[1024,768]{1,0:T(8,128)(2,1)} %param.31, f32[1024,768]{1,0:T(8,128)} %get-tuple-element.68, f32[1024,768]{1,0:T(8,128)} %copy-done.16, f32[768]{0:T(1024)S(1)} %copy-done.28), kind=kOutput, calls=%fused_computation.86 | convolution fusion | flops 1211105280 | bytes 10226688 | tf_op jit(solution)/shard_map/dot_general | solution.py:27
  127.1 24.2 %all-reduce.10.cloned.1.call-done = bf16[1024,768]{1,0:T(8,128)(2,1)} async-done(((bf16[1024,768]{1,0:T(8,128)(2,1)}), bf16[1024,768]{1,0:T(8,128)(2,1)}) %all-reduce.10.cloned.1.call-update) | async-done | bytes 1572880 | tf_op jit(solution)/shard_map/psum | solution.py:143
  151.3 4.1 convert_reduce_fusion.1
  164.7 3.5 convolution_convert_fusion.4
  168.2 4.2 reshape.215
  189.2 2.6 convolution_convert_fusion
  191.9 5.6 %fusion.54 = f32[768,768]{1,0:T(8,128)} fusion(bf16[1024,768]{1,0:T(8,128)(2,1)} %copy-done.50, f32[1024,768]{1,0:T(8,128)} %get-tuple-element.15, f32[1024]{0:T(1024)} %copy-done.32, f32[1024]{0:T(1024)} %copy-done.25, f32[768]{0:T(1024)} %param.26, f32[768]{0:T(1024)} %param.25), kind=kOutput, calls=%fused_computation.118 | convolution fusion | flops 1211891712 | bytes 7092224 | tf_op jit(solution)/shard_map/dot_general | solution.py:27
  197.5 4.7 fusion.47
  204.1 2.6 fusion.31
  206.7 53.9 %all-reduce.14.cloned.1.call-done = (bf16[1024,768]{1,0:T(8,128)(2,1)}, bf16[1024,768]{1,0:T(8,128)(2,1)}) async-done(((bf16[1024,768]{1,0:T(8,128)(2,1)}, bf16[1024,768]{1,0:T(8,128)(2,1)}), (bf16[1024,768]{1,0:T(8,128)(2,1)}, bf16[1024,768]{1,0:T(8,128)(2,1)})) %all-reduce.14.cloned.1.call-update) | async-done | bytes 3145744 | tf_op jit(solution)/shard_map/psum | solution.py:127
  265.4 2.9 fusion.107
  268.3 9.6 %scatter_custom_fusion = f32[1000,192]{1,0:T(8,128)} fusion(s32[1024]{0:T(1024)} %copy-done.37, f32[1024,768]{1,0:T(8,128)} %get-tuple-element.70, s32[]{:T(128)} %constant.51.clone.1, s32[]{:T(128)S(6)} %select_n.78, f32[]{:T(128)} %constant.21.clone.1), kind=kCustom, calls=%fused_computation.112 | custom fusion | flops 196608 | bytes 1817604 | tf_op jit(solution)/shard_map/scatter-add | solution.py:192
  278.6 39.9 %all-reduce = (f32[768]{0:T(1024)}, f32[768]{0:T(1024)}, f32[768]{0:T(1024)}, f32[768]{0:T(1024)}, f32[768]{0:T(1024)}, /*index=5*/f32[768]{0:T(1024)}) all-reduce(f32[768]{0:T(1024)S(1)} %get-tuple-element.45, f32[768]{0:T(1024)S(1)} %get-tuple-element.49, f32[768]{0:T(1024)S(1)} %copy-done.39, ...), channel_id=1, replica_groups=mesh['dp'=8,'tensor'=4] {'dp'}, use_global_device_ids=true, to_apply=%region_27.28 | all-reduce | flops 4608 | bytes 36864 | tf_op jit(solution)/shard_map/psum | solution.py:194
  318.5 2.9 add_convert_fusion.2
  321.4 222.8 %all-reduce.12.cloned.1.call-done = (f32[1000,192]{1,0:T(8,128)}, f32[768,3,192]{0,2,1:T(8,128)}, f32[192,768]{1,0:T(8,128)}, f32[768,768]{1,0:T(8,128)}, f32[768,768]{1,0:T(8,128)}) async-done(((f32[1000,192]{1,0:T(8,128)}, f32[768,3,192]{0,2,1:T(8,128)}, f32[192,768]{1,0:T(8,128)}, f32[768,768]{1,0:T(8,128)}, f32[768,768]{1,0:T(8,128)}), (f32[1000,192]{1,0:T(8,128)}, f32[768,3,192]{0,2,1:T(8,128)}, ...) | async-done | bytes 7845904 | tf_op jit(solution)/shard_map/psum | solution.py:194
  546.7 2.9 copy.130
  (175 shorter events, 66.7 us)
Async XLA Ops:
  7.2 5.1 copy-start
  7.2 76.4 %all-reduce.8.cloned.1.call-start = ((), (), s32[]{:S(2)}) async-start(), calls=%async_computation | async-start | bytes 3145728 | tf_op jit(solution)/shard_map/psum | solution.py:121
  37.9 113.4 %all-reduce.10.cloned.1.call-start = ((), (), s32[]{:S(2)}) async-start(), calls=%async_computation.1 | async-start | bytes 3145728 | tf_op jit(solution)/shard_map/psum | solution.py:143
  89.1 68.8 %copy-start.25 = (f32[1024]{0:T(1024)}, f32[1024]{0:T(1024)S(1)}, u32[]{:S(2)}) copy-start(f32[1024]{0:T(1024)S(1)} %broadcast_multiply_fusion.1) | copy-start | bytes 12292
  89.1 3.3 copy-start.29
  89.1 3.3 copy-start.43
  89.1 3.3 copy-start.47
  91.9 66.0 %copy-start.32 = (f32[1024]{0:T(1024)}, f32[1024]{0:T(1024)S(1)}, u32[]{:S(2)}) copy-start(f32[1024]{0:T(1024)S(1)} %fusion.65) | copy-start | bytes 12292
  94.3 10.2 %copy-start.16 = (f32[1024,768]{1,0:T(8,128)}, f32[1024,768]{1,0:T(8,128)S(1)}, u32[]{:S(2)}) copy-start(f32[1024,768]{1,0:T(8,128)S(1)} %fusion.112) | copy-start | bytes 9437188
  108.2 152.4 %all-reduce.14.cloned.1.call-start = ((), (), s32[]{:S(2)}) async-start(), calls=%async_computation.3 | async-start | bytes 6291456 | tf_op jit(solution)/shard_map/psum | solution.py:127
  151.3 4.1 copy-start.3
  151.3 4.1 copy-start.10
  157.9 3.8 copy-start.23
  162.6 5.6 %copy-start.26 = (f32[1024]{0:T(1024)}, f32[1024]{0:T(1024)S(1)}, u32[]{:S(2)}) copy-start(f32[1024]{0:T(1024)S(1)} %broadcast_multiply_fusion) | copy-start | bytes 12292
  163.7 4.5 copy-start.33
  176.9 5.7 %copy-start.5 = (f32[2,3,512,512]{2,3,1,0:T(8,128)}, f32[2,3,512,512]{2,3,1,0:T(8,128)S(1)}, u32[]{:S(2)}) copy-start(f32[2,3,512,512]{2,3,1,0:T(8,128)S(1)} %get-tuple-element.86) | copy-start | bytes 18874372
  191.8 352.4 %all-reduce.12.cloned.1.call-start = ((), (), s32[]{:S(2)}) async-start(), calls=%async_computation.2 | async-start | bytes 16203776 | tf_op jit(solution)/shard_map/psum | solution.py:194
  191.9 5.6 %copy-start.13 = (pred[2,512,512]{1,2,0:T(8,128)(4,1)S(1)}, pred[2,512,512]{1,2,0:T(8,128)(4,1)}, u32[]{:S(2)}) copy-start(pred[2,512,512]{1,2,0:T(8,128)(4,1)} %broadcast_compare_fusion) | copy-start | bytes 1572868
  197.5 5.2 copy-start.7
  206.7 56.5 %copy-start.36 = (f32[1024]{0:T(1024)S(1)}, f32[1024]{0:T(1024)}, u32[]{:S(2)}) copy-start(f32[1024]{0:T(1024)} %copy-done.35) | copy-start | bytes 12292
  277.9 40.6 %copy-start.4 = (f32[1024,768]{1,0:T(8,128)S(1)}, f32[1024,768]{1,0:T(8,128)}, u32[]{:S(2)}) copy-start(f32[1024,768]{1,0:T(8,128)} %get-tuple-element.15) | copy-start | bytes 9437188
  277.9 40.6 %copy-start.42 = (f32[768]{0:T(1024)S(1)}, f32[768]{0:T(1024)}, u32[]{:S(2)}) copy-start(f32[768]{0:T(1024)} %param.30) | copy-start | bytes 9220
  544.2 5.4 copy-start.24
  546.7 3.8 copy-start.18
  (31 other events, 52.4 us)
Sparse Core Ops, SparseCore 0:
  38.0 45.5 all-reduce.7
  108.3 42.8 all-reduce.9
  191.9 68.6 all-reduce.13
  278.1 266.0 all-reduce.11
where the time goes:
time: 569 us; the launch traced here: 560 us
  waiting for transfers between devices  346 us (61%)
  matrix products  71.1 us (12%)
  other arithmetic  51.3 us (9%)
  blocking collectives  39.9 us (7%)
  local copies, waits for them, and re-layouts  36.2 us (6%)
  between operations  15 us (3%)
    psum x1, waiting for transfers between devices, shards(): lax.psum((grad_time, grad_gain1, grad_bias1, grad_w_qkv, grad_w_out, grad...  223 us
    psum x1, waiting for transfers between devices, shards(): lax.psum(jnp.dot(forward_mlp[3], w_down, preferred_element_type=jnp.float...  53.9 us
    psum x1, waiting for transfers between devices, shards(): lax.psum(jnp.dot(forward_attn[6], w_out, preferred_element_type=jnp.float...  45.3 us
    psum x1, blocking collectives, shards(): lax.psum((grad_time, grad_gain1, grad_bias1, grad_w_qkv, grad_w_out, grad...  39.9 us
    dot_general x8, matrix products, contract(): lax.dot_general(left, right, (((left_dim,), (right_dim,)), ((), ())), pre...  31.9 us
    psum x1, waiting for transfers between devices, shards(): lax.psum(contract(grad_pre_low, w_up, 1, 1).astype(jnp.bfloat16), 'tensor')  24.2 us
    unnamed x110, local copies, waits for them, and re-layouts  15.6 us
    dot_general x1, matrix products, shards(): jnp.dot(forward_mlp[3], w_down, preferred_element_type=jnp.float32)  12.6 us
  transfers between devices with their start and end apart: 4, of which 4 were waited for; matrix products, arithmetic and copies ran while one was open for 7% of the time, Pallas kernels for 0%

commit v1 on v0

v1 whole, which is shorter than its diff:
```python
import functools

import jax
import jax.numpy as jnp
from jax import lax
from jax.experimental import pallas as pl
from jax.experimental.pallas import tpu as pltpu
from jax.sharding import PartitionSpec as P

HEAD_DIM = 64
SHORT = 128
PAIR = 256
EPS = 1e-05
NEG = -1000000000.0
SQRT_HALF = 0.7071067811865476
PHI_ZERO = 0.3989422804014327
CHUNKS = 1
VMEM_MB = 40

F32 = jnp.float32
BF16 = jnp.bfloat16


def mm(left, right, left_dim, right_dim):
    return lax.dot_general(
        left, right, (((left_dim,), (right_dim,)), ((), ())), preferred_element_type=F32
    )


def params(dims=1):
    return pltpu.CompilerParams(
        dimension_semantics=("arbitrary",) * dims, vmem_limit_bytes=VMEM_MB << 20
    )


def cost(flops, nbytes):
    return pl.CostEstimate(flops=int(flops), bytes_accessed=int(nbytes), transcendentals=0)


def shape(dims, dtype):
    return jax.ShapeDtypeStruct(dims, dtype)


def whole(array):
    zeros = (0,) * array.ndim
    return pl.BlockSpec(array.shape, lambda *_: zeros)


def core_swap(value):
    pairs = [(i, i ^ 1) for i in range(lax.axis_size("tensor"))]
    return lax.ppermute(value, "tensor", pairs)


def chip_swap(value):
    pairs = [(i, i ^ 2) for i in range(lax.axis_size("tensor"))]
    return lax.ppermute(value, "tensor", pairs)


def dp_swap(value, bit):
    pairs = [(i, i ^ bit) for i in range(lax.axis_size("dp"))]
    return lax.ppermute(value, "dp", pairs)


def norm_stats(values):
    mean = jnp.mean(values, axis=-1, keepdims=True)
    centred = values - mean
    variance = jnp.mean(centred * centred, axis=-1, keepdims=True)
    scale = lax.rsqrt(variance + EPS)
    return centred * scale, scale


def fill_slots(slot_ref, group, row_length, row_group, row_step):
    rows = row_length.shape[0]

    def long_row(r, pos):
        slot_ref[pos] = row_step[r]
        slot_ref[pos + 1] = row_step[r]
        hit = (row_group[r] == group) & (row_length[r] > SHORT)
        return pos + jnp.where(hit, 2, 0)

    def short_row(r, pos):
        slot_ref[pos] = row_step[r]
        hit = (row_group[r] == group) & (row_length[r] <= SHORT)
        return pos + jnp.where(hit, 1, 0)

    long_slots = lax.fori_loop(0, rows, long_row, 0)
    lax.fori_loop(0, rows, short_row, long_slots)
    return long_slots


def block_of(i, ids, chunk, half, chunks):
    side = jnp.where(i < half, 1 - ids[0], ids[0])
    return side * (half * chunks) + chunk * half + lax.rem(i, half)


def attend_kernel(
    chunk, half, chunks, slots, ids, row_length, row_group, row_step,
    tokens, table, gain, bias, wq, wk, wv, wo,
    send, keep, hidden_out, normed_out, q_out, k_out, v_out, p_out, c_out,
    slot_ref, rows_ref, sems,
):
    i = pl.program_id(0)

    def fetch(s):
        step = slot_ref[s]
        start = pl.multiple_of((step // 8) * 8, 8)
        return pltpu.make_async_copy(table.at[pl.ds(start, 8), :], rows_ref.at[s], sems.at[s])

    @pl.when(i == 0)
    def _():
        slot_ref[slots + 2] = fill_slots(slot_ref, ids[1], row_length, row_group, row_step)
        for s in range(slots):
            fetch(s).start()
        for s in range(slots):
            fetch(s).wait()

    block = block_of(i, ids, chunk, half, chunks)
    sub = lax.broadcasted_iota(jnp.int32, (8, 1), 0)

    def row_of(s):
        picked = sub == lax.rem(slot_ref[s], 8)
        return jnp.sum(jnp.where(picked, rows_ref[s].astype(F32), 0.0), axis=0, keepdims=True)

    low_half = lax.broadcasted_iota(jnp.int32, (PAIR, 1), 0) < SHORT
    step_row = jnp.where(low_half, row_of(2 * block), row_of(2 * block + 1))
    hidden = tokens[...].astype(F32) + step_row
    unit, _ = norm_stats(hidden)
    normed = (unit * gain[...] + bias[...]).astype(BF16)
    normed_out[...] = normed
    q = mm(normed, wq[...], 1, 0).astype(BF16)
    k = mm(normed, wk[...], 1, 0).astype(BF16)
    v = mm(normed, wv[...], 1, 0).astype(BF16)
    q_out[...] = q
    k_out[...] = k
    v_out[...] = v
    split = (2 * block >= slot_ref[slots + 2]).astype(jnp.int32)
    row_half = lax.broadcasted_iota(jnp.int32, (PAIR, PAIR), 0) // SHORT
    col_half = lax.broadcasted_iota(jnp.int32, (PAIR, PAIR), 1) // SHORT
    allowed = ((row_half ^ col_half) * split) == 0
    width = q.shape[1]
    head = lax.broadcasted_iota(jnp.int32, (1, width), 1) // HEAD_DIM
    context = jnp.zeros((PAIR, width), F32)
    for h in range(width // HEAD_DIM):
        mine = head == h
        qh = jnp.where(mine, q, jnp.zeros_like(q))
        scores = mm(qh, k, 1, 1) * (HEAD_DIM**-0.5)
        scores = jnp.where(allowed, scores, NEG)
        top = jnp.max(scores, axis=-1, keepdims=True)
        powers = jnp.exp(scores - top)
        total = jnp.sum(powers, axis=-1, keepdims=True)
        weights = (powers * (1.0 / total)).astype(BF16)
        p_out[0, h] = weights
        context = context + mm(weights, jnp.where(mine, v, jnp.zeros_like(v)), 1, 0)
    low = context.astype(BF16)
    c_out[...] = low
    part = mm(low, wo[...], 1, 0).astype(BF16)

    @pl.when(i < half)
    def _():
        send[...] = part

    @pl.when(i >= half)
    def _():
        keep[...] = part
        hidden_out[...] = hidden


def attend(chunk, chunks, scalars, tokens, table, gain, bias, wq, wk, wv, wo):
    count, width = tokens.shape
    local = wo.shape[0]
    blocks = count // PAIR // chunks
    half = blocks // 2
    rows = blocks * PAIR
    slots = count // SHORT
    own = rows // 2
    heads = local // HEAD_DIM
    first = lambda i, *_: (jnp.minimum(i, half - 1), 0)
    second = lambda i, *_: (jnp.maximum(i - half, 0), 0)
    step = lambda i, *_: (i, 0)
    row = pl.BlockSpec((PAIR, width), step)
    thin = pl.BlockSpec((PAIR, local), step)
    return pl.pallas_call(
        functools.partial(attend_kernel, chunk, half, chunks, slots),
        grid_spec=pltpu.PrefetchScalarGridSpec(
            num_scalar_prefetch=4,
            grid=(blocks,),
            in_specs=[
                pl.BlockSpec((PAIR, width), lambda i, ids, *_: (block_of(i, ids, chunk, half, chunks), 0)),
                pl.BlockSpec(memory_space=pl.ANY),
                whole(gain), whole(bias), whole(wq), whole(wk), whole(wv), whole(wo),
            ],
            out_specs=[
                pl.BlockSpec((PAIR, width), first),
                pl.BlockSpec((PAIR, width), second),
                pl.BlockSpec((PAIR, width), second),
                row, thin, thin, thin,
                pl.BlockSpec((1, heads, PAIR, PAIR), lambda i, *_: (i, 0, 0, 0)),
                thin,
            ],
            scratch_shapes=[
                pltpu.SMEM((slots + 4,), jnp.int32),
                pltpu.VMEM((slots, 8, width), BF16),
                pltpu.SemaphoreType.DMA((slots,)),
            ],
        ),
        out_shape=[
            shape((own, width), BF16), shape((own, width), BF16), shape((own, width), F32),
            shape((rows, width), BF16),
            shape((rows, local), BF16), shape((rows, local), BF16), shape((rows, local), BF16),
            shape((blocks, heads, PAIR, PAIR), BF16),
            shape((rows, local), BF16),
        ],
        compiler_params=params(),
        cost_estimate=cost(rows * width * local * 8, rows * width * 8),
        name="attend",
    )(*scalars, tokens, table, gain, bias, wq, wk, wv, wo)


def mid_kernel(hidden, pair, other, gain, bias, residual_out, normed_out):
    residual = hidden[...] + (pair[...].astype(F32) + other[...].astype(F32))
    residual_out[...] = residual
    unit, _ = norm_stats(residual)
    normed_out[...] = (unit * gain[...] + bias[...]).astype(BF16)


def mid_forward(hidden, pair, other, gain, bias):
    rows, width = hidden.shape
    row = pl.BlockSpec((PAIR, width), lambda i: (i, 0))
    return pl.pallas_call(
        mid_kernel,
        grid=(rows // PAIR,),
        in_specs=[row, row, row, whole(gain), whole(bias)],
        out_specs=[row, row],
        out_shape=[shape((rows, width), F32), shape((rows, width), BF16)],
        compiler_params=params(),
        cost_estimate=cost(rows * width * 12, rows * width * 14),
        name="mid_forward",
    )(hidden, pair, other, gain, bias)


def expand_kernel(half, ids, peer, own, cot, w_up, up_bias, w_down, send, keep, act_out, low_out, bias_out):
    i = pl.program_id(0)
    normed = jnp.where(i < half, peer[...], own[...])
    pre = mm(normed, w_up[...], 1, 0) + up_bias[...]
    grad_act = mm(cot[...], w_down[...], 1, 1)
    cdf = 0.5 * (1.0 + lax.erf(pre * SQRT_HALF))
    act_out[...] = (pre * cdf).astype(BF16)
    slope = cdf + pre * (PHI_ZERO * jnp.exp(-0.5 * (pre * pre)))
    grad_pre = grad_act * slope

    @pl.when(i == 0)
    def _():
        bias_out[...] = jnp.zeros_like(bias_out)

    bias_out[...] += jnp.sum(grad_pre, axis=0, keepdims=True)
    low = grad_pre.astype(BF16)
    low_out[...] = low
    part = mm(low, w_up[...], 1, 1).astype(BF16)

    @pl.when(i < half)
    def _():
        send[...] = part

    @pl.when(i >= half)
    def _():
        keep[...] = part


def expand(chunk, chunks, ids, peer, own, cot, w_up, up_bias, w_down):
    count, width = cot.shape
    local = w_up.shape[1]
    blocks = count // PAIR // chunks
    half = blocks // 2
    rows = blocks * PAIR
    first = lambda i, *_: (jnp.minimum(i, half - 1), 0)
    second = lambda i, *_: (jnp.maximum(i - half, 0), 0)
    step = lambda i, *_: (i, 0)
    return pl.pallas_call(
        functools.partial(expand_kernel, half),
        grid_spec=pltpu.PrefetchScalarGridSpec(
            num_scalar_prefetch=1,
            grid=(blocks,),
            in_specs=[
                pl.BlockSpec((PAIR, width), first),
                pl.BlockSpec((PAIR, width), second),
                pl.BlockSpec((PAIR, width), lambda i, ids: (block_of(i, ids, chunk, half, chunks), 0)),
                whole(w_up), whole(up_bias), whole(w_down),
            ],
            out_specs=[
                pl.BlockSpec((PAIR, width), first),
                pl.BlockSpec((PAIR, width), second),
                pl.BlockSpec((PAIR, local), step),
                pl.BlockSpec((PAIR, local), step),
                whole(up_bias),
            ],
        ),
        out_shape=[
            shape((rows // 2, width), BF16), shape((rows // 2, width), BF16),
            shape((rows, local), BF16), shape((rows, local), BF16),
            shape((1, local), F32),
        ],
        compiler_params=params(),
        cost_estimate=cost(rows * width * local * 6, rows * width * 12),
        name="expand",
    )(ids, peer, own, cot, w_up, up_bias, w_down)


def contract_kernel(half, act, w_down, send, keep):
    i = pl.program_id(0)
    part = mm(act[...], w_down[...], 1, 0).astype(BF16)

    @pl.when(i < half)
    def _():
        send[...] = part

    @pl.when(i >= half)
    def _():
        keep[...] = part


def contract_rows(act, w_down):
    rows, local = act.shape
    width = w_down.shape[1]
    blocks = rows // PAIR
    half = blocks // 2
    return pl.pallas_call(
        functools.partial(contract_kernel, half),
        grid=(blocks,),
        in_specs=[pl.BlockSpec((PAIR, local), lambda i: (i, 0)), whole(w_down)],
        out_specs=[
            pl.BlockSpec((PAIR, width), lambda i: (jnp.minimum(i, half - 1), 0)),
            pl.BlockSpec((PAIR, width), lambda i: (jnp.maximum(i - half, 0), 0)),
        ],
        out_shape=[shape((rows // 2, width), BF16), shape((rows // 2, width), BF16)],
        compiler_params=params(),
        cost_estimate=cost(rows * width * local * 2, rows * width * 4),
        name="contract_rows",
    )(act, w_down)


def weight_kernel(pieces, *refs):
    left, right, out = refs[1 : 1 + pieces], refs[1 + pieces : 1 + 2 * pieces], refs[-1]
    total = mm(left[0][...], right[0][...], 0, 0)
    for a, b in zip(left[1:], right[1:]):
        total = total + mm(a[...], b[...], 0, 0)
    out[...] = total.astype(BF16)


def weight_grad(ids, lefts, rights, tiles, name):
    pieces = len(lefts)
    rows_out = lefts[0][0].shape[1]
    tile = rows_out // tiles
    cols = rights[0][0].shape[1]
    count = sum(size for _, size, _ in lefts)
    specs = [pl.BlockSpec((size, tile), lambda i, ids, at=at: (at(ids), i)) for _, size, at in lefts]
    specs += [pl.BlockSpec((size, cols), lambda i, ids, at=at: (at(ids), 0)) for _, size, at in rights]
    return pl.pallas_call(
        functools.partial(weight_kernel, pieces),
        grid_spec=pltpu.PrefetchScalarGridSpec(
            num_scalar_prefetch=1,
            grid=(tiles,),
            in_specs=specs,
            out_specs=pl.BlockSpec((tile, cols), lambda i, ids: (i, 0)),
        ),
        out_shape=shape((rows_out, cols), BF16),
        compiler_params=params(),
        cost_estimate=cost(2 * count * rows_out * cols, 2 * (count * (rows_out + cols) + rows_out * cols)),
        name=name,
    )(ids, *[a for a, _, _ in lefts], *[b for b, _, _ in rights])


def mid_back_kernel(pair, other, residual, cot, gain, grad_out, low_out, sums):
    i = pl.program_id(0)
    err = pair[...].astype(F32) + other[...].astype(F32)
    unit, scale = norm_stats(residual[...])
    top = cot[...].astype(F32)
    f = err * gain[...]
    f_mean = jnp.mean(f, axis=-1, keepdims=True)
    fx_mean = jnp.mean(f * unit, axis=-1, keepdims=True)
    grad = top + scale * (f - f_mean - unit * fx_mean)
    grad_out[...] = grad
    low_out[...] = grad.astype(BF16)

    @pl.when(i == 0)
    def _():
        sums[...] = jnp.zeros_like(sums)

    sums[0:1] += jnp.sum(err * unit, axis=0, keepdims=True)
    sums[1:2] += jnp.sum(err, axis=0, keepdims=True)
    sums[2:3] += jnp.sum(top, axis=0, keepdims=True)


def mid_back(chunk, chunks, ids, pair, other, residual, cot, gain):
    rows, width = residual.shape
    half = rows // PAIR
    row = pl.BlockSpec((PAIR, width), lambda i, ids: (i, 0))
    return pl.pallas_call(
        lambda ids, *refs: mid_back_kernel(*refs),
        grid_spec=pltpu.PrefetchScalarGridSpec(
            num_scalar_prefetch=1,
            grid=(half,),
            in_specs=[
                row, row, row,
                pl.BlockSpec((PAIR, width), lambda i, ids: (block_of(i + half, ids, chunk, half, chunks), 0)),
                whole(gain),
            ],
            out_specs=[row, row, pl.BlockSpec((8, width), lambda i, ids: (0, 0))],
        ),
        out_shape=[shape((rows, width), F32), shape((rows, width), BF16), shape((8, width), F32)],
        compiler_params=params(),
        cost_estimate=cost(rows * width * 20, rows * width * 16),
        name="mid_back",
    )(ids, pair, other, residual, cot, gain)


def attend_back_kernel(half, peer, own, q_ref, k_ref, v_ref, p_ref, wq, wk, wv, wo, send, keep, dq_out, dk_out, dv_out):
    i = pl.program_id(0)
    low = jnp.where(i < half, peer[...], own[...])
    grad_context = mm(low, wo[...], 1, 1).astype(BF16)
    q, k, v = q_ref[...], k_ref[...], v_ref[...]
    width = q.shape[1]
    head = lax.broadcasted_iota(jnp.int32, (1, width), 1) // HEAD_DIM
    zero = jnp.zeros_like(q)
    dq = dk = dv = jnp.zeros((PAIR, width), F32)
    for h in range(width // HEAD_DIM):
        mine = head == h
        gh = jnp.where(mine, grad_context, zero)
        weights = p_ref[0, h]
        grad_p = mm(gh, v, 1, 1)
        wide = weights.astype(F32)
        dot = jnp.sum(wide * grad_p, axis=-1, keepdims=True)
        grad_s = (wide * (grad_p - dot)).astype(BF16)
        dv = dv + mm(weights, gh, 0, 0)
        dq = dq + mm(grad_s, jnp.where(mine, k, zero), 1, 0)
        dk = dk + mm(grad_s, jnp.where(mine, q, zero), 0, 0)
    scale = HEAD_DIM**-0.5
    dq = (dq * scale).astype(BF16)
    dk = (dk * scale).astype(BF16)
    dv = dv.astype(BF16)
    dq_out[...] = dq
    dk_out[...] = dk
    dv_out[...] = dv
    part = (mm(dq, wq[...], 1, 1) + mm(dk, wk[...], 1, 1) + mm(dv, wv[...], 1, 1)).astype(BF16)

    @pl.when(i < half)
    def _():
        send[...] = part

    @pl.when(i >= half)
    def _():
        keep[...] = part


def attend_back(peer, own, q, k, v, p, wq, wk, wv, wo):
    rows, local = q.shape
    width = wo.shape[1]
    blocks = rows // PAIR
    half = blocks // 2
    heads = local // HEAD_DIM
    first = pl.BlockSpec((PAIR, width), lambda i: (jnp.minimum(i, half - 1), 0))
    second = pl.BlockSpec((PAIR, width), lambda i: (jnp.maximum(i - half, 0), 0))
    thin = pl.BlockSpec((PAIR, local), lambda i: (i, 0))
    return pl.pallas_call(
        functools.partial(attend_back_kernel, half),
        grid=(blocks,),
        in_specs=[
            first, second, thin, thin, thin,
            pl.BlockSpec((1, heads, PAIR, PAIR), lambda i: (i, 0, 0, 0)),
            whole(wq), whole(wk), whole(wv), whole(wo),
        ],
        out_specs=[first, second, thin, thin, thin],
        out_shape=[
            shape((rows // 2, width), BF16), shape((rows // 2, width), BF16),
            shape((rows, local), BF16), shape((rows, local), BF16), shape((rows, local), BF16),
        ],
        compiler_params=params(),
        cost_estimate=cost(rows * width * local * 8, rows * width * 10),
        name="attend_back",
    )(peer, own, q, k, v, p, wq, wk, wv, wo)


def last_kernel(pair, other, hidden, grad_residual, gain, low_out, sums, times):
    i = pl.program_id(0)
    err = pair[...].astype(F32) + other[...].astype(F32)
    unit, scale = norm_stats(hidden[...])
    f = err * gain[...]
    f_mean = jnp.mean(f, axis=-1, keepdims=True)
    fx_mean = jnp.mean(f * unit, axis=-1, keepdims=True)
    grad = grad_residual[...] + scale * (f - f_mean - unit * fx_mean)
    low_out[...] = grad.astype(BF16)

    @pl.when(i == 0)
    def _():
        sums[...] = jnp.zeros_like(sums)

    sums[0:1] += jnp.sum(err * unit, axis=0, keepdims=True)
    sums[1:2] += jnp.sum(err, axis=0, keepdims=True)
    times[0, 0:1] = jnp.sum(grad[:SHORT], axis=0, keepdims=True)
    times[0, 1:2] = jnp.sum(grad[SHORT:], axis=0, keepdims=True)


def last_back(pair, other, hidden, grad_residual, gain):
    rows, width = hidden.shape
    half = rows // PAIR
    row = pl.BlockSpec((PAIR, width), lambda i: (i, 0))
    return pl.pallas_call(
        last_kernel,
        grid=(half,),
        in_specs=[row, row, row, row, whole(gain)],
        out_specs=[
            row,
            pl.BlockSpec((8, width), lambda i: (0, 0)),
            pl.BlockSpec((1, 2, width), lambda i: (i, 0, 0)),
        ],
        out_shape=[shape((rows, width), BF16), shape((8, width), F32), shape((half, 2, width), F32)],
        compiler_params=params(),
        cost_estimate=cost(rows * width * 20, rows * width * 16),
        name="last_back",
    )(pair, other, hidden, grad_residual, gain)


def time_kernel(slots, ids, row_length, row_group, row_step, sums, out, at_ref):
    groups = at_ref.shape[0]
    rows = row_length.shape[0]
    out[...] = jnp.zeros_like(out)

    def clear(g, _):
        at_ref[g] = 0
        return 0

    lax.fori_loop(0, groups, clear, 0)

    def place(long):
        def one(r, _):
            @pl.when((row_length[r] > SHORT) == long)
            def _():
                g = row_group[r]
                at = at_ref[g]
                at_ref[g] = at + (2 if long else 1)
                base = (g ^ ids[1]) * slots + at
                value = sums[pl.ds(base, 1), :]
                if long:
                    value = value + sums[pl.ds(base + 1, 1), :]
                step = pl.ds(row_step[r], 1)
                out[step, :] = out[step, :] + value

            return 0

        lax.fori_loop(0, rows, one, 0)

    place(True)
    place(False)


def time_table_grad(scalars, sums, steps, slots):
    width = sums.shape[1]
    groups = sums.shape[0] // slots
    return pl.pallas_call(
        functools.partial(time_kernel, slots),
        grid_spec=pltpu.PrefetchScalarGridSpec(
            num_scalar_prefetch=4,
            grid=(1,),
            in_specs=[whole(sums)],
            out_specs=pl.BlockSpec((steps, width), lambda *_: (0, 0)),
            scratch_shapes=[pltpu.SMEM((groups,), jnp.int32)],
        ),
        out_shape=shape((steps, width), F32),
        compiler_params=params(),
        cost_estimate=cost(steps * width, steps * width * 4),
        name="time_table_grad",
    )(*scalars, sums)


def add_low(a, b):
    return (a.astype(F32) + b.astype(F32)).astype(BF16)


def share(send, keep):
    pair = add_low(keep, core_swap(send))
    return pair, chip_swap(pair)


def in_order(core, own, other):
    return jnp.where(
        core == 0,
        jnp.concatenate([own, other], axis=0),
        jnp.concatenate([other, own], axis=0),
    )


def shards(
    tokens, row_length, row_group, row_step, time_table, norm1_gain, norm1_bias, w_qkv, w_out,
    norm2_gain, norm2_bias, w_up, up_bias, w_down, down_bias, cotangent,
):
    count, width = tokens.shape
    chunks = CHUNKS
    n_dp = lax.axis_size("dp")
    dp = lax.axis_index("dp")
    part = lax.axis_index("tensor")
    core = lax.rem(part, 2)
    ids = jnp.stack([core, dp, part, dp]).astype(jnp.int32)
    scalars = (ids, row_length, row_group, row_step)
    local = w_out.shape[0]
    slots = count // SHORT
    gain1, bias1 = norm1_gain[None], norm1_bias[None]
    gain2, bias2 = norm2_gain[None], norm2_bias[None]
    up_b = up_bias[None]
    wq, wk, wv = w_qkv[:, 0], w_qkv[:, 1], w_qkv[:, 2]
    size = count // 2 // chunks
    each = range(chunks)

    ahead = [attend(c, chunks, scalars, tokens, time_table, gain1, bias1, wq, wk, wv, w_out) for c in each]
    residual, own2, peer2 = [], [], []
    for c in each:
        pair, other = share(ahead[c][0], ahead[c][1])
        r, n = mid_forward(ahead[c][2], pair, other, gain2, bias2)
        residual.append(r)
        own2.append(n)
        peer2.append(core_swap(n))
    grown = [expand(c, chunks, ids, peer2[c], own2[c], cotangent, w_up, up_b, w_down) for c in each]

    peer_rows = lambda c: (lambda ids: (1 - ids[0]) * chunks + c)
    own_rows = lambda c: (lambda ids: ids[0] * chunks + c)
    zero = lambda ids: 0
    one = lambda ids: 1
    cots = [(cotangent, size, f(c)) for c in each for f in (peer_rows, own_rows)]
    acts = [(grown[c][2], size, f) for c in each for f in (zero, one)]
    lows = [(grown[c][3], size, f) for c in each for f in (zero, one)]
    norms = [(a[c], size, zero) for c in each for a in (peer2, own2)]
    down_grad = weight_grad(ids, acts, cots, 2, "down_grad")
    up_grad = weight_grad(ids, norms, lows, 2, "up_grad")
    down_sum, up_sum = lax.psum((down_grad, up_grad), "dp")

    back = []
    for c in each:
        pair, other = share(grown[c][0], grown[c][1])
        back.append(mid_back(c, chunks, ids, pair, other, residual[c], cotangent, gain2))
    peer_low = [core_swap(back[c][1]) for c in each]
    attn = [
        attend_back(peer_low[c], back[c][1], *ahead[c][4:8], wq, wk, wv, w_out) for c in each
    ]
    ctxs = [(ahead[c][8], size, f) for c in each for f in (zero, one)]
    lows1 = [(a, size, zero) for c in each for a in (peer_low[c], back[c][1])]
    norms1 = [(ahead[c][3], size, f) for c in each for f in (zero, one)]
    out_grad = weight_grad(ids, ctxs, lows1, 1, "out_grad")
    qkv = [
        weight_grad(ids, norms1, [(attn[c][j], size, f) for c in each for f in (zero, one)], 2, "qkv_grad")
        for j in (2, 3, 4)
    ]
    qkv_sum, out_sum = lax.psum((jnp.stack(qkv), out_grad), "dp")

    low_in, vec1, times = [], [], []
    for c in each:
        pair, other = share(attn[c][0], attn[c][1])
        a, b, t = last_back(pair, other, ahead[c][2], back[c][0], gain1)
        low_in.append(a)
        vec1.append(b)
        times.append(t.reshape(-1, width))

    finals = []
    for c in each:
        send, keep = contract_rows(grown[c][2], w_down)
        pair, other = share(send, keep)
        finals.append((residual[c] + (pair.astype(F32) + other.astype(F32)) + down_bias).astype(BF16))
    final = jnp.concatenate(finals, axis=0)
    block_output = in_order(core, final, core_swap(final))
    low_grad = jnp.concatenate(low_in, axis=0)
    input_grad = in_order(core, low_grad, core_swap(low_grad))

    own_vec = jnp.concatenate([sum(b[2] for b in back)[:3], sum(vec1)[:2]], axis=0)
    own_time = jnp.concatenate(times, axis=0)
    other_vec, other_time = core_swap((own_vec, own_time))
    vec = jnp.concatenate([own_vec + other_vec, sum(g[4] for g in grown)], axis=0)
    table = in_order(core, own_time, other_time)
    table = lax.dynamic_slice_in_dim(table, part * local, local, 1)
    bit = 1
    while bit < n_dp:
        got_vec, got_table = dp_swap((vec, table), bit)
        vec = vec + got_vec
        table = jnp.concatenate([table, got_table], axis=0)
        bit *= 2
    time_grad = time_table_grad(scalars, table, time_table.shape[0], slots)

    return (
        block_output,
        input_grad,
        time_grad,
        vec[3],
        vec[4],
        jnp.transpose(qkv_sum, (1, 0, 2)).astype(F32),
        out_sum.astype(F32),
        vec[0],
        vec[1],
        up_sum.astype(F32),
        vec[5],
        down_sum.astype(F32),
        vec[2],
    )


def solution(mesh):
    in_specs = (
        P("dp", None), P(), P(), P(), P(), P(), P(), P(None, None, "tensor"), P("tensor", None), P(), P(),
        P(None, "tensor"), P("tensor"), P("tensor", None), P(), P("dp", None),
    )
    out_specs = (
        P("dp", None), P("dp", None), P(None, "tensor"), P(), P(), P(None, None, "tensor"), P("tensor", None),
        P(), P(), P(None, "tensor"), P("tensor"), P("tensor", None), P(),
    )
    return jax.shard_map(shards, mesh=mesh, in_specs=in_specs, out_specs=out_specs, check_vma=False)
```

time: 569 us -> 268 us (0.47); the launches traced: 560 us -> 267 us
  waiting for transfers between devices: 346 us -> 158 us
  matrix products: 71.1 us -> 0 us
  Pallas kernels: 0 us -> 45.3 us
  blocking collectives: 39.9 us -> 0 us
  other arithmetic: 51.3 us -> 19.6 us
  local copies, waits for them, and re-layouts: 36.2 us -> 10.1 us
  starting transfers between devices: 0.51 us -> 19.7 us
    psum x4 -> x1, waiting for transfers between devices: 346 us -> 79.2 us  [shards(): qkv_sum, out_sum = lax.psum((jnp.stack(qkv), out_grad), 'dp')]
    ppermute x0 -> x20, waiting for transfers between devices: none -> 78.9 us  [the longest x4 67.1 us: chip_swap(): return lax.ppermute(value, 'tensor', pairs)]
    dot_general x21 -> x0, matrix products: 71.1 us -> none  [the longest x8 31.9 us: contract(): lax.dot_general(left, right, (((left_dim,), (right_dim,)), ((), ())), pre...]
    pallas_call x0 -> x14, Pallas kernels: none -> 45.3 us  [the longest x6 11.3 us: weight_grad(): pl.pallas_call(functools.partial(weight_kernel, pieces), grid_spec=pltpu....]
    psum x1 -> x0, blocking collectives: 39.9 us -> none  [shards(): lax.psum((grad_time, grad_gain1, grad_bias1, grad_w_qkv, grad_w_out, grad...]
    reduce_sum x17 -> x0, other arithmetic: 30.2 us -> none  [the longest x4 11.3 us: normalize(): return centred * lax.rsqrt(variance + EPS) * gain + bias]
    ppermute x0 -> x20, starting transfers between devices: none -> 19.7 us  [the longest x6 10.9 us: dp_swap(): return lax.ppermute(value, 'dp', pairs)]
    scatter-add x1 -> x0, other arithmetic: 9.59 us -> none  [shards(): jax.ops.segment_sum(hidden_cols, token_step, num_segments=time_table.shap...]
  transfers between devices with their start and end apart: 4 -> 21, of which waited for: 4 -> 12; matrix products, arithmetic and copies ran while one was open for 7% -> 6% of each run, Pallas kernels for 0% -> 10%
where the time goes in v1:
time: 268 us; the launch traced here: 267 us
  waiting for transfers between devices  158 us (59%)
  Pallas kernels  45.3 us (17%)
  starting transfers between devices  19.7 us (7%)
  other arithmetic  19.6 us (7%)
  between operations  14.6 us (5%)
  local copies, waits for them, and re-layouts  10.1 us (4%)
    psum x1, waiting for transfers between devices, shards(): qkv_sum, out_sum = lax.psum((jnp.stack(qkv), out_grad), 'dp')  79.2 us
    ppermute x4, waiting for transfers between devices, chip_swap(): return lax.ppermute(value, 'tensor', pairs)  67.1 us
    pallas_call x6, Pallas kernels, weight_grad(): pl.pallas_call(functools.partial(weight_kernel, pieces), grid_spec=pltpu....  11.3 us
    ppermute x6, starting transfers between devices, dp_swap(): return lax.ppermute(value, 'dp', pairs)  10.9 us
    pallas_call x1, Pallas kernels, attend(): pl.pallas_call(functools.partial(attend_kernel, chunk, half, chunks, slot...  8.56 us
    unnamed x81, local copies, waits for them, and re-layouts  8.21 us
    pallas_call x1, Pallas kernels, expand(): pl.pallas_call(functools.partial(expand_kernel, half), grid_spec=pltpu.Pr...  7.09 us
    pallas_call x1, Pallas kernels, attend_back(): pl.pallas_call(functools.partial(attend_back_kernel, half), grid=(blocks,...  6.85 us
  transfers between devices with their start and end apart: 21, of which 12 were waited for; matrix products, arithmetic and copies ran while one was open for 6% of the time, Pallas kernels for 10%

profile of v1, /device:TPU:0, one launch (start us, length us, event | category | flops | bytes accessed | tf_op | source)
XLA Modules:
  0.0 267.4 jit_solution(6104419841996008369)
XLA Ops:
  12.0 8.6 %attend.1 = (bf16[512,768]{1,0:T(8,128)(2,1)S(1)}, bf16[512,768]{1,0:T(8,128)(2,1)S(1)}, f32[512,768]{1,0:T(8,128)S(1)}, bf16[1024,768]{1,0:T(8,128)(2,1)S(1)}, ...) custom-call(s32[4]{0:T(128)S(1)} %pad_add_fusion.ids.refs_0_, ...), custom_call_target="tpu_custom_call" | custom-call | flops 1207959552 | bytes 6291456 | tf_op jit(solution)/shard_map/attend/pallas_call | solution.py:182
  24.0 3.0 %collective-permute-start.1 = (bf16[512,768]{1,0:T(8,128)(2,1)S(1)}, bf16[512,768]{1,0:T(8,128)(2,1)S(1)}, u32[]{:S(2)}, u32[]{:S(2)}) collective-permute-start(bf16[512,768]{1,0:T(8,128)(2,1)S(1)} %add_convert_fusion.4.pair), channel_id=1, source_target_pairs={{0,2},{1,3},{2,0},{3,1},{4,6},{5,7},{6,4},{7,5},{8,10},{9,11},{10,... | collective-permute-start | bytes 2359304 | tf_op jit(solution)/shard_map/ppermute | solution.py:56
  27.0 17.8 %collective-permute-done.1.other = bf16[512,768]{1,0:T(8,128)(2,1)S(1)} collective-permute-done((bf16[512,768]{1,0:T(8,128)(2,1)S(1)}, bf16[512,768]{1,0:T(8,128)(2,1)S(1)}, u32[]{:S(2)}, u32[]{:S(2)}) %collective-permute-start.1) | collective-permute-done | bytes 786464 | tf_op jit(solution)/shard_map/ppermute | solution.py:56
  45.6 2.2 collective-permute-done.2.peer.refs_1_
  47.9 7.1 %expand.1 = (bf16[512,768]{1,0:T(8,128)(2,1)S(1)}, bf16[512,768]{1,0:T(8,128)(2,1)S(1)}, bf16[1024,768]{1,0:T(8,128)(2,1)S(1)}, bf16[1024,768]{1,0:T(8,128)(2,1)S(1)}, f32[1,768]{1,0:T(1,128)S(1)}) custom-call(s32[4]{0:T(128)S(1)} %pad_add_fusion.ids.refs_0_, bf16[512,768]{1,0:T(8,128)(2,1)S(1)} %collective-permute-done.2.peer.refs_1_, ...), custom_call_target="tpu_custom_call" | custom-call | flops 3623878656 | bytes 9437184 | tf_op jit(solution)/shard_map/expand/pallas_call | solution.py:278
  55.2 2.2 collective-permute-done.6
  59.3 17.8 %collective-permute-done.7.refs_1_ = bf16[512,768]{1,0:T(8,128)(2,1)S(1)} collective-permute-done((bf16[512,768]{1,0:T(8,128)(2,1)S(1)}, bf16[512,768]{1,0:T(8,128)(2,1)S(1)}, u32[]{:S(2)}, u32[]{:S(2)}) %collective-permute-start.7) | collective-permute-done | bytes 786464 | tf_op jit(solution)/shard_map/ppermute | solution.py:56
  77.2 2.1 mid_back.1
  80.5 3.1 %contract_rows.1 = (bf16[512,768]{1,0:T(8,128)(2,1)}, bf16[512,768]{1,0:T(8,128)(2,1)S(1)}) custom-call(bf16[1024,768]{1,0:T(8,128)(2,1)S(1)} %get-tuple-element.47.act.refs_1_.refs_2_, bf16[768,768]{1,0:T(8,128)(2,1)S(1)} %copy-done.27), custom_call_target="tpu_custom_call" | custom-call | flops 1207959552 | bytes 3145728 | tf_op jit(solution)/shard_map/contract_rows/pallas_call | solution.py:326
  84.0 2.4 down_grad.1
  86.5 2.4 up_grad.1
  89.0 6.8 %attend_back.1 = (bf16[512,768]{1,0:T(8,128)(2,1)S(1)}, bf16[512,768]{1,0:T(8,128)(2,1)S(1)}, bf16[1024,192]{1,0:T(8,128)(2,1)S(1)}, bf16[1024,192]{1,0:T(8,128)(2,1)S(1)}, bf16[1024,192]{1,0:T(8,128)(2,1)S(1)}) custom-call(bf16[512,768]{1,0:T(8,128)(2,1)S(1)} %collective-permute-done.8.peer.refs_3_, bf16[512,768]{1,0:T(8,128)(2,1)S(1)} %get-tuple-element.52.own.refs_4_, ...), custom_call_target="tpu_custom_call" | custom-call | flops 1207959552 | bytes 7864320 | tf_op jit(solution)/shard_map/attend_back/pallas_call | solution.py:463
  103.9 2.5 add_convert_fusion.3
  109.5 17.6 %collective-permute-done.4 = bf16[512,768]{1,0:T(8,128)(2,1)} collective-permute-done((bf16[512,768]{1,0:T(8,128)(2,1)}, bf16[512,768]{1,0:T(8,128)(2,1)}, u32[]{:S(2)}, u32[]{:S(2)}) %collective-permute-start.4) | collective-permute-done | bytes 786464 | tf_op jit(solution)/shard_map/ppermute | solution.py:56
  127.0 2.5 add_convert_fusion.2
  129.6 13.9 %collective-permute-done.10.other = bf16[512,768]{1,0:T(8,128)(2,1)} collective-permute-done((bf16[512,768]{1,0:T(8,128)(2,1)}, bf16[512,768]{1,0:T(8,128)(2,1)}, u32[]{:S(2)}, u32[]{:S(2)}) %collective-permute-start.10) | collective-permute-done | bytes 786464 | tf_op jit(solution)/shard_map/ppermute | solution.py:56
  143.4 3.2 %last_back.1 = (bf16[512,768]{1,0:T(8,128)(2,1)}, f32[8,768]{1,0:T(8,128)S(1)}, f32[2,2,768]{2,1,0:T(2,128)S(1)}) custom-call(bf16[512,768]{1,0:T(8,128)(2,1)} %add_convert_fusion.pair, bf16[512,768]{1,0:T(8,128)(2,1)} %collective-permute-done.10.other, f32[512,768]{1,0:T(8,128)S(1)} %get-tuple-element.42.hidden, f32[512,768]{1,0:T(8,128)S(1)} %copy-done.9, ...), custom_call_target="tpu_custom_call" | custom-call | flops 7864320 | bytes 6291456 | tf_op jit(solution)/shard_map/last_back/pallas_call | solution.py:506
  155.8 2.4 collective-permute-start.15
  159.9 2.2 collective-permute-done.18
  163.9 3.1 %maximum_select_fusion = bf16[1024,768]{1,0:T(8,128)(2,1)} fusion(bf16[512,768]{1,0:T(8,128)(2,1)S(1)} %collective-permute-done.5, bf16[512,768]{1,0:T(8,128)(2,1)} %add_convert_fusion.2, pred[]{:T(512)S(6)} %eq.2), kind=kLoop, calls=%fused_computation | loop fusion | flops 7077888 | bytes 3145729 | tf_op jit(solution)/shard_map/jit(_where)/select_n | solution.py:584
  167.0 2.3 time_table_grad.1
  171.3 3.1 %maximum_select_fusion.1 = bf16[1024,768]{1,0:T(8,128)(2,1)} fusion(bf16[512,768]{1,0:T(8,128)(2,1)S(1)} %collective-permute-done.11, bf16[512,768]{1,0:T(8,128)(2,1)} %get-tuple-element.60, pred[]{:T(512)S(6)} %eq.2), kind=kLoop, calls=%fused_computation.1 | loop fusion | flops 7077888 | bytes 3145729 | tf_op jit(solution)/shard_map/jit(_where)/select_n | solution.py:584
  174.4 79.2 %all-reduce.3.cloned.1.call-done = (bf16[768,3,192]{2,0,1:T(8,128)(2,1)}, bf16[192,768]{1,0:T(8,128)(2,1)}, bf16[768,768]{1,0:T(8,128)(2,1)}, bf16[768,768]{1,0:T(8,128)(2,1)}) async-done(((bf16[768,3,192]{2,0,1:T(8,128)(2,1)}, bf16[192,768]{1,0:T(8,128)(2,1)}, bf16[768,768]{1,0:T(8,128)(2,1)}, bf16[768,768]{1,0:T(8,128)(2,1)}), (bf16[768,3,192]{2,0,1:T(8,128)(2,1)}, bf16[192,768]{1,0:T(8,128)(2,1)}, ...) | async-done | bytes 3538960 | tf_op jit(solution)/shard_map/psum | solution.py:650
  253.6 2.9 %convert_element_type.78 = f32[768,768]{1,0:T(8,128)} convert(bf16[768,768]{1,0:T(8,128)(2,1)} %get-tuple-element.92) | non-fusion elementwise | flops 589824 | bytes 3538944 | tf_op jit(solution)/shard_map/convert_element_type | solution.py:694
  (146 shorter events, 42.3 us)
Async XLA Ops:
  7.2 246.4 %all-reduce.3.cloned.1.call-start = ((), (), s32[]{:S(2)}) async-start(), calls=%async_computation | async-start | bytes 7667712 | tf_op jit(solution)/shard_map/psum | solution.py:650
  21.4 2.4 collective-permute-start
  23.8 24.1 %copy-start.26 = (bf16[768,768]{1,0:T(8,128)(2,1)S(1)}, bf16[768,768]{1,0:T(8,128)(2,1)}, u32[]{:S(2)}) copy-start(bf16[768,768]{1,0:T(8,128)(2,1)} %w_down.3) | copy-start | bytes 3538948
  24.0 20.8 %collective-permute-start.1 = (bf16[512,768]{1,0:T(8,128)(2,1)S(1)}, bf16[512,768]{1,0:T(8,128)(2,1)S(1)}, u32[]{:S(2)}, u32[]{:S(2)}) collective-permute-start(bf16[512,768]{1,0:T(8,128)(2,1)S(1)} %add_convert_fusion.4.pair), channel_id=1, source_target_pairs={{0,2},{1,3},{2,0},{3,1},{4,6},{5,7},{6,4},{7,5},{8,10},{9,11},{10,... | collective-permute-start | bytes 2359304 | tf_op jit(solution)/shard_map/ppermute | solution.py:56
  45.5 2.4 collective-permute-start.2
  55.0 2.4 collective-permute-start.6
  57.5 19.7 %collective-permute-start.7 = (bf16[512,768]{1,0:T(8,128)(2,1)S(1)}, bf16[512,768]{1,0:T(8,128)(2,1)S(1)}, u32[]{:S(2)}, u32[]{:S(2)}) collective-permute-start(bf16[512,768]{1,0:T(8,128)(2,1)S(1)} %add_convert_fusion.1.refs_0_), channel_id=1, source_target_pairs={{0,2},{1,3},{2,0},{3,1},{4,6},{5,7},{6,4},{7,5},{8,10},{9,11},{10,... | collective-permute-start | bytes 2359304 | tf_op jit(solution)/shard_map/ppermute | solution.py:56
  80.5 8.5 %collective-permute-start.8 = (bf16[512,768]{1,0:T(8,128)(2,1)S(1)}, bf16[512,768]{1,0:T(8,128)(2,1)S(1)}, u32[]{:S(2)}, u32[]{:S(2)}) collective-permute-start(bf16[512,768]{1,0:T(8,128)(2,1)S(1)} %get-tuple-element.52.own.refs_4_), channel_id=1, source_target_pairs={{0,1},{1,0},{2,3},{3,2},{4,5},{5,4},{6,7},{7,6},{8,9},{9,8},{10,11... | collective-permute-start | bytes 2359304 | tf_op jit(solution)/shard_map/ppermute | solution.py:51
  83.6 20.3 %collective-permute-start.3 = (bf16[512,768]{1,0:T(8,128)(2,1)}, bf16[512,768]{1,0:T(8,128)(2,1)}, u32[]{:S(2)}, u32[]{:S(2)}) collective-permute-start(bf16[512,768]{1,0:T(8,128)(2,1)} %get-tuple-element.49), channel_id=1, source_target_pairs={{0,1},{1,0},{2,3},{3,2},{4,5},{5,4},{6,7},{7,6},{8,9},{9,8},{10,11... | collective-permute-start | bytes 2359304 | tf_op jit(solution)/shard_map/ppermute | solution.py:51
  103.8 4.3 %collective-permute-start.9 = (bf16[512,768]{1,0:T(8,128)(2,1)}, bf16[512,768]{1,0:T(8,128)(2,1)S(1)}, u32[]{:S(2)}, u32[]{:S(2)}) collective-permute-start(bf16[512,768]{1,0:T(8,128)(2,1)} %copy-done.28), channel_id=1, source_target_pairs={{0,1},{1,0},{2,3},{3,2},{4,5},{5,4},{6,7},{7,6},{8,9},{9,8},{10,11... | collective-permute-start | bytes 2359304 | tf_op jit(solution)/shard_map/ppermute | solution.py:51
  106.4 20.7 %copy-start.32 = (f32[768]{0:T(1024)S(1)}, f32[768]{0:T(1024)}, u32[]{:S(2)}) copy-start(f32[768]{0:T(1024)} %param.30) | copy-start | bytes 9220
  106.4 20.7 %collective-permute-start.4 = (bf16[512,768]{1,0:T(8,128)(2,1)}, bf16[512,768]{1,0:T(8,128)(2,1)}, u32[]{:S(2)}, u32[]{:S(2)}) collective-permute-start(bf16[512,768]{1,0:T(8,128)(2,1)} %add_convert_fusion.3), channel_id=1, source_target_pairs={{0,2},{1,3},{2,0},{3,1},{4,6},{5,7},{6,4},{7,5},{8,10},{9,11},{10,... | collective-permute-start | bytes 2359304 | tf_op jit(solution)/shard_map/ppermute | solution.py:56
  109.2 34.2 %collective-permute-start.10 = (bf16[512,768]{1,0:T(8,128)(2,1)}, bf16[512,768]{1,0:T(8,128)(2,1)}, u32[]{:S(2)}, u32[]{:S(2)}) collective-permute-start(bf16[512,768]{1,0:T(8,128)(2,1)} %add_convert_fusion.pair), channel_id=1, source_target_pairs={{0,2},{1,3},{2,0},{3,1},{4,6},{5,7},{6,4},{7,5},{8,10},{9,11},{10,... | collective-permute-start | bytes 2359304 | tf_op jit(solution)/shard_map/ppermute | solution.py:56
  109.5 34.0 %copy-start.9 = (f32[512,768]{1,0:T(8,128)S(1)}, f32[512,768]{1,0:T(8,128)}, u32[]{:S(2)}) copy-start(f32[512,768]{1,0:T(8,128)} %copy-done.8) | copy-start | bytes 4718596
  129.6 34.4 %collective-permute-start.5 = (bf16[512,768]{1,0:T(8,128)(2,1)}, bf16[512,768]{1,0:T(8,128)(2,1)S(1)}, u32[]{:S(2)}, u32[]{:S(2)}) collective-permute-start(bf16[512,768]{1,0:T(8,128)(2,1)} %add_convert_fusion.2), channel_id=1, source_target_pairs={{0,1},{1,0},{2,3},{3,2},{4,5},{5,4},{6,7},{7,6},{8,9},{9,8},{10,11... | collective-permute-start | bytes 2359304 | tf_op jit(solution)/shard_map/ppermute | solution.py:51
  146.7 1.2 collective-permute-start.12
  146.8 2.9 %collective-permute-start.16 = (f32[5,768]{1,0:T(8,128)S(1)}, f32[5,768]{1,0:T(8,128)S(1)}, u32[]{:S(2)}, u32[]{:S(2)}) collective-permute-start(f32[5,768]{1,0:T(8,128)S(1)} %pad_maximum_fusion.2), channel_id=1, source_target_pairs={{0,1},{1,0},{2,3},{3,2},{4,5},{5,4},{6,7},{7,6},{8,9},{9,8},{10,11... | collective-permute-start | bytes 46088 | tf_op jit(solution)/shard_map/ppermute | solution.py:51
  147.3 23.9 %collective-permute-start.11 = (bf16[512,768]{1,0:T(8,128)(2,1)}, bf16[512,768]{1,0:T(8,128)(2,1)S(1)}, u32[]{:S(2)}, u32[]{:S(2)}) collective-permute-start(bf16[512,768]{1,0:T(8,128)(2,1)} %get-tuple-element.60), channel_id=1, source_target_pairs={{0,1},{1,0},{2,3},{3,2},{4,5},{5,4},{6,7},{7,6},{8,9},{9,8},{10,11... | collective-permute-start | bytes 2359304 | tf_op jit(solution)/shard_map/ppermute | solution.py:51
  148.0 3.7 %collective-permute-start.13 = (f32[8,192]{1,0:T(8,128)S(1)}, f32[8,192]{1,0:T(8,128)S(1)}, u32[]{:S(2)}, u32[]{:S(2)}) collective-permute-start(f32[8,192]{1,0:T(8,128)S(1)} %fusion.1), channel_id=1, source_target_pairs={{0,4},{4,0},{8,12},{12,8},{16,20},{20,16},{24,28},{28,24},{1,5},{5... | collective-permute-start | bytes 18440 | tf_op jit(solution)/shard_map/ppermute | solution.py:61
  151.7 4.1 %collective-permute-start.14 = (f32[16,192]{1,0:T(8,128)S(1)}, f32[16,192]{1,0:T(8,128)S(1)}, u32[]{:S(2)}, u32[]{:S(2)}) collective-permute-start(f32[16,192]{1,0:T(8,128)S(1)} %pad_maximum_fusion.4), channel_id=1, source_target_pairs={{0,8},{4,12},{8,0},{12,4},{16,24},{20,28},{24,16},{28,20},{1,9},{5... | collective-permute-start | bytes 36872 | tf_op jit(solution)/shard_map/ppermute | solution.py:61
  153.5 4.8 %collective-permute-start.17 = (f32[6,768]{1,0:T(8,128)S(1)}, f32[6,768]{1,0:T(8,128)S(1)}, u32[]{:S(2)}, u32[]{:S(2)}) collective-permute-start(f32[6,768]{1,0:T(8,128)S(1)} %pad_maximum_fusion.3), channel_id=1, source_target_pairs={{0,4},{4,0},{8,12},{12,8},{16,20},{20,16},{24,28},{28,24},{1,5},{5... | collective-permute-start | bytes 55304 | tf_op jit(solution)/shard_map/ppermute | solution.py:61
  155.8 8.1 %collective-permute-start.15 = (f32[32,192]{1,0:T(8,128)S(1)}, f32[32,192]{1,0:T(8,128)S(1)}, u32[]{:S(2)}, u32[]{:S(2)}) collective-permute-start(f32[32,192]{1,0:T(8,128)S(1)} %pad_maximum_fusion.1), channel_id=1, source_target_pairs={{0,16},{4,20},{8,24},{12,28},{16,0},{20,4},{24,8},{28,12},{1,17},{... | collective-permute-start | bytes 73736 | tf_op jit(solution)/shard_map/ppermute | solution.py:61
  158.2 3.9 %collective-permute-start.18 = (f32[6,768]{1,0:T(8,128)S(1)}, f32[6,768]{1,0:T(8,128)S(1)}, u32[]{:S(2)}, u32[]{:S(2)}) collective-permute-start(f32[6,768]{1,0:T(8,128)S(1)} %fusion.5), channel_id=1, source_target_pairs={{0,8},{4,12},{8,0},{12,4},{16,24},{20,28},{24,16},{28,20},{1,9},{5... | collective-permute-start | bytes 55304 | tf_op jit(solution)/shard_map/ppermute | solution.py:61
  162.1 8.5 %collective-permute-start.19 = (f32[6,768]{1,0:T(8,128)S(1)}, f32[6,768]{1,0:T(8,128)S(1)}, u32[]{:S(2)}, u32[]{:S(2)}) collective-permute-start(f32[6,768]{1,0:T(8,128)S(1)} %add.60), channel_id=1, source_target_pairs={{0,16},{4,20},{8,24},{12,28},{16,0},{20,4},{24,8},{28,12},{1,17},{... | collective-permute-start | bytes 55304 | tf_op jit(solution)/shard_map/ppermute | solution.py:61
  (35 other events, 123.7 us)
Sparse Core Ops, SparseCore 0:
  103.9 149.6 all-reduce.2

commit v2 on v1

v2 whole, which is shorter than its diff:
```python
import functools

import jax
import jax.numpy as jnp
from jax import lax
from jax.experimental import pallas as pl
from jax.experimental.pallas import tpu as pltpu
from jax.sharding import PartitionSpec as P

HEAD_DIM = 64
SHORT = 128
PAIR = 256
EPS = 1e-05
NEG = -1000000000.0
SQRT_HALF = 0.7071067811865476
PHI_ZERO = 0.3989422804014327
VMEM_MB = 16
SMALL_MB = 8

F32 = jnp.float32
BF16 = jnp.bfloat16


def mm(left, right, left_dim, right_dim):
    return lax.dot_general(
        left, right, (((left_dim,), (right_dim,)), ((), ())), preferred_element_type=F32
    )


def params(dims=1):
    return pltpu.CompilerParams(
        dimension_semantics=("arbitrary",) * dims, vmem_limit_bytes=VMEM_MB << 20
    )


COST_SCALE = 0.0


def cost(micros):
    return pl.CostEstimate(flops=int(micros * COST_SCALE * 1e9), bytes_accessed=int(micros * COST_SCALE * 3e6) + 1, transcendentals=0)


def shape(dims, dtype):
    return jax.ShapeDtypeStruct(dims, dtype)


def whole(array):
    zeros = (0,) * array.ndim
    return pl.BlockSpec(array.shape, lambda *_: zeros)


def swap(value, axis, bit, name):
    pairs = [(i, i ^ bit) for i in range(lax.axis_size(axis))]
    with jax.named_scope(name):
        return lax.ppermute(value, axis, pairs)


def core_swap(value, name="core", pieces=1):
    return swap_pieces(value, 1, name, pieces)


def swap_pieces(value, bit, name, pieces):
    if pieces == 1:
        return swap(value, "tensor", bit, name)
    rows = value.shape[0] // pieces
    parts = [swap(value[i * rows : (i + 1) * rows], "tensor", bit, name) for i in range(pieces)]
    return jnp.concatenate(parts, axis=0)


def chip_swap(value, name="chip", pieces=1):
    return swap_pieces(value, 2, name, pieces)


def dp_swap(value, bit, name="dp"):
    return swap(value, "dp", bit, name)


def norm_stats(values):
    mean = jnp.mean(values, axis=-1, keepdims=True)
    centred = values - mean
    variance = jnp.mean(centred * centred, axis=-1, keepdims=True)
    scale = lax.rsqrt(variance + EPS)
    return centred * scale, scale


IDS = 8


def row_fields(info):
    rows = (info.shape[0] - IDS) // 3
    return rows, [lambda r, at=at: info[IDS + at * rows + r] for at in range(3)]


def fill_slots(slot_ref, info):
    group = info[1]
    rows, (row_length, row_group, row_step) = row_fields(info)

    def long_row(r, pos):
        step = row_step(r)
        slot_ref[pos] = step
        slot_ref[pos + 1] = step
        hit = (row_group(r) == group) & (row_length(r) > SHORT)
        return pos + jnp.where(hit, 2, 0)

    def short_row(r, pos):
        slot_ref[pos] = row_step(r)
        hit = (row_group(r) == group) & (row_length(r) <= SHORT)
        return pos + jnp.where(hit, 1, 0)

    long_slots = lax.fori_loop(0, rows, long_row, 0)
    lax.fori_loop(0, rows, short_row, long_slots)
    return long_slots


def block_of(i, ids, chunk, half, chunks):
    side = jnp.where(i < half, 1 - ids[0], ids[0])
    return side * (half * chunks) + chunk * half + lax.rem(i, half)


def add_low(a, b):
    return (a.astype(F32) + b.astype(F32)).astype(BF16)


def row_vector(ref):
    return ref[...].reshape(1, ref.shape[0])


VM = pl.BlockSpec(memory_space=pltpu.VMEM)
ANY = pl.BlockSpec(memory_space=pl.ANY)


def small_call(kernel, out_shape, operands, after, name):
    count = len(operands)
    return pl.pallas_call(
        lambda *refs: kernel(*refs[:count], *refs[count + len(after) :]),
        in_specs=[VM] * count + [ANY] * len(after),
        out_specs=[VM] * len(out_shape),
        out_shape=out_shape,
        compiler_params=pltpu.CompilerParams(vmem_limit_bytes=SMALL_MB << 20),
        cost_estimate=cost(0.2),
        name=name,
    )(*operands, *after)


def add_two(a, b, after, name):
    def kernel(a_ref, b_ref, out):
        out[...] = add_low(a_ref[...], b_ref[...])

    return small_call(kernel, [shape(a.shape, BF16)], [a, b], after, name)[0]


def attend_kernel(
    chunk, half, chunks, slots, ids,
    tokens, table, gain, bias, w_qkv, wo,
    send, keep, hidden_out, normed_out, q_out, k_out, v_out, p_out, c_out,
    slot_ref, rows_ref, sems,
):
    i = pl.program_id(0)

    def fetch(s):
        step = slot_ref[s]
        start = pl.multiple_of((step // 8) * 8, 8)
        return pltpu.make_async_copy(table.at[pl.ds(start, 8), :], rows_ref.at[s], sems.at[s])

    @pl.when(i == 0)
    def _():
        slot_ref[slots + 2] = fill_slots(slot_ref, ids)
        for s in range(slots):
            fetch(s).start()
        for s in range(slots):
            fetch(s).wait()

    block = block_of(i, ids, chunk, half, chunks)
    sub = lax.broadcasted_iota(jnp.int32, (8, 1), 0)

    def row_of(s):
        picked = sub == lax.rem(slot_ref[s], 8)
        return jnp.sum(jnp.where(picked, rows_ref[s].astype(F32), 0.0), axis=0, keepdims=True)

    low_half = lax.broadcasted_iota(jnp.int32, (PAIR, 1), 0) < SHORT
    step_row = jnp.where(low_half, row_of(2 * block), row_of(2 * block + 1))
    hidden = tokens[...].astype(F32) + step_row
    unit, _ = norm_stats(hidden)
    normed = (unit * row_vector(gain) + row_vector(bias)).astype(BF16)
    normed_out[...] = normed
    q = mm(normed, w_qkv[0], 1, 1).astype(BF16)
    k = mm(normed, w_qkv[1], 1, 1).astype(BF16)
    v = mm(normed, w_qkv[2], 1, 1).astype(BF16)
    q_out[...] = q
    k_out[...] = k
    v_out[...] = v
    split = (2 * block >= slot_ref[slots + 2]).astype(jnp.int32)
    row_half = lax.broadcasted_iota(jnp.int32, (PAIR, PAIR), 0) // SHORT
    col_half = lax.broadcasted_iota(jnp.int32, (PAIR, PAIR), 1) // SHORT
    allowed = ((row_half ^ col_half) * split) == 0
    width = q.shape[1]
    head = lax.broadcasted_iota(jnp.int32, (1, width), 1) // HEAD_DIM
    context = jnp.zeros((PAIR, width), F32)
    for h in range(width // HEAD_DIM):
        mine = head == h
        qh = jnp.where(mine, q, jnp.zeros_like(q))
        scores = mm(qh, k, 1, 1) * (HEAD_DIM**-0.5)
        scores = jnp.where(allowed, scores, NEG)
        top = jnp.max(scores, axis=-1, keepdims=True)
        powers = jnp.exp(scores - top)
        total = jnp.sum(powers, axis=-1, keepdims=True)
        weights = (powers * (1.0 / total)).astype(BF16)
        p_out[0, h] = weights
        context = context + mm(weights, jnp.where(mine, v, jnp.zeros_like(v)), 1, 0)
    low = context.astype(BF16)
    c_out[...] = low
    part = mm(low, wo[...], 1, 0).astype(BF16)

    @pl.when(i < half)
    def _():
        send[...] = part

    @pl.when(i >= half)
    def _():
        keep[...] = part
        hidden_out[...] = hidden


def attend(chunk, chunks, scalars, tokens, table, gain, bias, w_qkv, wo, after):
    count, width = tokens.shape
    local = wo.shape[0]
    blocks = count // PAIR // chunks
    half = blocks // 2
    rows = blocks * PAIR
    slots = count // SHORT
    own = rows // 2
    heads = local // HEAD_DIM
    first = lambda i, *_: (jnp.minimum(i, half - 1), 0)
    second = lambda i, *_: (jnp.maximum(i - half, 0), 0)
    step = lambda i, *_: (i, 0)
    row = pl.BlockSpec((PAIR, width), step)
    thin = pl.BlockSpec((PAIR, local), step)
    return pl.pallas_call(
        lambda *refs: attend_kernel(chunk, half, chunks, slots, *refs[:7], *refs[7 + len(after) :]),
        grid_spec=pltpu.PrefetchScalarGridSpec(
            num_scalar_prefetch=1,
            grid=(blocks,),
            in_specs=[
                pl.BlockSpec((PAIR, width), lambda i, ids, *_: (block_of(i, ids, chunk, half, chunks), 0)),
                pl.BlockSpec(memory_space=pltpu.HBM),
                whole(gain), whole(bias), whole(w_qkv), whole(wo),
            ]
            + [ANY] * len(after),
            out_specs=[
                pl.BlockSpec((PAIR, width), first),
                pl.BlockSpec((PAIR, width), second),
                pl.BlockSpec((PAIR, width), second),
                row, thin, thin, thin,
                pl.BlockSpec((1, heads, PAIR, PAIR), lambda i, *_: (i, 0, 0, 0)),
                thin,
            ],
            scratch_shapes=[
                pltpu.SMEM((slots + 4,), jnp.int32),
                pltpu.VMEM((slots, 8, width), BF16),
                pltpu.SemaphoreType.DMA((slots,)),
            ],
        ),
        out_shape=[
            shape((own, width), BF16), shape((own, width), BF16), shape((own, width), F32),
            shape((rows, width), BF16),
            shape((rows, local), BF16), shape((rows, local), BF16), shape((rows, local), BF16),
            shape((blocks, heads, PAIR, PAIR), BF16),
            shape((rows, local), BF16),
        ],
        compiler_params=params(),
        cost_estimate=cost(4.5),
        name="attend",
    )(scalars, tokens, table, gain, bias, w_qkv, wo, *after)


def mid_kernel(hidden, pair, other, gain, bias, residual_out, normed_out):
    residual = hidden[...] + (pair[...].astype(F32) + other[...].astype(F32))
    residual_out[...] = residual
    unit, _ = norm_stats(residual)
    normed_out[...] = (unit * row_vector(gain) + row_vector(bias)).astype(BF16)


def mid_forward(hidden, pair, other, gain, bias, after):
    rows, width = hidden.shape
    row = pl.BlockSpec((PAIR, width), lambda i: (i, 0))
    return pl.pallas_call(
        lambda *refs: mid_kernel(*refs[:5], *refs[5 + len(after) :]),
        grid=(rows // PAIR,),
        in_specs=[row, row, row, whole(gain), whole(bias)] + [ANY] * len(after),
        out_specs=[row, row],
        out_shape=[shape((rows, width), F32), shape((rows, width), BF16)],
        compiler_params=params(),
        cost_estimate=cost(0.4),
        name="mid_forward",
    )(hidden, pair, other, gain, bias, *after)


def expand_kernel(half, ids, peer, own, cot, w_up, up_bias, w_down, send, keep, act_out, low_out, bias_out):
    i = pl.program_id(0)
    normed = jnp.where(i < half, peer[...], own[...])
    pre = mm(normed, w_up[...], 1, 0) + row_vector(up_bias)
    grad_act = mm(cot[...], w_down[...], 1, 1)
    cdf = 0.5 * (1.0 + lax.erf(pre * SQRT_HALF))
    act_out[...] = (pre * cdf).astype(BF16)
    slope = cdf + pre * (PHI_ZERO * jnp.exp(-0.5 * (pre * pre)))
    grad_pre = grad_act * slope

    @pl.when(i == 0)
    def _():
        bias_out[...] = jnp.zeros_like(bias_out)

    bias_out[...] += jnp.sum(grad_pre, axis=0, keepdims=True)
    low = grad_pre.astype(BF16)
    low_out[...] = low
    part = mm(low, w_up[...], 1, 1).astype(BF16)

    @pl.when(i < half)
    def _():
        send[...] = part

    @pl.when(i >= half)
    def _():
        keep[...] = part


def expand(chunk, chunks, ids, peer, own, cot, w_up, up_bias, w_down, after):
    count, width = cot.shape
    local = w_up.shape[1]
    blocks = count // PAIR // chunks
    half = blocks // 2
    rows = blocks * PAIR
    first = lambda i, *_: (jnp.minimum(i, half - 1), 0)
    second = lambda i, *_: (jnp.maximum(i - half, 0), 0)
    step = lambda i, *_: (i, 0)
    return pl.pallas_call(
        lambda *refs: expand_kernel(half, *refs[:7], *refs[7 + len(after) :]),
        grid_spec=pltpu.PrefetchScalarGridSpec(
            num_scalar_prefetch=1,
            grid=(blocks,),
            in_specs=[
                pl.BlockSpec((PAIR, width), first),
                pl.BlockSpec((PAIR, width), second),
                pl.BlockSpec((PAIR, width), lambda i, ids: (block_of(i, ids, chunk, half, chunks), 0)),
                whole(w_up), whole(up_bias), whole(w_down),
            ]
            + [ANY] * len(after),
            out_specs=[
                pl.BlockSpec((PAIR, width), first),
                pl.BlockSpec((PAIR, width), second),
                pl.BlockSpec((PAIR, local), step),
                pl.BlockSpec((PAIR, local), step),
                pl.BlockSpec((1, local), lambda i, *_: (0, 0)),
            ],
        ),
        out_shape=[
            shape((rows // 2, width), BF16), shape((rows // 2, width), BF16),
            shape((rows, local), BF16), shape((rows, local), BF16),
            shape((1, local), F32),
        ],
        compiler_params=params(),
        cost_estimate=cost(3.7),
        name="expand",
    )(ids, peer, own, cot, w_up, up_bias, w_down, *after)


def contract_kernel(act, w_down, send, keep):
    i = pl.program_id(0)
    part = mm(act[...], w_down[...], 1, 0).astype(BF16)

    @pl.when(i < 2)
    def _():
        send[...] = part

    @pl.when(i >= 2)
    def _():
        keep[...] = part


def contract_rows(act, w_down, after):
    rows, local = act.shape
    width = w_down.shape[1]
    return pl.pallas_call(
        lambda *refs: contract_kernel(*refs[:2], *refs[2 + len(after) :]),
        grid=(rows // PAIR,),
        in_specs=[pl.BlockSpec((PAIR, local), lambda i: (i, 0)), whole(w_down)] + [ANY] * len(after),
        out_specs=[
            pl.BlockSpec((PAIR, width), lambda i: (jnp.minimum(i, 1), 0)),
            pl.BlockSpec((PAIR, width), lambda i: (jnp.maximum(i - 2, 0), 0)),
        ],
        out_shape=[shape((rows // 2, width), BF16), shape((rows // 2, width), BF16)],
        compiler_params=params(),
        cost_estimate=cost(2.1),
        name="contract_rows",
    )(act, w_down, *after)


def weight_kernel(order, groups, ids, *refs):
    count = sum(len(lefts) for lefts in groups)
    left, right = refs[:count], refs[count : 2 * count]
    send, keep, scratch = refs[2 * count : 2 * count + 3]
    i = pl.program_id(0)
    many = len(groups) > 1
    rows = send.shape[-2]
    at = 0
    for n, sizes in enumerate(groups):
        total = mm(left[at][...], right[at][...], 0, 0)
        for j in range(at + 1, at + len(sizes)):
            total = total + mm(left[j][...], right[j][...], 0, 0)
        at += len(sizes)
        scratch[n] = total

    def write(out):
        for r in range(4):
            start = pl.multiple_of((ids[order + 1] ^ r) * rows, 8)
            for n in range(len(groups)):
                value = scratch[n, pl.ds(start, rows), :].astype(BF16)
                if many:
                    out[r, n] = value
                else:
                    out[r] = value

    @pl.when(i == 0)
    def _():
        write(send)

    @pl.when(i == 1)
    def _():
        write(keep)


def weight_grad(ids, order, groups, after, name):
    rows_out = groups[0][0][0][0].shape[1]
    tile = rows_out // 2
    part = tile // 4
    cols = groups[0][0][1][0].shape[1]
    lefts = [left for pieces in groups for left, _ in pieces]
    rights = [right for pieces in groups for _, right in pieces]
    count = sum(size for _, size, _ in lefts)

    def column(i, ids):
        return jnp.where(i == 0, 1 - ids[order], ids[order])

    specs = [pl.BlockSpec((size, tile), lambda i, ids, at=at: (at(ids), column(i, ids))) for _, size, at in lefts]
    specs += [pl.BlockSpec((size, cols), lambda i, ids, at=at: (at(ids), 0)) for _, size, at in rights]
    dims = (4, part, cols) if len(groups) == 1 else (4, len(groups), part, cols)
    out = pl.BlockSpec(dims, lambda i, ids: (0,) * len(dims))
    kernel = functools.partial(weight_kernel, order, [[size for (_, size, _), _ in g] for g in groups])
    total = len(lefts)
    return list(pl.pallas_call(
        lambda ids, *refs: kernel(ids, *refs[: 2 * total], *refs[2 * total + len(after) :]),
        grid_spec=pltpu.PrefetchScalarGridSpec(
            num_scalar_prefetch=1,
            grid=(2,),
            in_specs=specs + [ANY] * len(after),
            out_specs=[out, out],
            scratch_shapes=[pltpu.VMEM((len(groups), tile, cols), F32)],
        ),
        out_shape=[shape(dims, BF16), shape(dims, BF16)],
        compiler_params=params(),
        cost_estimate=cost(2.5),
        name=name,
    )(ids, *[a for a, _, _ in lefts], *[b for b, _, _ in rights], *after))


def head_grad(ids, order, first, second, after, name):
    rows_out, cols = first[0][0].shape[1], first[0][1].shape[1]
    part = rows_out // 8
    pieces = [len(first), len(second)]
    flat = [x for pair in (*first, *second) for x in pair]

    def kernel(ids_ref, *refs):
        values = refs[: len(flat)]
        send, keep, scratch = refs[len(flat) + len(after) :]
        at = 0
        for n in range(2):
            total = jnp.zeros((rows_out, cols), F32)
            for _ in range(pieces[n]):
                total = total + mm(values[at][...], values[at + 1][...], 0, 0)
                at += 2
            scratch[n] = total
        for half, out in ((1 - ids_ref[order], send), (ids_ref[order], keep)):
            for r in range(4):
                start = pl.multiple_of((half * 4 + (ids_ref[order + 1] ^ r)) * part, 8)
                for n in range(2):
                    out[r, n] = scratch[n, pl.ds(start, part), :].astype(BF16)

    dims = (4, 2, part, cols)
    return pl.pallas_call(
        kernel,
        grid_spec=pltpu.PrefetchScalarGridSpec(
            num_scalar_prefetch=1,
            grid=(1,),
            in_specs=[VM] * len(flat) + [ANY] * len(after),
            out_specs=[VM, VM],
            scratch_shapes=[pltpu.VMEM((2, rows_out, cols), F32)],
        ),
        out_shape=[shape(dims, BF16), shape(dims, BF16)],
        compiler_params=params(),
        cost_estimate=cost(0.2),
        name=name,
    )(ids, *flat, *after)


class Dual:
    def __init__(self, bits, direct, name):
        self.bits, self.direct, self.name, self.level = bits, direct, name, 0
        self.halves, self.got = [None, None], [None, None]

    def begin(self, which, halves):
        self.halves[which] = list(halves)
        if self.direct:
            self.got[which] = dp_swap(halves[0], self.bits[which][0], f"{self.name}_start_{which}")

    def step(self, after):
        if not self.direct:
            return after
        (_, keep_a), (_, keep_b) = self.halves
        level, name = self.level, f"{self.name}_{self.level}"
        self.level += 1
        first, second = self.bits
        if level < 2:
            parts, rest = keep_a.shape[0], keep_a.shape[1:]
            half = parts // 2
            if level == 0:

                def kernel(ka, ga, kb, gb, sa, oa, sb, ob):
                    for k, g, send, out in ((ka, ga, sa, oa), (kb, gb, sb, ob)):
                        send[...] = add_low(k[half:], g[half:])
                        out[...] = add_low(k[:half], g[:half])

                out = [shape((half, *rest), BF16)] * 4
                sa, oa, sb, ob = small_call(kernel, out, [keep_a, self.got[0], keep_b, self.got[1]], [after], name)
                self.halves = [[sa, oa], [sb, ob]]
                self.got = [dp_swap(sa, first[1], name + "_a"), dp_swap(sb, second[1], name + "_b")]
                return oa

            def kernel(ka, ga, kb, gb, out):
                for n, (k, g) in enumerate(((ka, ga), (kb, gb))):
                    out[n] = add_low(k[...], g[...])

            out = [shape((2, parts, *rest), BF16)]
            both = small_call(kernel, out, [keep_a, self.got[0], keep_b, self.got[1]], [after], name)[0]
            self.halves = [[None, both], [None, both]]
            self.got = [dp_swap(both, first[2], name + "_far"), None]
            return both
        if level == 2:

            def kernel(k, g, oa, ob):
                for n, out in enumerate((oa, ob)):
                    for j in range(2):
                        out[j] = add_low(k[n, j], g[n, 1 - j])

            out = [shape(keep_a.shape[1:], BF16)] * 2
            oa, ob = small_call(kernel, out, [keep_a, self.got[0]], [after], name)
            self.halves = [[None, oa], [None, ob]]
            self.got = [dp_swap(oa, first[1], name + "_a"), dp_swap(ob, second[1], name + "_b")]
            return oa
        rest = keep_a.shape[1:]

        def kernel(ka, ga, kb, gb, oa, ob):
            for k, g, out in ((ka, ga, oa), (kb, gb, ob)):
                out[:2] = k[...]
                out[2:] = g[...]

        out = [shape((4, *rest), BF16)] * 2
        oa, ob = small_call(kernel, out, [keep_a, self.got[0], keep_b, self.got[1]], [after], name)
        self.halves = [[None, oa], [None, ob]]
        self.got = [dp_swap(oa, first[0], name + "_a"), dp_swap(ob, second[0], name + "_b")]
        return oa

    def collect(self, which):
        if not self.direct:
            send, keep = lax.psum(tuple(self.halves[which]), "dp")
            return keep, send
        return self.halves[which][1], self.got[which]


def place_half(ids, order, value, flip, base, after, name):
    _, part, cols = value.shape
    rows = 8 * part
    given = [] if base is None else [pltpu.with_memory_space_constraint(base, pltpu.HBM)]

    def kernel(ids_ref, value_ref, *refs):
        out = refs[-1]
        for r in range(4):
            start = pl.multiple_of((ids_ref[order + 1] ^ r) * part, 8)
            out[pl.ds(start, part), :] = value_ref[r].astype(F32)

    return pl.pallas_call(
        kernel,
        grid_spec=pltpu.PrefetchScalarGridSpec(
            num_scalar_prefetch=1,
            grid=(1,),
            in_specs=[VM] + [ANY] * (len(given) + len(after)),
            out_specs=pl.BlockSpec((4 * part, cols), lambda i, ids: (ids[order] ^ flip, 0)),
        ),
        out_shape=pltpu.HBM((rows, cols), F32),
        input_output_aliases={2: 0} if given else {},
        compiler_params=params(),
        cost_estimate=cost(1.6),
        name=name,
    )(ids, value, *given, *after)


def place_heads(ids, orders, a, b, after):
    _, _, part, cols = a[0].shape
    rows = 8 * part

    def kernel(ids_ref, near_a, far_a, near_b, far_b, *refs):
        qkv_out, proj_out = refs[len(after) :]
        for half in range(2):
            for n, (pick, order) in enumerate((((near_a, far_a), orders[0]), ((near_b, far_b), orders[1]))):
                for r in range(4):
                    at = (ids_ref[order] ^ half) * 4 + (ids_ref[order + 1] ^ r)
                    at = pl.ds(pl.multiple_of(at * part, 8), part)
                    if n == 0:
                        qkv_out[0, at, :] = pick[half][r, 0].astype(F32)
                        qkv_out[1, at, :] = pick[half][r, 1].astype(F32)
                    else:
                        qkv_out[2, at, :] = pick[half][r, 0].astype(F32)
                        proj_out[at, :] = pick[half][r, 1].astype(F32)

    return pl.pallas_call(
        kernel,
        grid_spec=pltpu.PrefetchScalarGridSpec(
            num_scalar_prefetch=1,
            grid=(1,),
            in_specs=[VM] * 4 + [ANY] * len(after),
            out_specs=[
                pl.BlockSpec((3, rows, cols), lambda *_: (0, 0, 0)),
                pl.BlockSpec((rows, cols), lambda *_: (0, 0)),
            ],
        ),
        out_shape=[pltpu.HBM((3, rows, cols), F32), pltpu.HBM((rows, cols), F32)],
        compiler_params=params(),
        cost_estimate=cost(2.1),
        name="place_heads",
    )(ids, *a, *b, *after)


def mid_back_kernel(pair, other, residual, cot, gain, grad_out, low_out, sums):
    i = pl.program_id(0)
    err = pair[...].astype(F32) + other[...].astype(F32)
    unit, scale = norm_stats(residual[...])
    top = cot[...].astype(F32)
    f = err * row_vector(gain)
    f_mean = jnp.mean(f, axis=-1, keepdims=True)
    fx_mean = jnp.mean(f * unit, axis=-1, keepdims=True)
    grad = top + scale * (f - f_mean - unit * fx_mean)
    grad_out[...] = grad
    low_out[...] = grad.astype(BF16)

    @pl.when(i == 0)
    def _():
        sums[...] = jnp.zeros_like(sums)

    sums[0:1] += jnp.sum(err * unit, axis=0, keepdims=True)
    sums[1:2] += jnp.sum(err, axis=0, keepdims=True)
    sums[2:3] += jnp.sum(top, axis=0, keepdims=True)


def mid_back(chunk, chunks, ids, pair, other, residual, cot, gain, after):
    rows, width = residual.shape
    half = rows // PAIR
    row = pl.BlockSpec((PAIR, width), lambda i, ids: (i, 0))
    return pl.pallas_call(
        lambda ids, *refs: mid_back_kernel(*refs[:5], *refs[5 + len(after) :]),
        grid_spec=pltpu.PrefetchScalarGridSpec(
            num_scalar_prefetch=1,
            grid=(half,),
            in_specs=[
                row, row, row,
                pl.BlockSpec((PAIR, width), lambda i, ids: (block_of(i + half, ids, chunk, half, chunks), 0)),
                whole(gain),
            ]
            + [ANY] * len(after),
            out_specs=[row, row, pl.BlockSpec((8, width), lambda i, ids: (0, 0))],
        ),
        out_shape=[shape((rows, width), F32), shape((rows, width), BF16), shape((8, width), F32)],
        compiler_params=params(),
        cost_estimate=cost(1.2),
        name="mid_back",
    )(ids, pair, other, residual, cot, gain, *after)


def attend_back_kernel(half, peer, own, q_ref, k_ref, v_ref, p_ref, w_qkv, wo, send, keep, dq_out, dk_out, dv_out):
    i = pl.program_id(0)
    low = jnp.where(i < half, peer[...], own[...])
    grad_context = mm(low, wo[...], 1, 1).astype(BF16)
    q, k, v = q_ref[...], k_ref[...], v_ref[...]
    width = q.shape[1]
    head = lax.broadcasted_iota(jnp.int32, (1, width), 1) // HEAD_DIM
    zero = jnp.zeros_like(q)
    dq = dk = dv = jnp.zeros((PAIR, width), F32)
    for h in range(width // HEAD_DIM):
        mine = head == h
        gh = jnp.where(mine, grad_context, zero)
        weights = p_ref[0, h]
        grad_p = mm(gh, v, 1, 1)
        wide = weights.astype(F32)
        dot = jnp.sum(wide * grad_p, axis=-1, keepdims=True)
        grad_s = (wide * (grad_p - dot)).astype(BF16)
        dv = dv + mm(weights, gh, 0, 0)
        dq = dq + mm(grad_s, jnp.where(mine, k, zero), 1, 0)
        dk = dk + mm(grad_s, jnp.where(mine, q, zero), 0, 0)
    scale = HEAD_DIM**-0.5
    dq = (dq * scale).astype(BF16)
    dk = (dk * scale).astype(BF16)
    dv = dv.astype(BF16)
    dq_out[...] = dq
    dk_out[...] = dk
    dv_out[...] = dv
    part = (mm(dq, w_qkv[0], 1, 0) + mm(dk, w_qkv[1], 1, 0) + mm(dv, w_qkv[2], 1, 0)).astype(BF16)

    @pl.when(i < half)
    def _():
        send[...] = part

    @pl.when(i >= half)
    def _():
        keep[...] = part


def attend_back(peer, own, q, k, v, p, w_qkv, wo, after):
    rows, local = q.shape
    width = wo.shape[1]
    blocks = rows // PAIR
    half = blocks // 2
    heads = local // HEAD_DIM
    first = pl.BlockSpec((PAIR, width), lambda i: (jnp.minimum(i, half - 1), 0))
    second = pl.BlockSpec((PAIR, width), lambda i: (jnp.maximum(i - half, 0), 0))
    thin = pl.BlockSpec((PAIR, local), lambda i: (i, 0))
    return pl.pallas_call(
        lambda *refs: attend_back_kernel(half, *refs[:8], *refs[8 + len(after) :]),
        grid=(blocks,),
        in_specs=[
            first, second, thin, thin, thin,
            pl.BlockSpec((1, heads, PAIR, PAIR), lambda i: (i, 0, 0, 0)),
            whole(w_qkv), whole(wo),
        ]
        + [ANY] * len(after),
        out_specs=[first, second, thin, thin, thin],
        out_shape=[
            shape((rows // 2, width), BF16), shape((rows // 2, width), BF16),
            shape((rows, local), BF16), shape((rows, local), BF16), shape((rows, local), BF16),
        ],
        compiler_params=params(),
        cost_estimate=cost(3.5),
        name="attend_back",
    )(peer, own, q, k, v, p, w_qkv, wo, *after)


def last_kernel(pair, other, hidden, grad_residual, gain, low_out, sums, times):
    i = pl.program_id(0)
    err = pair[...].astype(F32) + other[...].astype(F32)
    unit, scale = norm_stats(hidden[...])
    f = err * row_vector(gain)
    f_mean = jnp.mean(f, axis=-1, keepdims=True)
    fx_mean = jnp.mean(f * unit, axis=-1, keepdims=True)
    grad = grad_residual[...] + scale * (f - f_mean - unit * fx_mean)
    low_out[...] = grad.astype(BF16)

    @pl.when(i == 0)
    def _():
        sums[...] = jnp.zeros_like(sums)

    sums[0:1] += jnp.sum(err * unit, axis=0, keepdims=True)
    sums[1:2] += jnp.sum(err, axis=0, keepdims=True)
    times[0, 0:1] = jnp.sum(grad[:SHORT], axis=0, keepdims=True)
    times[0, 1:2] = jnp.sum(grad[SHORT:], axis=0, keepdims=True)


def last_back(pair, other, hidden, grad_residual, gain, after):
    rows, width = hidden.shape
    half = rows // PAIR
    row = pl.BlockSpec((PAIR, width), lambda i: (i, 0))
    return pl.pallas_call(
        lambda *refs: last_kernel(*refs[:5], *refs[5 + len(after) :]),
        grid=(half,),
        in_specs=[row, row, row, row, whole(gain)] + [ANY] * len(after),
        out_specs=[
            row,
            pl.BlockSpec((8, width), lambda i: (0, 0)),
            pl.BlockSpec((1, 2, width), lambda i: (i, 0, 0)),
        ],
        out_shape=[shape((rows, width), BF16), shape((8, width), F32), shape((half, 2, width), F32)],
        compiler_params=params(),
        cost_estimate=cost(0.7),
        name="last_back",
    )(pair, other, hidden, grad_residual, gain, *after)


def pack_sums(vec2, vec1, up, times, after):
    pairs, _, width = times.shape

    def kernel(v2, v1, u, t, out):
        out[0:3] = v2[0:3]
        out[3:5] = v1[0:2]
        out[5:6] = u[...]
        out[6:8] = jnp.zeros((2, width), F32)
        for n in range(pairs):
            out[8 + 2 * n : 10 + 2 * n] = t[n]

    return small_call(kernel, [shape((8 + 2 * pairs, width), F32)], [vec2, vec1, up, times], after, "pack_sums")[0]


def join_sums(a, b, after, name):
    rows, width = a.shape
    more = rows - 8

    def kernel(a_ref, b_ref, out):
        out[0:8] = a_ref[0:8] + b_ref[0:8]
        out[8 : 8 + more] = a_ref[8:]
        out[8 + more :] = b_ref[8:]

    return small_call(kernel, [shape((8 + 2 * more, width), F32)], [a, b], after, name)[0]


def table_kernel(slots, steps, ids, own, other, vec_out, out, table, acc, at_ref):
    groups = at_ref.shape[0]
    rows, (row_length, row_group, row_step) = row_fields(ids)
    local = table.shape[2]
    half = slots // 2
    vec_out[...] = own[0:8] + other[0:8]
    vec_out[5:6] = own[5:6]
    for p in range(own.shape[1] // local):

        @pl.when(ids[2] == p)
        def _():
            table[0] = own[8:, p * local : (p + 1) * local]
            table[1] = other[8:, p * local : (p + 1) * local]

    acc[...] = jnp.zeros_like(acc)

    def clear(g, _):
        at_ref[g] = 0
        return 0

    lax.fori_loop(0, groups, clear, 0)

    def place(long):
        def one(r, _):
            @pl.when((row_length(r) > SHORT) == long)
            def _():
                g = row_group(r)
                at = at_ref[g]
                at_ref[g] = at + (2 if long else 1)
                which = (at // half) ^ ids[0]
                base = (g ^ ids[1]) * half + lax.rem(at, half)
                value = table[which, pl.ds(base, 1), :]
                if long:
                    value = value + table[which, pl.ds(base + 1, 1), :]
                step = pl.ds(row_step(r), 1)
                acc[step, :] = acc[step, :] + value

            return 0

        lax.fori_loop(0, rows, one, 0)

    place(True)
    place(False)
    out[...] = jnp.transpose(acc[...])[:, :steps]


def table_grad(scalars, own, other, steps, local, slots, after):
    rows, width = own.shape
    groups = (rows - 8) * 2 // slots
    return pl.pallas_call(
        lambda *refs: table_kernel(slots, steps, *refs[:3], *refs[3 + len(after) :]),
        grid_spec=pltpu.PrefetchScalarGridSpec(
            num_scalar_prefetch=1,
            grid=(1,),
            in_specs=[VM, VM] + [ANY] * len(after),
            out_specs=[pl.BlockSpec((8, width), lambda *_: (0, 0)), pl.BlockSpec((local, steps), lambda *_: (0, 0))],
            scratch_shapes=[
                pltpu.VMEM((2, rows - 8, local), F32),
                pltpu.VMEM((pl.cdiv(steps, 128) * 128, local), F32),
                pltpu.SMEM((groups,), jnp.int32),
            ],
        ),
        out_shape=[shape((8, width), F32), pltpu.HBM((local, steps), F32)],
        compiler_params=params(),
        cost_estimate=cost(3.9),
        name="table_grad",
    )(scalars, own, other, *after)


def finish(residuals, pair, other, bias, after):
    rows, width = pair.shape
    part = rows // len(residuals)

    def kernel(*refs):
        res = refs[: len(residuals)]
        pair_ref, other_ref, bias_ref = refs[len(residuals) : len(residuals) + 3]
        out = refs[-1]
        for n, r in enumerate(res):
            at = slice(n * part, (n + 1) * part)
            total = r[...] + (pair_ref[at].astype(F32) + other_ref[at].astype(F32))
            out[at] = (total + row_vector(bias_ref)).astype(BF16)

    return small_call(kernel, [shape((rows, width), BF16)], [*residuals, pair, other, bias], after, "finish")[0]


def order_rows(ids, own, other, after, name):
    count = len(own)
    part, width = own[0].shape

    def kernel(ids_ref, *refs):
        out = refs[-1]
        i = pl.program_id(0)
        for n in range(2 * count):

            @pl.when(i == n)
            def _():
                out[...] = refs[n][...]

    return pl.pallas_call(
        kernel,
        grid_spec=pltpu.PrefetchScalarGridSpec(
            num_scalar_prefetch=1,
            grid=(2 * count,),
            in_specs=[VM] * (2 * count) + [ANY] * len(after),
            out_specs=pl.BlockSpec(
                (part, width), lambda i, ids: ((ids[0] ^ (i // count)) * count + lax.rem(i, count), 0)
            ),
        ),
        out_shape=pltpu.HBM((2 * count * part, width), BF16),
        compiler_params=params(),
        cost_estimate=cost(2.0),
        name=name,
    )(ids, *own, *other, *after)


def shards(
    tokens, row_length, row_group, row_step, time_table, norm1_gain, norm1_bias, w_qkv, w_out,
    norm2_gain, norm2_bias, w_up, up_bias, w_down, down_bias, cotangent,
):
    count, width = tokens.shape
    n_dp = lax.axis_size("dp")
    dp = lax.axis_index("dp")
    part = lax.axis_index("tensor")
    core = lax.rem(part, 2)
    direct = n_dp == 8
    low_bit, mid_bit, top_bit = dp & 1, (dp >> 1) & 1, (dp >> 2) & 1
    if direct:
        orders = [low_bit, 2 * mid_bit + top_bit, mid_bit, 2 * low_bit + top_bit]
    else:
        orders = [1, 0, 1, 0]
    ids = jnp.stack([core, dp, part, *[jnp.int32(o) for o in orders], jnp.int32(0)]).astype(jnp.int32)
    scalars = jnp.concatenate([ids, row_length, row_group, row_step])
    order_a, order_b = 3, 5
    bits = ((1, 2, 4), (2, 1, 4))
    local = w_out.shape[0]
    slots = count // SHORT
    heads = jnp.transpose(w_qkv, (1, 2, 0))
    far = lambda x: pltpu.with_memory_space_constraint(x, pltpu.HBM)
    size = count // 2
    peer_rows = lambda ids: 1 - ids[0]
    own_rows = lambda ids: ids[0]
    zero = lambda ids: 0
    one = lambda ids: 1

    send, keep, hidden, normed, q, k, v, p, ctx = attend(
        0, 1, scalars, *[far(x) for x in (tokens, time_table, norm1_gain, norm1_bias, heads, w_out)], []
    )
    pair = add_two(keep, core_swap(send, "core_one"), [], "pair_one")
    residual, own2 = mid_forward(hidden, pair, chip_swap(pair, "chip_one"), norm2_gain, norm2_bias, [])
    peer2 = core_swap(own2, "core_norm")
    send, keep, act, low, up_sum = expand(0, 1, ids, peer2, own2, far(cotangent), far(w_up), up_bias, far(w_down), [])
    got = core_swap(send, "core_two")
    cots = [(cotangent, size, f) for f in (peer_rows, own_rows)]
    acts = [(act, size, f) for f in (zero, one)]
    lows = [(low, size, f) for f in (zero, one)]
    norms = [(peer2, size, zero), (own2, size, zero)]
    down = weight_grad(ids, order_a, [list(zip(acts, cots))], [keep], "down_grad")
    mlp = Dual(bits, direct, "mlp")
    mlp.begin(0, down)
    pair = add_two(keep, got, [down[1]], "pair_two")
    other = chip_swap(pair, "chip_two")
    up = weight_grad(ids, order_b, [list(zip(norms, lows))], [pair], "up_grad")
    mlp.begin(1, up)
    send_e, keep_e = contract_rows(act, w_down, [up[1]])
    got_e = core_swap(send_e, "core_out", 4)
    mark = mlp.step(keep_e)
    grad_residual, low_own, vec2 = mid_back(0, 1, ids, pair, other, residual, cotangent, norm2_gain, [mark])
    low_peer = core_swap(low_own, "core_low", 4)
    send, keep, dq, dk, dv = attend_back(low_peer, low_own, q, k, v, p, heads, w_out, [])
    got = core_swap(send, "core_three", 4)
    heads_sum = Dual(bits, direct, "heads")
    mark = mlp.step(keep)
    qk = head_grad(ids, order_a, [(dq, normed)], [(dk, normed)], [mark], "qk_grad")
    heads_sum.begin(0, qk)
    pair = add_two(keep, got, [qk[1]], "pair_three")
    other = chip_swap(pair, "chip_three", 2)
    mark = pair
    lows1 = jnp.concatenate([low_peer, low_own], axis=0)
    vo = head_grad(ids, order_b, [(dv, normed)], [(ctx, lows1)], [mark], "vo_grad")
    heads_sum.begin(1, vo)
    mark = heads_sum.step(vo[1])
    low_in, vec1, times = last_back(pair, other, hidden, grad_residual, norm1_gain, [mark])
    low_got = core_swap(low_in, "core_input", 4)
    sums = pack_sums(vec2, vec1, up_sum, times, [low_in])
    sums_got = dp_swap(sums, 1, "sums_0")
    mark = heads_sum.step(sums)
    pair_e = add_two(keep_e, got_e, [mark], "pair_out")
    other_e = chip_swap(pair_e, "chip_out", 2)
    mark = mlp.step(pair_e)
    sums = join_sums(sums, sums_got, [mark], "join_sums_0")
    sums_got = dp_swap(sums, 2, "sums_1")
    input_grad = order_rows(ids, [low_in], [low_got], [sums], "order_input")
    sums = join_sums(sums, sums_got, [far(input_grad)], "join_sums_1")
    sums_got = dp_swap(sums, 4, "sums_2")
    mark = heads_sum.step(sums)
    mark = mlp.step(mark)
    near_down, far_down = mlp.collect(0)
    near_up, far_up = mlp.collect(1)
    down_out = place_half(ids, order_a, near_down, 0, None, [mark], "place_down_0")
    up_out = place_half(ids, order_b, near_up, 0, None, [far(down_out)], "place_up_0")
    sums = join_sums(sums, sums_got, [far(up_out)], "join_sums_2")
    bit = 8
    while bit < n_dp:
        sums = join_sums(sums, dp_swap(sums, bit), [], f"join_sums_{bit}")
        bit *= 2
    sums_peer = core_swap(sums, "core_sums")
    mark = heads_sum.step(sums)
    final = finish([residual], pair_e, other_e, down_bias, [mark])
    final_got = core_swap(final, "core_final", 4)
    vec, time_grad = table_grad(scalars, sums, sums_peer, time_table.shape[0], local, slots, [final])
    down_out = place_half(ids, order_a, far_down, 1, down_out, [vec], "place_down_1")
    up_out = place_half(ids, order_b, far_up, 1, up_out, [far(down_out)], "place_up_1")
    qkv_out, proj_out = place_heads(ids, (order_a, order_b), heads_sum.collect(0), heads_sum.collect(1), [far(up_out)])
    block_output = order_rows(ids, [final], [final_got], [far(proj_out)], "order_output")

    return (
        block_output,
        input_grad,
        time_grad.T,
        vec[3],
        vec[4],
        jnp.transpose(qkv_out, (2, 0, 1)),
        proj_out,
        vec[0],
        vec[1],
        up_out,
        vec[5],
        down_out,
        vec[2],
    )


def solution(mesh):
    in_specs = (
        P("dp", None), P(), P(), P(), P(), P(), P(), P(None, None, "tensor"), P("tensor", None), P(), P(),
        P(None, "tensor"), P("tensor"), P("tensor", None), P(), P("dp", None),
    )
    out_specs = (
        P("dp", None), P("dp", None), P(None, "tensor"), P(), P(), P(None, None, "tensor"), P("tensor", None),
        P(), P(), P(None, "tensor"), P("tensor"), P("tensor", None), P(),
    )
    return jax.shard_map(shards, mesh=mesh, in_specs=in_specs, out_specs=out_specs, check_vma=False)
```

time: 268 us -> 179 us (0.67)
  waiting for transfers between devices: 158 us -> 73.9 us
  starting transfers between devices: 19.7 us -> 40.6 us
  other arithmetic: 19.6 us -> 0.37 us
  Pallas kernels: 45.3 us -> 59.9 us
  between operations: 14.6 us -> 1.27 us
  local copies, waits for them, and re-layouts: 10.1 us -> 2.87 us
    psum x1 -> x0, waiting for transfers between devices: 79.2 us -> none  [shards(): qkv_sum, out_sum = lax.psum((jnp.stack(qkv), out_grad), 'dp')]
    ppermute x20 -> x51, starting transfers between devices: 19.7 us -> 40.6 us  [swap(): return lax.ppermute(value, axis, pairs)]
    pallas_call x14 -> x36, Pallas kernels: 45.3 us -> 59.9 us  [the longest x1 9.79 us: attend(): pl.pallas_call(lambda *refs: attend_kernel(chunk, half, chunks, slots, *r...]
    convert_element_type x9 -> x0, other arithmetic: 13.1 us -> none  [the longest x4 3.92 us: add_low(): return (a.astype(F32) + b.astype(F32)).astype(BF16)]
    unnamed x81 -> x46, local copies, waits for them, and re-layouts: 8.21 us -> 0.95 us
    select_n x3 -> x0, other arithmetic: 6.33 us -> none  [in_order(): jnp.where(core == 0, jnp.concatenate([own, other], axis=0), jnp.concatena...]
    ppermute x20 -> x51, waiting for transfers between devices: 78.9 us -> 73.9 us  [swap(): return lax.ppermute(value, axis, pairs)]
  transfers between devices with their start and end apart: 21 -> 51, of which waited for: 12 -> 18; matrix products, arithmetic and copies ran while one was open for 6% -> 1% of each run, Pallas kernels for 10% -> 19%
where the time goes in v2:
time: 179 us
  waiting for transfers between devices  73.9 us (41%)
  Pallas kernels  59.9 us (33%)
  starting transfers between devices  40.6 us (23%)
  local copies, waits for them, and re-layouts  2.87 us (2%)
    ppermute x51, waiting for transfers between devices, swap(): return lax.ppermute(value, axis, pairs)  73.9 us
    ppermute x51, starting transfers between devices, swap(): return lax.ppermute(value, axis, pairs)  40.6 us
    pallas_call x1, Pallas kernels, attend(): pl.pallas_call(lambda *refs: attend_kernel(chunk, half, chunks, slots, *r...  9.79 us
    pallas_call x1, Pallas kernels, expand(): pl.pallas_call(lambda *refs: expand_kernel(half, *refs[:7], *refs[7 + len...  8.99 us
    pallas_call x1, Pallas kernels, attend_back(): pl.pallas_call(lambda *refs: attend_back_kernel(half, *refs[:8], *refs[8...  7.02 us
    pallas_call x4, Pallas kernels, place_half(): pl.pallas_call(kernel, grid_spec=pltpu.PrefetchScalarGridSpec(num_scalar_...  6.54 us
    pallas_call x2, Pallas kernels, weight_grad(): pl.pallas_call(lambda ids, *refs: kernel(ids, *refs[:2 * total], *refs[2...  5.96 us
    pallas_call x1, Pallas kernels, table_grad(): pl.pallas_call(lambda *refs: table_kernel(slots, steps, *refs[:3], *refs[...  3.97 us
  transfers between devices with their start and end apart: 51, of which 18 were waited for; matrix products, arithmetic and copies ran while one was open for 1% of the time, Pallas kernels for 19%

profile of v2, /device:TPU:0, one launch (start us, length us, event | category | flops | bytes accessed | tf_op | source)
XLA Modules:
  0.0 179.0 jit_solution(6168417022447311551)
XLA Ops:
  1.4 9.8 %attend.1 = (bf16[512,768]{1,0:T(8,128)(2,1)S(1)}, bf16[512,768]{1,0:T(8,128)(2,1)S(1)}, f32[512,768]{1,0:T(8,128)S(1)}, bf16[1024,768]{1,0:T(8,128)(2,1)S(1)}, ...) custom-call(s32[152]{0:T(256)S(1)} %concatenate.29.refs_0_, ...), custom_call_target="tpu_custom_call" | custom-call | bytes 1 | tf_op jit(solution)/shard_map/attend/pallas_call | solution.py:238
  14.7 3.0 %collective-permute-start.1 = (bf16[512,768]{1,0:T(8,128)(2,1)S(1)}, bf16[512,768]{1,0:T(8,128)(2,1)S(1)}, u32[]{:S(2)}, u32[]{:S(2)}) collective-permute-start(bf16[512,768]{1,0:T(8,128)(2,1)S(1)} %pair_one.1.refs_1_), channel_id=1, source_target_pairs={{0,2},{1,3},{2,0},{3,1},{4,6},{5,7},{6,4},{7,5},{8,10},{9,11},{10,... | collective-permute-start | bytes 2359304 | tf_op jit(solution)/shard_map/chip_one/ppermute | solution.py:55
  17.6 17.8 %collective-permute-done.1.refs_2_ = bf16[512,768]{1,0:T(8,128)(2,1)S(1)} collective-permute-done((bf16[512,768]{1,0:T(8,128)(2,1)S(1)}, bf16[512,768]{1,0:T(8,128)(2,1)S(1)}, u32[]{:S(2)}, u32[]{:S(2)}) %collective-permute-start.1) | collective-permute-done | bytes 786464 | tf_op jit(solution)/shard_map/chip_one/ppermute | solution.py:55
  37.2 2.5 %collective-permute-done.2.refs_1_.refs_0_ = bf16[512,768]{1,0:T(8,128)(2,1)} collective-permute-done((bf16[512,768]{1,0:T(8,128)(2,1)}, bf16[512,768]{1,0:T(8,128)(2,1)}, u32[]{:S(2)}, u32[]{:S(2)}) %collective-permute-start.2) | collective-permute-done | bytes 786464 | tf_op jit(solution)/shard_map/core_norm/ppermute | solution.py:55
  39.7 9.0 %expand.1 = (bf16[512,768]{1,0:T(8,128)(2,1)S(1)}, bf16[512,768]{1,0:T(8,128)(2,1)S(1)}, bf16[1024,768]{1,0:T(8,128)(2,1)S(1)}, bf16[1024,768]{1,0:T(8,128)(2,1)S(1)}, f32[1,768]{1,0:T(1,128)S(1)}) custom-call(s32[8]{0:T(128)S(1)} %stack.31.refs_0_.ids.ids_ref, bf16[512,768]{1,0:T(8,128)(2,1)} %collective-permute-done.2.refs_1_.refs_0_, ...), custom_call_target="tpu_custom_call" | custom-call | bytes 1 | tf_op jit(solution)/shard_map/expand/pallas_call | solution.py:335
  48.9 2.5 %down_grad.1 = (bf16[4,96,768]{2,1,0:T(8,128)(2,1)S(1)}, bf16[4,96,768]{2,1,0:T(8,128)(2,1)S(1)}) custom-call(s32[8]{0:T(128)S(1)} %stack.31.refs_0_.ids.ids_ref, bf16[1024,768]{1,0:T(8,128)(2,1)S(1)} %get-tuple-element.75.refs_0_.refs_1_, bf16[1024,768]{1,0:T(8,128)(2,1)S(1)} %get-tuple-element.75.refs_0_.refs_1_, bf16[1024,768]{1,0:T(8,128)(2,1)S(1)} %copy-done, ...), custom_call_target="tpu_custom_call" | custom-call | bytes 1 | tf_op jit(solution)/shard_map/down_grad/pallas_call | solution.py:449
  54.9 3.4 %up_grad.1 = (bf16[4,96,768]{2,1,0:T(8,128)(2,1)S(1)}, bf16[4,96,768]{2,1,0:T(8,128)(2,1)S(1)}) custom-call(s32[8]{0:T(128)S(1)} %stack.31.refs_0_.ids.ids_ref, bf16[512,768]{1,0:T(8,128)(2,1)} %collective-permute-done.2.refs_1_.refs_0_, bf16[512,768]{1,0:T(8,128)(2,1)} %get-tuple-element.74.refs_2_.refs_1_, ...), custom_call_target="tpu_custom_call" | custom-call | bytes 1 | tf_op jit(solution)/shard_map/up_grad/pallas_call | solution.py:449
  60.0 2.1 %contract_rows.1 = (bf16[512,768]{1,0:T(8,128)(2,1)S(1)}, bf16[512,768]{1,0:T(8,128)(2,1)S(1)}) custom-call(bf16[1024,768]{1,0:T(8,128)(2,1)S(1)} %get-tuple-element.75.refs_0_.refs_1_, bf16[768,768]{1,0:T(8,128)(2,1)S(1)} %copy-done.3, bf16[4,96,768]{2,1,0:T(8,128)(2,1)S(1)} %get-tuple-element.80.refs_2_), custom_call_target="tpu_custom_call" | custom-call | bytes 1 | tf_op jit(solution)/shard_map/contract_rows/pallas_call | solution.py:382
  62.1 6.6 %collective-permute-done.9.refs_1_ = bf16[4,96,768]{2,1,0:T(8,128)(2,1)S(1)} collective-permute-done((bf16[4,96,768]{2,1,0:T(8,128)(2,1)S(1)}, bf16[4,96,768]{2,1,0:T(8,128)(2,1)S(1)}, u32[]{:S(2)}, u32[]{:S(2)}) %collective-permute-start.9) | collective-permute-done | bytes 589856 | tf_op jit(solution)/shard_map/mlp_start_0/ppermute | solution.py:55
  68.7 4.7 %collective-permute-done.10.refs_3_ = bf16[4,96,768]{2,1,0:T(8,128)(2,1)S(1)} collective-permute-done((bf16[4,96,768]{2,1,0:T(8,128)(2,1)S(1)}, bf16[4,96,768]{2,1,0:T(8,128)(2,1)S(1)}, u32[]{:S(2)}, u32[]{:S(2)}) %collective-permute-start.10) | collective-permute-done | bytes 589856 | tf_op jit(solution)/shard_map/mlp_start_1/ppermute | solution.py:55
  73.8 2.1 %mid_back.1 = (f32[512,768]{1,0:T(8,128)S(1)}, bf16[512,768]{1,0:T(8,128)(2,1)S(1)}, f32[8,768]{1,0:T(8,128)S(1)}) custom-call(s32[8]{0:T(128)S(1)} %stack.31.refs_0_.ids.ids_ref, bf16[512,768]{1,0:T(8,128)(2,1)S(1)} %pair_two.1.refs_4_.refs_0_, bf16[512,768]{1,0:T(8,128)(2,1)S(1)} %collective-permute-done.8.refs_1_, ...), custom_call_target="tpu_custom_call" | custom-call | bytes 1 | tf_op jit(solution)/shard_map/mid_back/pallas_call | solution.py:666
  79.7 7.0 %attend_back.1 = (bf16[512,768]{1,0:T(8,128)(2,1)S(1)}, bf16[512,768]{1,0:T(8,128)(2,1)S(1)}, bf16[1024,192]{1,0:T(8,128)(2,1)S(1)}, bf16[1024,192]{1,0:T(8,128)(2,1)S(1)}, bf16[1024,192]{1,0:T(8,128)(2,1)S(1)}) custom-call(bf16[512,768]{1,0:T(8,128)(2,1)S(1)} %pad_maximum_fusion.1.refs_0_, bf16[512,768]{1,0:T(8,128)(2,1)S(1)} %get-tuple-element.86.refs_1_, ...), custom_call_target="tpu_custom_call" | custom-call | bytes 1 | tf_op jit(solution)/shard_map/attend_back/pallas_call | solution.py:733
  96.2 2.6 %collective-permute-start.31 = (bf16[2,2,96,768]{3,2,1,0:T(8,128)(2,1)S(1)}, bf16[2,2,96,768]{3,2,1,0:T(8,128)(2,1)S(1)}, u32[]{:S(2)}, u32[]{:S(2)}) collective-permute-start(bf16[2,2,96,768]{3,2,1,0:T(8,128)(2,1)S(1)} %mlp_1.1.refs_4_.refs_0_), channel_id=1, source_target_pairs={{0,16},{4,20},{8,24},{12,28},{16,0},{20,4},{24,8},{28,12},{1,17},{... | collective-permute-start | bytes 1769480 | tf_op jit(solution)/shard_map/mlp_1_far/ppermute | solution.py:55
  98.8 4.2 %collective-permute-done.17.refs_1_ = bf16[4,2,24,768]{3,2,1,0:T(8,128)(2,1)S(1)} collective-permute-done((bf16[4,2,24,768]{3,2,1,0:T(8,128)(2,1)S(1)}, bf16[4,2,24,768]{3,2,1,0:T(8,128)(2,1)S(1)}, u32[]{:S(2)}, u32[]{:S(2)}) %collective-permute-start.17) | collective-permute-done | bytes 294944 | tf_op jit(solution)/shard_map/heads_start_0/ppermute | solution.py:55
  103.1 8.5 %collective-permute-done.22.refs_3_ = bf16[4,2,24,768]{3,2,1,0:T(8,128)(2,1)S(1)} collective-permute-done((bf16[4,2,24,768]{3,2,1,0:T(8,128)(2,1)S(1)}, bf16[4,2,24,768]{3,2,1,0:T(8,128)(2,1)S(1)}, u32[]{:S(2)}, u32[]{:S(2)}) %collective-permute-start.22) | collective-permute-done | bytes 294944 | tf_op jit(solution)/shard_map/heads_start_1/ppermute | solution.py:55
  115.7 2.4 %collective-permute-done.23.refs_1_ = bf16[2,2,24,768]{3,2,1,0:T(8,128)(2,1)S(1)} collective-permute-done((bf16[2,2,24,768]{3,2,1,0:T(8,128)(2,1)S(1)}, bf16[2,2,24,768]{3,2,1,0:T(8,128)(2,1)S(1)}, u32[]{:S(2)}, u32[]{:S(2)}) %collective-permute-start.23) | collective-permute-done | bytes 147488 | tf_op jit(solution)/shard_map/heads_0_a/ppermute | solution.py:55
  118.8 5.5 %collective-permute-done.31.refs_1_ = bf16[2,2,96,768]{3,2,1,0:T(8,128)(2,1)S(1)} collective-permute-done((bf16[2,2,96,768]{3,2,1,0:T(8,128)(2,1)S(1)}, bf16[2,2,96,768]{3,2,1,0:T(8,128)(2,1)S(1)}, u32[]{:S(2)}, u32[]{:S(2)}) %collective-permute-start.31) | collective-permute-done | bytes 589856 | tf_op jit(solution)/shard_map/mlp_1_far/ppermute | solution.py:55
  125.4 3.3 %collective-permute-done.32.refs_1_ = f32[16,768]{1,0:T(8,128)S(1)} collective-permute-done((f32[16,768]{1,0:T(8,128)S(1)}, f32[16,768]{1,0:T(8,128)S(1)}, u32[]{:S(2)}, u32[]{:S(2)}) %collective-permute-start.32) | collective-permute-done | bytes 49184 | tf_op jit(solution)/shard_map/sums_1/ppermute | solution.py:55
  130.7 2.4 %collective-permute-start.29 = (bf16[2,2,2,24,768]{4,3,2,1,0:T(8,128)(2,1)S(1)}, bf16[2,2,2,24,768]{4,3,2,1,0:T(8,128)(2,1)S(1)}, u32[]{:S(2)}, u32[]{:S(2)}) collective-permute-start(bf16[2,2,2,24,768]{4,3,2,1,0:T(8,128)(2,1)S(1)} %heads_1.1.refs_2_.refs_0_), channel_id=1, source_target_pairs={{0,16},{4,20},{8,24},{12,28},{16,0},{20,4},{24,8},{28,12},{1,17},{... | collective-permute-start | bytes 884744 | tf_op jit(solution)/shard_map/heads_1_far/ppermute | solution.py:55
  137.3 8.8 %collective-permute-done.29.refs_1_ = bf16[2,2,2,24,768]{4,3,2,1,0:T(8,128)(2,1)S(1)} collective-permute-done((bf16[2,2,2,24,768]{4,3,2,1,0:T(8,128)(2,1)S(1)}, bf16[2,2,2,24,768]{4,3,2,1,0:T(8,128)(2,1)S(1)}, u32[]{:S(2)}, u32[]{:S(2)}) %collective-permute-start.29) | collective-permute-done | bytes 294944 | tf_op jit(solution)/shard_map/heads_1_far/ppermute | solution.py:55
  147.2 3.8 %collective-permute-start.37 = (bf16[2,2,24,768]{3,2,1,0:T(8,128)(2,1)S(1)}, bf16[2,2,24,768]{3,2,1,0:T(8,128)(2,1)S(1)}, u32[]{:S(2)}, u32[]{:S(2)}) collective-permute-start(bf16[2,2,24,768]{3,2,1,0:T(8,128)(2,1)S(1)} %get-tuple-element.116.refs_4_.refs_0_), channel_id=1, source_target_pairs={{0,8},{4,12},{8,0},{12,4},{16,24},{20,28},{24,16},{28,20},{1,9},{5... | collective-permute-start | bytes 442376 | tf_op jit(solution)/shard_map/heads_2_a/ppermute | solution.py:55
  161.0 4.0 %table_grad.1 = (f32[8,768]{1,0:T(8,128)S(1)}, f32[192,1000]{1,0:T(8,128)}) custom-call(s32[152]{0:T(256)S(1)} %concatenate.29.refs_0_, f32[40,768]{1,0:T(8,128)S(1)} %join_sums_2.1.refs_4_.refs_1_, f32[40,768]{1,0:T(8,128)S(1)} %collective-permute-done.50.refs_2_, bf16[512,768]{1,0:T(8,128)(2,1)S(1)} %finish.1.refs_3_.refs_0_), custom_call_target="tpu_custom_call" | custom-call | bytes 1 | tf_op jit(solution)/shard_map/table_grad/pallas_call | solution.py:868
  165.7 5.0 %collective-permute-done.49.value_ref = bf16[4,96,768]{2,1,0:T(8,128)(2,1)S(1)} collective-permute-done((bf16[4,96,768]{2,1,0:T(8,128)(2,1)S(1)}, bf16[4,96,768]{2,1,0:T(8,128)(2,1)S(1)}, u32[]{:S(2)}, u32[]{:S(2)}) %collective-permute-start.49) | collective-permute-done | bytes 589856 | tf_op jit(solution)/shard_map/mlp_3_a/ppermute | solution.py:55
  175.1 2.1 %place_heads.1 = (f32[3,192,768]{2,1,0:T(8,128)}, f32[192,768]{1,0:T(8,128)}) custom-call(s32[8]{0:T(128)S(1)} %stack.31.refs_0_.ids.ids_ref, bf16[4,2,24,768]{3,2,1,0:T(8,128)(2,1)S(1)} %get-tuple-element.121.refs_4_.near_a, bf16[4,2,24,768]{3,2,1,0:T(8,128)(2,1)S(1)} %collective-permute-done.46.far_a, ...), custom_call_target="tpu_custom_call" | custom-call | bytes 1 | tf_op jit(solution)/shard_map/place_heads/pallas_call | solution.py:623
  (178 shorter events, 54.5 us)
Async XLA Ops:
  14.7 20.8 %collective-permute-start.1 = (bf16[512,768]{1,0:T(8,128)(2,1)S(1)}, bf16[512,768]{1,0:T(8,128)(2,1)S(1)}, u32[]{:S(2)}, u32[]{:S(2)}) collective-permute-start(bf16[512,768]{1,0:T(8,128)(2,1)S(1)} %pair_one.1.refs_1_), channel_id=1, source_target_pairs={{0,2},{1,3},{2,0},{3,1},{4,6},{5,7},{6,4},{7,5},{8,10},{9,11},{10,... | collective-permute-start | bytes 2359304 | tf_op jit(solution)/shard_map/chip_one/ppermute | solution.py:55
  51.6 22.1 %collective-permute-start.8 = (bf16[512,768]{1,0:T(8,128)(2,1)S(1)}, bf16[512,768]{1,0:T(8,128)(2,1)S(1)}, u32[]{:S(2)}, u32[]{:S(2)}) collective-permute-start(bf16[512,768]{1,0:T(8,128)(2,1)S(1)} %pair_two.1.refs_4_.refs_0_), channel_id=1, source_target_pairs={{0,2},{1,3},{2,0},{3,1},{4,6},{5,7},{6,4},{7,5},{8,10},{9,11},{10,... | collective-permute-start | bytes 2359304 | tf_op jit(solution)/shard_map/chip_two/ppermute | solution.py:55
  53.4 15.3 %collective-permute-start.9 = (bf16[4,96,768]{2,1,0:T(8,128)(2,1)S(1)}, bf16[4,96,768]{2,1,0:T(8,128)(2,1)S(1)}, u32[]{:S(2)}, u32[]{:S(2)}) collective-permute-start(bf16[4,96,768]{2,1,0:T(8,128)(2,1)S(1)} %get-tuple-element.83), channel_id=1, source_target_pairs={{0,4},{4,0},{8,12},{12,8},{16,20},{20,16},{24,28},{28,24},{1,5},{5... | collective-permute-start | bytes 1769480 | tf_op jit(solution)/shard_map/mlp_start_0/ppermute | solution.py:55
  58.4 15.1 %collective-permute-start.10 = (bf16[4,96,768]{2,1,0:T(8,128)(2,1)S(1)}, bf16[4,96,768]{2,1,0:T(8,128)(2,1)S(1)}, u32[]{:S(2)}, u32[]{:S(2)}) collective-permute-start(bf16[4,96,768]{2,1,0:T(8,128)(2,1)S(1)} %get-tuple-element.84), channel_id=1, source_target_pairs={{0,8},{4,12},{8,0},{12,4},{16,24},{20,28},{24,16},{28,20},{1,9},{5... | collective-permute-start | bytes 1769480 | tf_op jit(solution)/shard_map/mlp_start_1/ppermute | solution.py:55
  77.1 14.4 %collective-permute-start.4 = (bf16[128,768]{1,0:T(8,128)(2,1)S(1)}, bf16[128,768]{1,0:T(8,128)(2,1)S(1)}, u32[]{:S(2)}, u32[]{:S(2)}) collective-permute-start(bf16[128,768]{1,0:T(8,128)(2,1)S(1)} %get-tuple-element.153), channel_id=1, source_target_pairs={{0,1},{1,0},{2,3},{3,2},{4,5},{5,4},{6,7},{7,6},{8,9},{9,8},{10,11... | collective-permute-start | bytes 589832 | tf_op jit(solution)/shard_map/core_out/ppermute | solution.py:55
  77.5 9.9 %collective-permute-start.15 = (bf16[2,96,768]{2,1,0:T(8,128)(2,1)S(1)}, bf16[2,96,768]{2,1,0:T(8,128)(2,1)S(1)}, u32[]{:S(2)}, u32[]{:S(2)}) collective-permute-start(bf16[2,96,768]{2,1,0:T(8,128)(2,1)S(1)} %get-tuple-element.94), channel_id=1, source_target_pairs={{0,8},{4,12},{8,0},{12,4},{16,24},{20,28},{24,16},{28,20},{1,9},{5... | collective-permute-start | bytes 884744 | tf_op jit(solution)/shard_map/mlp_0_a/ppermute | solution.py:55
  91.0 21.2 %collective-permute-start.25 = (bf16[256,768]{1,0:T(8,128)(2,1)S(1)}, bf16[256,768]{1,0:T(8,128)(2,1)S(1)}, u32[]{:S(2)}, u32[]{:S(2)}) collective-permute-start(bf16[256,768]{1,0:T(8,128)(2,1)S(1)} %get-tuple-element.143), channel_id=1, source_target_pairs={{0,2},{1,3},{2,0},{3,1},{4,6},{5,7},{6,4},{7,5},{8,10},{9,11},{10,... | collective-permute-start | bytes 1179656 | tf_op jit(solution)/shard_map/chip_three/ppermute | solution.py:55
  91.6 20.6 %collective-permute-start.26 = (bf16[256,768]{1,0:T(8,128)(2,1)S(1)}, bf16[256,768]{1,0:T(8,128)(2,1)S(1)}, u32[]{:S(2)}, u32[]{:S(2)}) collective-permute-start(bf16[256,768]{1,0:T(8,128)(2,1)S(1)} %get-tuple-element.144), channel_id=1, source_target_pairs={{0,2},{1,3},{2,0},{3,1},{4,6},{5,7},{6,4},{7,5},{8,10},{9,11},{10,... | collective-permute-start | bytes 1179656 | tf_op jit(solution)/shard_map/chip_three/ppermute | solution.py:55
  95.7 15.8 %collective-permute-start.22 = (bf16[4,2,24,768]{3,2,1,0:T(8,128)(2,1)S(1)}, bf16[4,2,24,768]{3,2,1,0:T(8,128)(2,1)S(1)}, u32[]{:S(2)}, u32[]{:S(2)}) collective-permute-start(bf16[4,2,24,768]{3,2,1,0:T(8,128)(2,1)S(1)} %get-tuple-element.104), channel_id=1, source_target_pairs={{0,8},{4,12},{8,0},{12,4},{16,24},{20,28},{24,16},{28,20},{1,9},{5... | collective-permute-start | bytes 884744 | tf_op jit(solution)/shard_map/heads_start_1/ppermute | solution.py:55
  96.2 28.1 %collective-permute-start.31 = (bf16[2,2,96,768]{3,2,1,0:T(8,128)(2,1)S(1)}, bf16[2,2,96,768]{3,2,1,0:T(8,128)(2,1)S(1)}, u32[]{:S(2)}, u32[]{:S(2)}) collective-permute-start(bf16[2,2,96,768]{3,2,1,0:T(8,128)(2,1)S(1)} %mlp_1.1.refs_4_.refs_0_), channel_id=1, source_target_pairs={{0,16},{4,20},{8,24},{12,28},{16,0},{20,4},{24,8},{28,12},{1,17},{... | collective-permute-start | bytes 1769480 | tf_op jit(solution)/shard_map/mlp_1_far/ppermute | solution.py:55
  113.8 10.6 %collective-permute-start.30 = (f32[12,768]{1,0:T(8,128)S(1)}, f32[12,768]{1,0:T(8,128)S(1)}, u32[]{:S(2)}, u32[]{:S(2)}) collective-permute-start(f32[12,768]{1,0:T(8,128)S(1)} %pack_sums.1.refs_4_.refs_0_), channel_id=1, source_target_pairs={{0,4},{4,0},{8,12},{12,8},{16,20},{20,16},{24,28},{28,24},{1,5},{5... | collective-permute-start | bytes 110600 | tf_op jit(solution)/shard_map/sums_0/ppermute | solution.py:55
  115.6 13.6 %collective-permute-start.33 = (bf16[128,768]{1,0:T(8,128)(2,1)S(1)}, bf16[128,768]{1,0:T(8,128)(2,1)S(1)}, u32[]{:S(2)}, u32[]{:S(2)}) collective-permute-start(bf16[128,768]{1,0:T(8,128)(2,1)S(1)} %get-tuple-element.137), channel_id=1, source_target_pairs={{0,1},{1,0},{2,3},{3,2},{4,5},{5,4},{6,7},{7,6},{8,9},{9,8},{10,11... | collective-permute-start | bytes 589832 | tf_op jit(solution)/shard_map/core_input/ppermute | solution.py:55
  118.0 12.7 %collective-permute-start.36 = (bf16[128,768]{1,0:T(8,128)(2,1)S(1)}, bf16[128,768]{1,0:T(8,128)(2,1)S(1)}, u32[]{:S(2)}, u32[]{:S(2)}) collective-permute-start(bf16[128,768]{1,0:T(8,128)(2,1)S(1)} %get-tuple-element.138), channel_id=1, source_target_pairs={{0,1},{1,0},{2,3},{3,2},{4,5},{5,4},{6,7},{7,6},{8,9},{9,8},{10,11... | collective-permute-start | bytes 589832 | tf_op jit(solution)/shard_map/core_input/ppermute | solution.py:55
  118.0 15.1 %collective-permute-start.35 = (bf16[128,768]{1,0:T(8,128)(2,1)S(1)}, bf16[128,768]{1,0:T(8,128)(2,1)S(1)}, u32[]{:S(2)}, u32[]{:S(2)}) collective-permute-start(bf16[128,768]{1,0:T(8,128)(2,1)S(1)} %get-tuple-element.139), channel_id=1, source_target_pairs={{0,1},{1,0},{2,3},{3,2},{4,5},{5,4},{6,7},{7,6},{8,9},{9,8},{10,11... | collective-permute-start | bytes 589832 | tf_op jit(solution)/shard_map/core_input/ppermute | solution.py:55
  128.7 25.7 %collective-permute-start.27 = (bf16[256,768]{1,0:T(8,128)(2,1)S(1)}, bf16[256,768]{1,0:T(8,128)(2,1)S(1)}, u32[]{:S(2)}, u32[]{:S(2)}) collective-permute-start(bf16[256,768]{1,0:T(8,128)(2,1)S(1)} %get-tuple-element.141), channel_id=1, source_target_pairs={{0,2},{1,3},{2,0},{3,1},{4,6},{5,7},{6,4},{7,5},{8,10},{9,11},{10,... | collective-permute-start | bytes 1179656 | tf_op jit(solution)/shard_map/chip_out/ppermute | solution.py:55
  129.2 26.6 %collective-permute-start.28 = (bf16[256,768]{1,0:T(8,128)(2,1)S(1)}, bf16[256,768]{1,0:T(8,128)(2,1)S(1)}, u32[]{:S(2)}, u32[]{:S(2)}) collective-permute-start(bf16[256,768]{1,0:T(8,128)(2,1)S(1)} %get-tuple-element.142), channel_id=1, source_target_pairs={{0,2},{1,3},{2,0},{3,1},{4,6},{5,7},{6,4},{7,5},{8,10},{9,11},{10,... | collective-permute-start | bytes 1179656 | tf_op jit(solution)/shard_map/chip_out/ppermute | solution.py:55
  130.7 15.4 %collective-permute-start.29 = (bf16[2,2,2,24,768]{4,3,2,1,0:T(8,128)(2,1)S(1)}, bf16[2,2,2,24,768]{4,3,2,1,0:T(8,128)(2,1)S(1)}, u32[]{:S(2)}, u32[]{:S(2)}) collective-permute-start(bf16[2,2,2,24,768]{4,3,2,1,0:T(8,128)(2,1)S(1)} %heads_1.1.refs_2_.refs_0_), channel_id=1, source_target_pairs={{0,16},{4,20},{8,24},{12,28},{16,0},{20,4},{24,8},{28,12},{1,17},{... | collective-permute-start | bytes 884744 | tf_op jit(solution)/shard_map/heads_1_far/ppermute | solution.py:55
  133.1 13.1 %collective-permute-start.41 = (bf16[2,96,768]{2,1,0:T(8,128)(2,1)S(1)}, bf16[2,96,768]{2,1,0:T(8,128)(2,1)S(1)}, u32[]{:S(2)}, u32[]{:S(2)}) collective-permute-start(bf16[2,96,768]{2,1,0:T(8,128)(2,1)S(1)} %get-tuple-element.118.refs_2_), channel_id=1, source_target_pairs={{0,4},{4,0},{8,12},{12,8},{16,20},{20,16},{24,28},{28,24},{1,5},{5... | collective-permute-start | bytes 884744 | tf_op jit(solution)/shard_map/mlp_2_b/ppermute | solution.py:55
  133.8 13.4 %collective-permute-start.40 = (bf16[2,96,768]{2,1,0:T(8,128)(2,1)S(1)}, bf16[2,96,768]{2,1,0:T(8,128)(2,1)S(1)}, u32[]{:S(2)}, u32[]{:S(2)}) collective-permute-start(bf16[2,96,768]{2,1,0:T(8,128)(2,1)S(1)} %get-tuple-element.115.refs_2_.refs_0_), channel_id=1, source_target_pairs={{0,8},{4,12},{8,0},{12,4},{16,24},{20,28},{24,16},{28,20},{1,9},{5... | collective-permute-start | bytes 884744 | tf_op jit(solution)/shard_map/mlp_2_a/ppermute | solution.py:55
  146.2 9.6 %collective-permute-start.38 = (bf16[2,2,24,768]{3,2,1,0:T(8,128)(2,1)S(1)}, bf16[2,2,24,768]{3,2,1,0:T(8,128)(2,1)S(1)}, u32[]{:S(2)}, u32[]{:S(2)}) collective-permute-start(bf16[2,2,24,768]{3,2,1,0:T(8,128)(2,1)S(1)} %get-tuple-element.117.refs_2_), channel_id=1, source_target_pairs={{0,4},{4,0},{8,12},{12,8},{16,20},{20,16},{24,28},{28,24},{1,5},{5... | collective-permute-start | bytes 442376 | tf_op jit(solution)/shard_map/heads_2_b/ppermute | solution.py:55
  154.3 18.0 %collective-permute-start.48 = (bf16[4,96,768]{2,1,0:T(8,128)(2,1)S(1)}, bf16[4,96,768]{2,1,0:T(8,128)(2,1)S(1)}, u32[]{:S(2)}, u32[]{:S(2)}) collective-permute-start(bf16[4,96,768]{2,1,0:T(8,128)(2,1)S(1)} %get-tuple-element.119.value_ref), channel_id=1, source_target_pairs={{0,8},{4,12},{8,0},{12,4},{16,24},{20,28},{24,16},{28,20},{1,9},{5... | collective-permute-start | bytes 1769480 | tf_op jit(solution)/shard_map/mlp_3_b/ppermute | solution.py:55
  154.4 16.3 %collective-permute-start.49 = (bf16[4,96,768]{2,1,0:T(8,128)(2,1)S(1)}, bf16[4,96,768]{2,1,0:T(8,128)(2,1)S(1)}, u32[]{:S(2)}, u32[]{:S(2)}) collective-permute-start(bf16[4,96,768]{2,1,0:T(8,128)(2,1)S(1)} %get-tuple-element.120.value_ref.refs_0_), channel_id=1, source_target_pairs={{0,4},{4,0},{8,12},{12,8},{16,20},{20,16},{24,28},{28,24},{1,5},{5... | collective-permute-start | bytes 1769480 | tf_op jit(solution)/shard_map/mlp_3_a/ppermute | solution.py:55
  158.3 16.7 %collective-permute-start.47 = (bf16[4,2,24,768]{3,2,1,0:T(8,128)(2,1)S(1)}, bf16[4,2,24,768]{3,2,1,0:T(8,128)(2,1)S(1)}, u32[]{:S(2)}, u32[]{:S(2)}) collective-permute-start(bf16[4,2,24,768]{3,2,1,0:T(8,128)(2,1)S(1)} %get-tuple-element.122.near_b), channel_id=1, source_target_pairs={{0,8},{4,12},{8,0},{12,4},{16,24},{20,28},{24,16},{28,20},{1,9},{5... | collective-permute-start | bytes 884744 | tf_op jit(solution)/shard_map/heads_3_b/ppermute | solution.py:55
  160.3 14.8 %collective-permute-start.46 = (bf16[4,2,24,768]{3,2,1,0:T(8,128)(2,1)S(1)}, bf16[4,2,24,768]{3,2,1,0:T(8,128)(2,1)S(1)}, u32[]{:S(2)}, u32[]{:S(2)}) collective-permute-start(bf16[4,2,24,768]{3,2,1,0:T(8,128)(2,1)S(1)} %get-tuple-element.121.refs_4_.near_a), channel_id=1, source_target_pairs={{0,4},{4,0},{8,12},{12,8},{16,20},{20,16},{24,28},{28,24},{1,5},{5... | collective-permute-start | bytes 884744 | tf_op jit(solution)/shard_map/heads_3_a/ppermute | solution.py:55
  (48 other events, 365.7 us)

commit v3 on v2

--- a/solution.py
+++ b/solution.py
@@ -1,4 +1,5 @@
 import functools
+import types
 
 import jax
 import jax.numpy as jnp
@@ -15,6 +16,9 @@
 SQRT_HALF = 0.7071067811865476
 PHI_ZERO = 0.3989422804014327
 VMEM_MB = 16
+LOW_PIECES = 2
+PART_PIECES = 4
+
 SMALL_MB = 8
 
 F32 = jnp.float32
@@ -33,11 +37,11 @@
     )
 
 
-COST_SCALE = 0.0
-
-
-def cost(micros):
-    return pl.CostEstimate(flops=int(micros * COST_SCALE * 1e9), bytes_accessed=int(micros * COST_SCALE * 3e6) + 1, transcendentals=0)
+COSTS = {"expand": 1, "finish": 0.5, "order_input": 0.5}
+
+
+def cost(name):
+    return pl.CostEstimate(flops=int(COSTS.get(name, 0) * 1e9), bytes_accessed=1, transcendentals=0)
 
 
 def shape(dims, dtype):
@@ -49,30 +53,20 @@
     return pl.BlockSpec(array.shape, lambda *_: zeros)
 
 
-def swap(value, axis, bit, name):
-    pairs = [(i, i ^ bit) for i in range(lax.axis_size(axis))]
-    with jax.named_scope(name):
-        return lax.ppermute(value, axis, pairs)
-
-
-def core_swap(value, name="core", pieces=1):
-    return swap_pieces(value, 1, name, pieces)
-
-
-def swap_pieces(value, bit, name, pieces):
-    if pieces == 1:
-        return swap(value, "tensor", bit, name)
-    rows = value.shape[0] // pieces
-    parts = [swap(value[i * rows : (i + 1) * rows], "tensor", bit, name) for i in range(pieces)]
-    return jnp.concatenate(parts, axis=0)
-
-
-def chip_swap(value, name="chip", pieces=1):
-    return swap_pieces(value, 2, name, pieces)
-
-
-def dp_swap(value, bit, name="dp"):
-    return swap(value, "dp", bit, name)
+def swap(value, axis, bit):
+    return lax.ppermute(value, axis, [(i, i ^ bit) for i in range(lax.axis_size(axis))])
+
+
+def core_swap(value):
+    return swap(value, "tensor", 1)
+
+
+def chip_swap(value):
+    return swap(value, "tensor", 2)
+
+
+def dp_swap(value, bit):
+    return swap(value, "dp", bit)
 
 
 def norm_stats(values):
@@ -137,9 +131,32 @@
         out_specs=[VM] * len(out_shape),
         out_shape=out_shape,
         compiler_params=pltpu.CompilerParams(vmem_limit_bytes=SMALL_MB << 20),
-        cost_estimate=cost(0.2),
+        cost_estimate=cost(name),
         name=name,
     )(*operands, *after)
+
+
+def stage(arrays, after):
+    count = len(arrays)
+
+    def kernel(*refs):
+        out, sems = refs[count + len(after) : -1], refs[-1]
+        copies = [pltpu.make_async_copy(refs[n], out[n], sems.at[n]) for n in range(count)]
+        for copy in copies:
+            copy.start()
+        for copy in copies:
+            copy.wait()
+
+    return pl.pallas_call(
+        kernel,
+        in_specs=[pl.BlockSpec(memory_space=pltpu.HBM)] * count + [ANY] * len(after),
+        out_specs=[VM] * count,
+        out_shape=[pltpu.VMEM(a.shape, a.dtype) for a in arrays],
+        scratch_shapes=[pltpu.SemaphoreType.DMA((count,))],
+        compiler_params=pltpu.CompilerParams(vmem_limit_bytes=SMALL_MB << 20),
+        cost_estimate=cost("stage"),
+        name="stage",
+    )(*arrays, *after)
 
 
 def add_two(a, b, after, name):
@@ -268,7 +285,7 @@
             shape((rows, local), BF16),
         ],
         compiler_params=params(),
-        cost_estimate=cost(4.5),
+        cost_estimate=cost("attend"),
         name="attend",
     )(scalars, tokens, table, gain, bias, w_qkv, wo, *after)
 
@@ -290,20 +307,38 @@
         out_specs=[row, row],
         out_shape=[shape((rows, width), F32), shape((rows, width), BF16)],
         compiler_params=params(),
-        cost_estimate=cost(0.4),
+        cost_estimate=cost("mid_forward"),
         name="mid_forward",
     )(hidden, pair, other, gain, bias, *after)
 
 
-def expand_kernel(half, ids, peer, own, cot, w_up, up_bias, w_down, send, keep, act_out, low_out, bias_out):
+def act_grad(cot, w_down):
+    rows, width = cot.shape
+    local = w_down.shape[0]
+
+    def kernel(cot_ref, w_ref, out):
+        out[...] = mm(cot_ref[...], w_ref[...], 1, 1)
+
+    return pl.pallas_call(
+        kernel,
+        grid=(rows // PAIR,),
+        in_specs=[pl.BlockSpec((PAIR, width), lambda i: (i, 0)), VM],
+        out_specs=pl.BlockSpec((PAIR, local), lambda i: (i, 0)),
+        out_shape=shape((rows, local), F32),
+        compiler_params=params(),
+        cost_estimate=cost("act_grad"),
+        name="act_grad",
+    )(cot, w_down)
+
+
+def expand_kernel(half, ids, peer, own, grad_act, w_up, up_bias, send, keep, act_out, low_out, bias_out):
     i = pl.program_id(0)
     normed = jnp.where(i < half, peer[...], own[...])
     pre = mm(normed, w_up[...], 1, 0) + row_vector(up_bias)
-    grad_act = mm(cot[...], w_down[...], 1, 1)
     cdf = 0.5 * (1.0 + lax.erf(pre * SQRT_HALF))
     act_out[...] = (pre * cdf).astype(BF16)
     slope = cdf + pre * (PHI_ZERO * jnp.exp(-0.5 * (pre * pre)))
-    grad_pre = grad_act * slope
+    grad_pre = grad_act[...] * slope
 
     @pl.when(i == 0)
     def _():
@@ -323,8 +358,8 @@
         keep[...] = part
 
 
-def expand(chunk, chunks, ids, peer, own, cot, w_up, up_bias, w_down, after):
-    count, width = cot.shape
+def expand(chunk, chunks, ids, peer, own, grad_act, w_up, up_bias, after):
+    count, width = grad_act.shape[0], peer.shape[1]
     local = w_up.shape[1]
     blocks = count // PAIR // chunks
     half = blocks // 2
@@ -333,15 +368,15 @@
     second = lambda i, *_: (jnp.maximum(i - half, 0), 0)
     step = lambda i, *_: (i, 0)
     return pl.pallas_call(
-        lambda *refs: expand_kernel(half, *refs[:7], *refs[7 + len(after) :]),
+        lambda *refs: expand_kernel(half, *refs[:6], *refs[6 + len(after) :]),
         grid_spec=pltpu.PrefetchScalarGridSpec(
             num_scalar_prefetch=1,
             grid=(blocks,),
             in_specs=[
                 pl.BlockSpec((PAIR, width), first),
                 pl.BlockSpec((PAIR, width), second),
-                pl.BlockSpec((PAIR, width), lambda i, ids: (block_of(i, ids, chunk, half, chunks), 0)),
-                whole(w_up), whole(up_bias), whole(w_down),
+                pl.BlockSpec((PAIR, local), lambda i, ids: (block_of(i, ids, chunk, half, chunks), 0)),
+                VM, whole(up_bias),
             ]
             + [ANY] * len(after),
             out_specs=[
@@ -358,9 +393,9 @@
             shape((1, local), F32),
         ],
         compiler_params=params(),
-        cost_estimate=cost(3.7),
+        cost_estimate=cost("expand"),
         name="expand",
-    )(ids, peer, own, cot, w_up, up_bias, w_down, *after)
+    )(ids, peer, own, grad_act, w_up, up_bias, *after)
 
 
 def contract_kernel(act, w_down, send, keep):
@@ -382,14 +417,14 @@
     return pl.pallas_call(
         lambda *refs: contract_kernel(*refs[:2], *refs[2 + len(after) :]),
         grid=(rows // PAIR,),
-        in_specs=[pl.BlockSpec((PAIR, local), lambda i: (i, 0)), whole(w_down)] + [ANY] * len(after),
+        in_specs=[pl.BlockSpec((PAIR, local), lambda i: (i, 0)), VM] + [ANY] * len(after),
         out_specs=[
             pl.BlockSpec((PAIR, width), lambda i: (jnp.minimum(i, 1), 0)),
             pl.BlockSpec((PAIR, width), lambda i: (jnp.maximum(i - 2, 0), 0)),
         ],
         out_shape=[shape((rows // 2, width), BF16), shape((rows // 2, width), BF16)],
         compiler_params=params(),
-        cost_estimate=cost(2.1),
+        cost_estimate=cost("contract_rows"),
         name="contract_rows",
     )(act, w_down, *after)
 
@@ -457,27 +492,25 @@
         ),
         out_shape=[shape(dims, BF16), shape(dims, BF16)],
         compiler_params=params(),
-        cost_estimate=cost(2.5),
+        cost_estimate=cost(name),
         name=name,
     )(ids, *[a for a, _, _ in lefts], *[b for b, _, _ in rights], *after))
 
 
 def head_grad(ids, order, first, second, after, name):
-    rows_out, cols = first[0][0].shape[1], first[0][1].shape[1]
+    rows_out, cols = first[0].shape[1], first[1][0].shape[1]
     part = rows_out // 8
-    pieces = [len(first), len(second)]
-    flat = [x for pair in (*first, *second) for x in pair]
+    flat = [first[0], *first[1], second[0], *second[1]]
 
     def kernel(ids_ref, *refs):
         values = refs[: len(flat)]
         send, keep, scratch = refs[len(flat) + len(after) :]
         at = 0
-        for n in range(2):
-            total = jnp.zeros((rows_out, cols), F32)
-            for _ in range(pieces[n]):
-                total = total + mm(values[at][...], values[at + 1][...], 0, 0)
-                at += 2
-            scratch[n] = total
+        for n, (_, pieces) in enumerate((first, second)):
+            rights = [values[at + 1 + j][...] for j in range(len(pieces))]
+            right = rights[0] if len(rights) == 1 else jnp.concatenate(rights, axis=0)
+            scratch[n] = mm(values[at][...], right, 0, 0)
+            at += 1 + len(pieces)
         for half, out in ((1 - ids_ref[order], send), (ids_ref[order], keep)):
             for r in range(4):
                 start = pl.multiple_of((half * 4 + (ids_ref[order + 1] ^ r)) * part, 8)
@@ -496,26 +529,41 @@
         ),
         out_shape=[shape(dims, BF16), shape(dims, BF16)],
         compiler_params=params(),
-        cost_estimate=cost(0.2),
+        cost_estimate=cost(name),
         name=name,
     )(ids, *flat, *after)
 
 
+def add_pieces(a, b, pieces, after, name):
+    rows, width = a.shape
+    size, out_size = rows // len(b), rows // pieces
+    step = min(size, out_size)
+
+    def kernel(a_ref, *refs):
+        given, out = refs[: len(b)], refs[len(b) :]
+        for at in range(0, rows, step):
+            got = given[at // size][at % size : at % size + step]
+            out[at // out_size][at % out_size : at % out_size + step] = add_low(a_ref[at : at + step], got)
+
+    return list(small_call(kernel, [shape((out_size, width), BF16)] * pieces, [a, *b], after, name))
+
+
 class Dual:
-    def __init__(self, bits, direct, name):
-        self.bits, self.direct, self.name, self.level = bits, direct, name, 0
+    def __init__(self, bits, direct):
+        self.bits, self.direct, self.level = bits, direct, 0
+        self.summed = [None, None]
         self.halves, self.got = [None, None], [None, None]
 
     def begin(self, which, halves):
         self.halves[which] = list(halves)
         if self.direct:
-            self.got[which] = dp_swap(halves[0], self.bits[which][0], f"{self.name}_start_{which}")
+            self.got[which] = dp_swap(halves[0], self.bits[which][0])
 
     def step(self, after):
         if not self.direct:
             return after
         (_, keep_a), (_, keep_b) = self.halves
-        level, name = self.level, f"{self.name}_{self.level}"
+        level, name = self.level, "exchange"
         self.level += 1
         first, second = self.bits
         if level < 2:
@@ -531,7 +579,7 @@
                 out = [shape((half, *rest), BF16)] * 4
                 sa, oa, sb, ob = small_call(kernel, out, [keep_a, self.got[0], keep_b, self.got[1]], [after], name)
                 self.halves = [[sa, oa], [sb, ob]]
-                self.got = [dp_swap(sa, first[1], name + "_a"), dp_swap(sb, second[1], name + "_b")]
+                self.got = [dp_swap(sa, first[1]), dp_swap(sb, second[1])]
                 return oa
 
             def kernel(ka, ga, kb, gb, out):
@@ -541,7 +589,7 @@
             out = [shape((2, parts, *rest), BF16)]
             both = small_call(kernel, out, [keep_a, self.got[0], keep_b, self.got[1]], [after], name)[0]
             self.halves = [[None, both], [None, both]]
-            self.got = [dp_swap(both, first[2], name + "_far"), None]
+            self.got = [dp_swap(both, first[2]), None]
             return both
         if level == 2:
 
@@ -553,7 +601,7 @@
             out = [shape(keep_a.shape[1:], BF16)] * 2
             oa, ob = small_call(kernel, out, [keep_a, self.got[0]], [after], name)
             self.halves = [[None, oa], [None, ob]]
-            self.got = [dp_swap(oa, first[1], name + "_a"), dp_swap(ob, second[1], name + "_b")]
+            self.got = [dp_swap(oa, first[1]), dp_swap(ob, second[1])]
             return oa
         rest = keep_a.shape[1:]
 
@@ -565,80 +613,96 @@
         out = [shape((4, *rest), BF16)] * 2
         oa, ob = small_call(kernel, out, [keep_a, self.got[0], keep_b, self.got[1]], [after], name)
         self.halves = [[None, oa], [None, ob]]
-        self.got = [dp_swap(oa, first[0], name + "_a"), dp_swap(ob, second[0], name + "_b")]
+        self.got = [dp_swap(oa, first[0]), dp_swap(ob, second[0])]
         return oa
 
     def collect(self, which):
         if not self.direct:
-            send, keep = lax.psum(tuple(self.halves[which]), "dp")
-            return keep, send
+            if self.summed[which] is None:
+                send, keep = lax.psum(tuple(self.halves[which]), "dp")
+                self.summed[which] = keep, send
+            return self.summed[which]
         return self.halves[which][1], self.got[which]
+
+
+HB = pl.BlockSpec(memory_space=pltpu.HBM)
 
 
 def place_half(ids, order, value, flip, base, after, name):
     _, part, cols = value.shape
-    rows = 8 * part
     given = [] if base is None else [pltpu.with_memory_space_constraint(base, pltpu.HBM)]
 
     def kernel(ids_ref, value_ref, *refs):
-        out = refs[-1]
+        out, wide, sems = refs[-3:]
+        copies = []
         for r in range(4):
-            start = pl.multiple_of((ids_ref[order + 1] ^ r) * part, 8)
-            out[pl.ds(start, part), :] = value_ref[r].astype(F32)
+            start = ((ids_ref[order] ^ flip) * 4 + (ids_ref[order + 1] ^ r)) * part
+            wide[r] = value_ref[r].astype(F32)
+            rows = out.at[pl.ds(pl.multiple_of(start, 8), part), :]
+            copies.append(pltpu.make_async_copy(wide.at[r], rows, sems.at[r]))
+            copies[-1].start()
+        for copy in copies:
+            copy.wait()
 
     return pl.pallas_call(
         kernel,
         grid_spec=pltpu.PrefetchScalarGridSpec(
             num_scalar_prefetch=1,
             grid=(1,),
-            in_specs=[VM] + [ANY] * (len(given) + len(after)),
-            out_specs=pl.BlockSpec((4 * part, cols), lambda i, ids: (ids[order] ^ flip, 0)),
+            in_specs=[VM] + [HB] * len(given) + [ANY] * len(after),
+            out_specs=HB,
+            scratch_shapes=[pltpu.VMEM((4, part, cols), F32), pltpu.SemaphoreType.DMA((4,))],
         ),
-        out_shape=pltpu.HBM((rows, cols), F32),
+        out_shape=pltpu.HBM((8 * part, cols), F32),
         input_output_aliases={2: 0} if given else {},
         compiler_params=params(),
-        cost_estimate=cost(1.6),
+        cost_estimate=cost(name),
         name=name,
     )(ids, value, *given, *after)
 
 
-def place_heads(ids, orders, a, b, after):
-    _, _, part, cols = a[0].shape
+def place_heads(ids, orders, a, b, flip, bases, after, name):
+    _, _, part, cols = a.shape
     rows = 8 * part
-
-    def kernel(ids_ref, near_a, far_a, near_b, far_b, *refs):
-        qkv_out, proj_out = refs[len(after) :]
-        for half in range(2):
-            for n, (pick, order) in enumerate((((near_a, far_a), orders[0]), ((near_b, far_b), orders[1]))):
-                for r in range(4):
-                    at = (ids_ref[order] ^ half) * 4 + (ids_ref[order + 1] ^ r)
-                    at = pl.ds(pl.multiple_of(at * part, 8), part)
-                    if n == 0:
-                        qkv_out[0, at, :] = pick[half][r, 0].astype(F32)
-                        qkv_out[1, at, :] = pick[half][r, 1].astype(F32)
-                    else:
-                        qkv_out[2, at, :] = pick[half][r, 0].astype(F32)
-                        proj_out[at, :] = pick[half][r, 1].astype(F32)
-
-    return pl.pallas_call(
-        kernel,
-        grid_spec=pltpu.PrefetchScalarGridSpec(
-            num_scalar_prefetch=1,
-            grid=(1,),
-            in_specs=[VM] * 4 + [ANY] * len(after),
-            out_specs=[
-                pl.BlockSpec((3, rows, cols), lambda *_: (0, 0, 0)),
-                pl.BlockSpec((rows, cols), lambda *_: (0, 0)),
-            ],
-        ),
-        out_shape=[pltpu.HBM((3, rows, cols), F32), pltpu.HBM((rows, cols), F32)],
-        compiler_params=params(),
-        cost_estimate=cost(2.1),
-        name="place_heads",
-    )(ids, *a, *b, *after)
-
-
-def mid_back_kernel(pair, other, residual, cot, gain, grad_out, low_out, sums):
+    given = [pltpu.with_memory_space_constraint(x, pltpu.HBM) for x in bases]
+
+    def kernel(ids_ref, a_ref, b_ref, *refs):
+        qkv_out, proj_out, wide, sems = refs[-4:]
+        copies = []
+        for n, (pick, order) in enumerate(((a_ref, orders[0]), (b_ref, orders[1]))):
+            for r in range(4):
+                at = (ids_ref[order] ^ flip) * 4 + (ids_ref[order + 1] ^ r)
+                at = pl.ds(pl.multiple_of(at * part, 8), part)
+                for j in range(2):
+                    k = len(copies)
+                    wide[k] = pick[r, j].astype(F32)
+                    out = proj_out.at[at, :] if n + j == 2 else qkv_out.at[2 * n + j, at, :]
+                    copies.append(pltpu.make_async_copy(wide.at[k], out, sems.at[k]))
+                    copies[-1].start()
+        for copy in copies:
+            copy.wait()
+
+    return list(
+        pl.pallas_call(
+            kernel,
+            grid_spec=pltpu.PrefetchScalarGridSpec(
+                num_scalar_prefetch=1,
+                grid=(1,),
+                in_specs=[VM, VM] + [HB] * len(given) + [ANY] * len(after),
+                out_specs=[HB, HB],
+                scratch_shapes=[pltpu.VMEM((16, part, cols), F32), pltpu.SemaphoreType.DMA((16,))],
+            ),
+            out_shape=[pltpu.HBM((3, rows, cols), F32), pltpu.HBM((rows, cols), F32)],
+            input_output_aliases={3: 0, 4: 1} if given else {},
+            compiler_params=params(),
+            cost_estimate=cost(name),
+            name=name,
+        )(ids, a, b, *given, *after)
+    )
+
+
+def mid_back_kernel(pair, other, residual, cot, gain, grad_out, *refs):
+    low_out, sums = refs[:-1], refs[-1]
     i = pl.program_id(0)
     err = pair[...].astype(F32) + other[...].astype(F32)
     unit, scale = norm_stats(residual[...])
@@ -648,7 +712,14 @@
     fx_mean = jnp.mean(f * unit, axis=-1, keepdims=True)
     grad = top + scale * (f - f_mean - unit * fx_mean)
     grad_out[...] = grad
-    low_out[...] = grad.astype(BF16)
+    low = grad.astype(BF16)
+    per = PAIR // low_out[0].shape[0]
+    for n, piece in enumerate(low_out):
+
+        @pl.when(i == n // per)
+        def _():
+            rows = piece.shape[0]
+            piece[...] = low[(n % per) * rows : (n % per + 1) * rows]
 
     @pl.when(i == 0)
     def _():
@@ -659,7 +730,7 @@
     sums[2:3] += jnp.sum(top, axis=0, keepdims=True)
 
 
-def mid_back(chunk, chunks, ids, pair, other, residual, cot, gain, after):
+def mid_back(chunk, chunks, ids, pair, other, residual, cot, gain, pieces, after):
     rows, width = residual.shape
     half = rows // PAIR
     row = pl.BlockSpec((PAIR, width), lambda i, ids: (i, 0))
@@ -674,18 +745,29 @@
                 whole(gain),
             ]
             + [ANY] * len(after),
-            out_specs=[row, row, pl.BlockSpec((8, width), lambda i, ids: (0, 0))],
+            out_specs=[row] + [VM] * pieces + [pl.BlockSpec((8, width), lambda i, ids: (0, 0))],
         ),
-        out_shape=[shape((rows, width), F32), shape((rows, width), BF16), shape((8, width), F32)],
+        out_shape=[shape((rows, width), F32)] + [shape((rows // pieces, width), BF16)] * pieces + [shape((8, width), F32)],
         compiler_params=params(),
-        cost_estimate=cost(1.2),
+        cost_estimate=cost("mid_back"),
         name="mid_back",
     )(ids, pair, other, residual, cot, gain, *after)
 
 
-def attend_back_kernel(half, peer, own, q_ref, k_ref, v_ref, p_ref, w_qkv, wo, send, keep, dq_out, dk_out, dv_out):
+def attend_back_kernel(count, blocks, *refs):
+    peers, owns = refs[:count], refs[count : 2 * count]
+    q_ref, k_ref, v_ref, p_ref, w_qkv, wo = refs[2 * count : 2 * count + 6]
+    sends, (keep, dq_out, dk_out, dv_out, low_ref, part_ref) = refs[2 * count + 6 : -6], refs[-6:]
     i = pl.program_id(0)
-    low = jnp.where(i < half, peer[...], own[...])
+    half = blocks // 2
+    rows = peers[0].shape[0]
+
+    @pl.when(i == 0)
+    def _():
+        for n, piece in enumerate((*peers, *owns)):
+            low_ref[n * rows : (n + 1) * rows] = piece[...]
+
+    low = low_ref[pl.ds(pl.multiple_of(i * PAIR, PAIR), PAIR), :]
     grad_context = mm(low, wo[...], 1, 1).astype(BF16)
     q, k, v = q_ref[...], k_ref[...], v_ref[...]
     width = q.shape[1]
@@ -711,48 +793,58 @@
     dk_out[...] = dk
     dv_out[...] = dv
     part = (mm(dq, w_qkv[0], 1, 0) + mm(dk, w_qkv[1], 1, 0) + mm(dv, w_qkv[2], 1, 0)).astype(BF16)
-
-    @pl.when(i < half)
-    def _():
-        send[...] = part
+    part_ref[...] = part
+    per = PAIR // sends[0].shape[0]
+    for n, piece in enumerate(sends):
+
+        @pl.when(i == n // per)
+        def _():
+            size = piece.shape[0]
+            piece[...] = part_ref[(n % per) * size : (n % per + 1) * size]
 
     @pl.when(i >= half)
     def _():
         keep[...] = part
 
 
-def attend_back(peer, own, q, k, v, p, w_qkv, wo, after):
+def attend_back(peers, owns, q, k, v, p, w_qkv, wo, pieces, after):
     rows, local = q.shape
     width = wo.shape[1]
     blocks = rows // PAIR
     half = blocks // 2
     heads = local // HEAD_DIM
-    first = pl.BlockSpec((PAIR, width), lambda i: (jnp.minimum(i, half - 1), 0))
+    count = len(peers)
+    ins = 2 * count + 6
     second = pl.BlockSpec((PAIR, width), lambda i: (jnp.maximum(i - half, 0), 0))
     thin = pl.BlockSpec((PAIR, local), lambda i: (i, 0))
     return pl.pallas_call(
-        lambda *refs: attend_back_kernel(half, *refs[:8], *refs[8 + len(after) :]),
+        lambda *refs: attend_back_kernel(count, blocks, *refs[:ins], *refs[ins + len(after) :]),
         grid=(blocks,),
-        in_specs=[
-            first, second, thin, thin, thin,
+        in_specs=[VM] * (2 * count)
+        + [
+            thin, thin, thin,
             pl.BlockSpec((1, heads, PAIR, PAIR), lambda i: (i, 0, 0, 0)),
             whole(w_qkv), whole(wo),
         ]
         + [ANY] * len(after),
-        out_specs=[first, second, thin, thin, thin],
-        out_shape=[
-            shape((rows // 2, width), BF16), shape((rows // 2, width), BF16),
-            shape((rows, local), BF16), shape((rows, local), BF16), shape((rows, local), BF16),
-        ],
+        out_specs=[VM] * pieces + [second, thin, thin, thin],
+        out_shape=[shape((rows // 2 // pieces, width), BF16)] * pieces
+        + [shape((rows // 2, width), BF16)]
+        + [shape((rows, local), BF16)] * 3,
+        scratch_shapes=[pltpu.VMEM((rows, width), BF16), pltpu.VMEM((PAIR, width), BF16)],
         compiler_params=params(),
-        cost_estimate=cost(3.5),
+        cost_estimate=cost("attend_back"),
         name="attend_back",
-    )(peer, own, q, k, v, p, w_qkv, wo, *after)
-
-
-def last_kernel(pair, other, hidden, grad_residual, gain, low_out, sums, times):
+    )(*peers, *owns, q, k, v, p, w_qkv, wo, *after)
+
+
+def last_kernel(count, *refs):
+    pairs, others = refs[:count], refs[count : 2 * count]
+    hidden, grad_residual, gain, low_out, sums, times = refs[2 * count :]
     i = pl.program_id(0)
-    err = pair[...].astype(F32) + other[...].astype(F32)
+    pair = jnp.where(i == 0, pairs[0][...], pairs[1][...])
+    other = jnp.where(i == 0, others[0][...], others[1][...])
+    err = pair.astype(F32) + other.astype(F32)
     unit, scale = norm_stats(hidden[...])
     f = err * row_vector(gain)
     f_mean = jnp.mean(f, axis=-1, keepdims=True)
@@ -775,9 +867,9 @@
     half = rows // PAIR
     row = pl.BlockSpec((PAIR, width), lambda i: (i, 0))
     return pl.pallas_call(
-        lambda *refs: last_kernel(*refs[:5], *refs[5 + len(after) :]),
+        lambda *refs: last_kernel(2, *refs[:7], *refs[7 + len(after) :]),
         grid=(half,),
-        in_specs=[row, row, row, row, whole(gain)] + [ANY] * len(after),
+        in_specs=[VM] * 4 + [row, row, whole(gain)] + [ANY] * len(after),
         out_specs=[
             row,
             pl.BlockSpec((8, width), lambda i: (0, 0)),
@@ -785,9 +877,9 @@
         ],
         out_shape=[shape((rows, width), BF16), shape((8, width), F32), shape((half, 2, width), F32)],
         compiler_params=params(),
-        cost_estimate=cost(0.7),
+        cost_estimate=cost("last_back"),
         name="last_back",
-    )(pair, other, hidden, grad_residual, gain, *after)
+    )(*pair, *other, hidden, grad_residual, gain, *after)
 
 
 def pack_sums(vec2, vec1, up, times, after):
@@ -816,13 +908,15 @@
     return small_call(kernel, [shape((8 + 2 * more, width), F32)], [a, b], after, name)[0]
 
 
-def table_kernel(slots, steps, ids, own, other, vec_out, out, table, acc, at_ref):
+def table_kernel(slots, steps, ids, own, other, *refs):
+    vec_out, (out, table, acc, at_ref) = refs[:6], refs[6:]
     groups = at_ref.shape[0]
     rows, (row_length, row_group, row_step) = row_fields(ids)
     local = table.shape[2]
     half = slots // 2
-    vec_out[...] = own[0:8] + other[0:8]
-    vec_out[5:6] = own[5:6]
+    for n, vec in enumerate(vec_out):
+        row = own[n : n + 1] + (other[n : n + 1] if n < 5 else 0.0)
+        vec[...] = row.reshape(row.shape[1])
     for p in range(own.shape[1] // local):
 
         @pl.when(ids[2] == p)
@@ -871,16 +965,16 @@
             num_scalar_prefetch=1,
             grid=(1,),
             in_specs=[VM, VM] + [ANY] * len(after),
-            out_specs=[pl.BlockSpec((8, width), lambda *_: (0, 0)), pl.BlockSpec((local, steps), lambda *_: (0, 0))],
+            out_specs=[pl.BlockSpec((width,), lambda *_: (0,))] * 6 + [pl.BlockSpec((local, steps), lambda *_: (0, 0))],
             scratch_shapes=[
                 pltpu.VMEM((2, rows - 8, local), F32),
                 pltpu.VMEM((pl.cdiv(steps, 128) * 128, local), F32),
                 pltpu.SMEM((groups,), jnp.int32),
             ],
         ),
-        out_shape=[shape((8, width), F32), pltpu.HBM((local, steps), F32)],
+        out_shape=[pltpu.HBM((width,), F32)] * 6 + [pltpu.HBM((local, steps), F32)],
         compiler_params=params(),
-        cost_estimate=cost(3.9),
+        cost_estimate=cost("table_grad"),
         name="table_grad",
     )(scalars, own, other, *after)
 
@@ -902,33 +996,32 @@
 
 
 def order_rows(ids, own, other, after, name):
-    count = len(own)
-    part, width = own[0].shape
-
-    def kernel(ids_ref, *refs):
-        out = refs[-1]
-        i = pl.program_id(0)
-        for n in range(2 * count):
-
-            @pl.when(i == n)
-            def _():
-                out[...] = refs[n][...]
+    part, width = own.shape
+
+    def kernel(ids_ref, own_ref, other_ref, *refs):
+        out, sems = refs[len(after) :]
+        copies = []
+        for n, ref in enumerate((own_ref, other_ref)):
+            start = pl.multiple_of((ids_ref[0] ^ n) * part, 16)
+            copies.append(pltpu.make_async_copy(ref, out.at[pl.ds(start, part), :], sems.at[n]))
+            copies[-1].start()
+        for copy in copies:
+            copy.wait()
 
     return pl.pallas_call(
         kernel,
         grid_spec=pltpu.PrefetchScalarGridSpec(
             num_scalar_prefetch=1,
-            grid=(2 * count,),
-            in_specs=[VM] * (2 * count) + [ANY] * len(after),
-            out_specs=pl.BlockSpec(
-                (part, width), lambda i, ids: ((ids[0] ^ (i // count)) * count + lax.rem(i, count), 0)
-            ),
+            grid=(1,),
+            in_specs=[VM, VM] + [ANY] * len(after),
+            out_specs=HB,
+            scratch_shapes=[pltpu.SemaphoreType.DMA((2,))],
         ),
-        out_shape=pltpu.HBM((2 * count * part, width), BF16),
+        out_shape=pltpu.HBM((2 * part, width), BF16),
         compiler_params=params(),
-        cost_estimate=cost(2.0),
+        cost_estimate=cost(name),
         name=name,
-    )(ids, *own, *other, *after)
+    )(ids, own, other, *after)
 
 
 def shards(
@@ -946,8 +1039,9 @@
         orders = [low_bit, 2 * mid_bit + top_bit, mid_bit, 2 * low_bit + top_bit]
     else:
         orders = [1, 0, 1, 0]
-    ids = jnp.stack([core, dp, part, *[jnp.int32(o) for o in orders], jnp.int32(0)]).astype(jnp.int32)
-    scalars = jnp.concatenate([ids, row_length, row_group, row_step])
+    own = jnp.stack([core, dp, part, *[jnp.int32(o) for o in orders], jnp.int32(0)]).astype(jnp.int32)
+    ids = jnp.concatenate([own, row_length, row_group, row_step])
+    scalars = ids
     order_a, order_b = 3, 5
     bits = ((1, 2, 4), (2, 1, 4))
     local = w_out.shape[0]
@@ -963,73 +1057,158 @@
     send, keep, hidden, normed, q, k, v, p, ctx = attend(
         0, 1, scalars, *[far(x) for x in (tokens, time_table, norm1_gain, norm1_bias, heads, w_out)], []
     )
-    pair = add_two(keep, core_swap(send, "core_one"), [], "pair_one")
-    residual, own2 = mid_forward(hidden, pair, chip_swap(pair, "chip_one"), norm2_gain, norm2_bias, [])
-    peer2 = core_swap(own2, "core_norm")
-    send, keep, act, low, up_sum = expand(0, 1, ids, peer2, own2, far(cotangent), far(w_up), up_bias, far(w_down), [])
-    got = core_swap(send, "core_two")
+    pair = add_two(keep, core_swap(send), [], "pair_one")
+    other = chip_swap(pair)
+    w_up, w_down, cotangent = stage([far(x) for x in (w_up, w_down, cotangent)], [pair])
+    grad_act = act_grad(cotangent, w_down)
+    residual, own2 = mid_forward(hidden, pair, other, norm2_gain, norm2_bias, [grad_act])
+    peer2 = core_swap(own2)
+    send, keep, act, low, up_sum = expand(0, 1, ids, peer2, own2, grad_act, w_up, up_bias, [])
+    got_two = core_swap(send)
+    first_keep = keep
     cots = [(cotangent, size, f) for f in (peer_rows, own_rows)]
     acts = [(act, size, f) for f in (zero, one)]
     lows = [(low, size, f) for f in (zero, one)]
     norms = [(peer2, size, zero), (own2, size, zero)]
-    down = weight_grad(ids, order_a, [list(zip(acts, cots))], [keep], "down_grad")
-    mlp = Dual(bits, direct, "mlp")
-    mlp.begin(0, down)
-    pair = add_two(keep, got, [down[1]], "pair_two")
-    other = chip_swap(pair, "chip_two")
-    up = weight_grad(ids, order_b, [list(zip(norms, lows))], [pair], "up_grad")
-    mlp.begin(1, up)
-    send_e, keep_e = contract_rows(act, w_down, [up[1]])
-    got_e = core_swap(send_e, "core_out", 4)
-    mark = mlp.step(keep_e)
-    grad_residual, low_own, vec2 = mid_back(0, 1, ids, pair, other, residual, cotangent, norm2_gain, [mark])
-    low_peer = core_swap(low_own, "core_low", 4)
-    send, keep, dq, dk, dv = attend_back(low_peer, low_own, q, k, v, p, heads, w_out, [])
-    got = core_swap(send, "core_three", 4)
-    heads_sum = Dual(bits, direct, "heads")
-    mark = mlp.step(keep)
-    qk = head_grad(ids, order_a, [(dq, normed)], [(dk, normed)], [mark], "qk_grad")
-    heads_sum.begin(0, qk)
-    pair = add_two(keep, got, [qk[1]], "pair_three")
-    other = chip_swap(pair, "chip_three", 2)
-    mark = pair
-    lows1 = jnp.concatenate([low_peer, low_own], axis=0)
-    vo = head_grad(ids, order_b, [(dv, normed)], [(ctx, lows1)], [mark], "vo_grad")
-    heads_sum.begin(1, vo)
-    mark = heads_sum.step(vo[1])
-    low_in, vec1, times = last_back(pair, other, hidden, grad_residual, norm1_gain, [mark])
-    low_got = core_swap(low_in, "core_input", 4)
-    sums = pack_sums(vec2, vec1, up_sum, times, [low_in])
-    sums_got = dp_swap(sums, 1, "sums_0")
-    mark = heads_sum.step(sums)
-    pair_e = add_two(keep_e, got_e, [mark], "pair_out")
-    other_e = chip_swap(pair_e, "chip_out", 2)
-    mark = mlp.step(pair_e)
-    sums = join_sums(sums, sums_got, [mark], "join_sums_0")
-    sums_got = dp_swap(sums, 2, "sums_1")
-    input_grad = order_rows(ids, [low_in], [low_got], [sums], "order_input")
-    sums = join_sums(sums, sums_got, [far(input_grad)], "join_sums_1")
-    sums_got = dp_swap(sums, 4, "sums_2")
-    mark = heads_sum.step(sums)
-    mark = mlp.step(mark)
-    near_down, far_down = mlp.collect(0)
-    near_up, far_up = mlp.collect(1)
-    down_out = place_half(ids, order_a, near_down, 0, None, [mark], "place_down_0")
-    up_out = place_half(ids, order_b, near_up, 0, None, [far(down_out)], "place_up_0")
-    sums = join_sums(sums, sums_got, [far(up_out)], "join_sums_2")
-    bit = 8
-    while bit < n_dp:
-        sums = join_sums(sums, dp_swap(sums, bit), [], f"join_sums_{bit}")
-        bit *= 2
-    sums_peer = core_swap(sums, "core_sums")
-    mark = heads_sum.step(sums)
-    final = finish([residual], pair_e, other_e, down_bias, [mark])
-    final_got = core_swap(final, "core_final", 4)
-    vec, time_grad = table_grad(scalars, sums, sums_peer, time_table.shape[0], local, slots, [final])
-    down_out = place_half(ids, order_a, far_down, 1, down_out, [vec], "place_down_1")
-    up_out = place_half(ids, order_b, far_up, 1, up_out, [far(down_out)], "place_up_1")
-    qkv_out, proj_out = place_heads(ids, (order_a, order_b), heads_sum.collect(0), heads_sum.collect(1), [far(up_out)])
-    block_output = order_rows(ids, [final], [final_got], [far(proj_out)], "order_output")
+    mlp = Dual(bits, direct)
+    heads_sum = Dual(bits, direct)
+    it = types.SimpleNamespace(attn=[])
+    placed = [None, None]
+
+    def down_grad(after):
+        halves = weight_grad(ids, order_a, [list(zip(acts, cots))], after, "down_grad")
+        mlp.begin(0, halves)
+        return halves[1]
+
+    def up_grad(after):
+        halves = weight_grad(ids, order_b, [list(zip(norms, lows))], after, "up_grad")
+        mlp.begin(1, halves)
+        return halves[1]
+
+    def pair_two(after):
+        it.pair2 = add_two(first_keep, got_two, after, "pair_two")
+        it.other2 = chip_swap(it.pair2)
+        return it.pair2
+
+    def contract(after):
+        send, it.keep_e = contract_rows(act, w_down, after)
+        it.got_e = core_swap(send)
+        return it.keep_e
+
+    def mid(after):
+        it.grad_res, *it.low_own, it.vec2 = mid_back(
+            0, 1, ids, it.pair2, it.other2, residual, cotangent, norm2_gain, LOW_PIECES, after
+        )
+        it.low_peer = [core_swap(x) for x in it.low_own]
+        return it.low_own[0]
+
+    def attend_grad(after):
+        *send, it.keep3, it.dq, it.dk, it.dv = attend_back(
+            it.low_peer, it.low_own, q, k, v, p, heads, w_out, PART_PIECES, after
+        )
+        it.got3 = [core_swap(x) for x in send]
+        return it.keep3
+
+    def qk_grad(after):
+        halves = head_grad(ids, order_a, (it.dq, [normed]), (it.dk, [normed]), after, "qk_grad")
+        heads_sum.begin(0, halves)
+        return halves[1]
+
+    def vo_grad(after):
+        lows = [*it.low_peer, *it.low_own]
+        halves = head_grad(ids, order_b, (it.dv, [normed]), (ctx, lows), after, "vo_grad")
+        heads_sum.begin(1, halves)
+        return halves[1]
+
+    def pair_three(after):
+        it.pair3 = add_pieces(it.keep3, it.got3, 2, after, "pair_three")
+        it.other3 = [chip_swap(x) for x in it.pair3]
+        return it.pair3[0]
+
+    def pair_out(after):
+        it.pair_e = add_two(it.keep_e, it.got_e, after, "pair_out")
+        it.other_e = chip_swap(it.pair_e)
+        return it.pair_e
+
+    def last(after):
+        it.low_in, it.vec1, it.times = last_back(
+            it.pair3, it.other3, hidden, it.grad_res, norm1_gain, after
+        )
+        it.low_got = core_swap(it.low_in)
+        return it.low_in
+
+    def pack(after):
+        it.sums = pack_sums(it.vec2, it.vec1, up_sum, it.times, after)
+        it.sums_got = dp_swap(it.sums, 1)
+        return it.sums
+
+    def join(level):
+        def run(after):
+            bit = 2 << level
+            sums = join_sums(it.sums, it.sums_got, after, "join_sums")
+            while level == 2 and bit < n_dp:
+                sums = join_sums(sums, dp_swap(sums, bit), [], "join_sums")
+                bit *= 2
+            it.sums = sums
+            if level < 2:
+                it.sums_got = dp_swap(sums, bit)
+            else:
+                it.sums_peer = core_swap(sums)
+            return sums
+
+        return run
+
+    def input_rows(after):
+        it.input_grad = order_rows(ids, it.low_in, it.low_got, after, "order_input")
+        return far(it.input_grad)
+
+    def final(after):
+        it.final = finish([residual], it.pair_e, it.other_e, down_bias, after)
+        it.final_got = core_swap(it.final)
+        return it.final
+
+    def output_rows(after):
+        it.block_output = order_rows(ids, it.final, it.final_got, after, "order_output")
+        return far(it.block_output)
+
+    def table(after):
+        *it.vec, it.time_grad = table_grad(
+            scalars, it.sums, it.sums_peer, time_table.shape[0], local, slots, after
+        )
+        return far(it.vec[0])
+
+    def place(which, half):
+        def run(after):
+            order, value = (order_a, order_b)[which], mlp.collect(which)[half]
+            placed[which] = place_half(ids, order, value, half, placed[which], after, ("place_down", "place_up")[which])
+            return far(placed[which])
+
+        return run
+
+    def place_attn(half):
+        def run(after):
+            a, b = heads_sum.collect(0)[half], heads_sum.collect(1)[half]
+            it.attn = place_heads(ids, (order_a, order_b), a, b, half, it.attn, after, "place_heads")
+            return far(it.attn[1])
+
+        return run
+
+    def sum_step(group):
+        return lambda after: group.step(after[0])
+
+    order = (
+        down_grad, pair_two, up_grad, contract, mid, sum_step(mlp), attend_grad, sum_step(mlp), pair_out,
+        vo_grad, pair_three, qk_grad, sum_step(heads_sum), last, sum_step(heads_sum), pack, sum_step(mlp),
+        join(0), sum_step(heads_sum), join(1), sum_step(mlp), place(0, 0), sum_step(heads_sum), place(1, 0),
+        join(2), final, input_rows, output_rows, table, place_attn(0), place(1, 1), place(0, 1), place_attn(1),
+    )
+    mark = first_keep
+    for step in order:
+        mark = step([mark])
+    vec, time_grad = it.vec, it.time_grad
+    block_output, input_grad = it.block_output, it.input_grad
+    down_out, up_out = placed
+    qkv_out, proj_out = it.attn
 
     return (
         block_output,

time: 179 us -> 166 us (0.927)
  waiting for transfers between devices: 73.9 us -> 65.5 us
  starting transfers between devices: 40.6 us -> 36.9 us
    ppermute x51 -> x39, waiting for transfers between devices: 73.9 us -> 65.5 us  [swap(): lax.ppermute(value, axis, [(i, i ^ bit) for i in range(lax.axis_size(axis...]
    ppermute x51 -> x39, starting transfers between devices: 40.6 us -> 36.9 us  [swap(): lax.ppermute(value, axis, [(i, i ^ bit) for i in range(lax.axis_size(axis...]
    pallas_call x3 -> x5, Pallas kernels: 17.5 us -> 19 us  [the longest x1 7.19 us: attend_back(): pl.pallas_call(lambda *refs: attend_back_kernel(count, blocks, *refs[:ins...]
  transfers between devices with their start and end apart: 51 -> 39, of which waited for: 18 -> 13; matrix products, arithmetic and copies ran while one was open for 1% -> 0% of each run, Pallas kernels for 19% -> 26%
where the time goes in v3:
time: 166 us
  waiting for transfers between devices  65.5 us (39%)
  Pallas kernels  61.2 us (37%)
  starting transfers between devices  36.9 us (22%)
    ppermute x39, waiting for transfers between devices, swap(): lax.ppermute(value, axis, [(i, i ^ bit) for i in range(lax.axis_size(axis...  65.5 us
    ppermute x39, starting transfers between devices, swap(): lax.ppermute(value, axis, [(i, i ^ bit) for i in range(lax.axis_size(axis...  36.9 us
    pallas_call x1, Pallas kernels, attend(): pl.pallas_call(lambda *refs: attend_kernel(chunk, half, chunks, slots, *r...  9.79 us
    pallas_call x1, Pallas kernels, attend_back(): pl.pallas_call(lambda *refs: attend_back_kernel(count, blocks, *refs[:ins...  7.19 us
    pallas_call x4, Pallas kernels, place_half(): pl.pallas_call(kernel, grid_spec=pltpu.PrefetchScalarGridSpec(num_scalar_...  6.43 us
    pallas_call x1, Pallas kernels, expand(): pl.pallas_call(lambda *refs: expand_kernel(half, *refs[:6], *refs[6 + len...  6.03 us
    pallas_call x2, Pallas kernels, weight_grad(): pl.pallas_call(lambda ids, *refs: kernel(ids, *refs[:2 * total], *refs[2...  5.1 us
    pallas_call x1, Pallas kernels, table_grad(): pl.pallas_call(lambda *refs: table_kernel(slots, steps, *refs[:3], *refs[...  3.98 us
  transfers between devices with their start and end apart: 39, of which 13 were waited for; matrix products, arithmetic and copies ran while one was open for 0% of the time, Pallas kernels for 26%

profile of v3, /device:TPU:0, one launch (start us, length us, event | category | flops | bytes accessed | tf_op | source)
XLA Modules:
  0.0 165.9 jit_solution(11926763056044472625)
XLA Ops:
  1.4 9.8 %attend.1 = (bf16[512,768]{1,0:T(8,128)(2,1)S(1)}, bf16[512,768]{1,0:T(8,128)(2,1)S(1)}, f32[512,768]{1,0:T(8,128)S(1)}, bf16[1024,768]{1,0:T(8,128)(2,1)S(1)}, ...) custom-call(s32[152]{0:T(256)S(1)} %concatenate.3.refs_0_.ids.ids_re, ...), custom_call_target="tpu_custom_call" | custom-call | bytes 1 | tf_op jit(solution)/shard_map/attend/pallas_call | solution.py:255
  13.8 3.0 %collective-permute-start.1 = (bf16[512,768]{1,0:T(8,128)(2,1)S(1)}, bf16[512,768]{1,0:T(8,128)(2,1)S(1)}, u32[]{:S(2)}, u32[]{:S(2)}) collective-permute-start(bf16[512,768]{1,0:T(8,128)(2,1)S(1)} %pair_one.1.refs_3_.refs_1_), channel_id=1, source_target_pairs={{0,2},{1,3},{2,0},{3,1},{4,6},{5,7},{6,4},{7,5},{8,10},{9,11},{10,... | collective-permute-start | bytes 2359304 | tf_op jit(solution)/shard_map/ppermute | solution.py:57
  16.8 2.1 %stage.1 = (bf16[768,768]{1,0:T(8,128)(2,1)S(1)}, bf16[768,768]{1,0:T(8,128)(2,1)S(1)}, bf16[1024,768]{1,0:T(8,128)(2,1)S(1)}) custom-call(bf16[768,768]{1,0:T(8,128)(2,1)} %refs_0_.1, bf16[768,768]{1,0:T(8,128)(2,1)} %refs_1_.3, bf16[1024,768]{1,0:T(8,128)(2,1)} %refs_2_.3, bf16[512,768]{1,0:T(8,128)(2,1)S(1)} %pair_one.1.refs_3_.refs_1_), custom_call_target="tpu_custom_call" | custom-call | bytes 1 | tf_op jit(solution)/shard_map/stage/pallas_call | solution.py:150
  19.0 2.1 %act_grad.1.refs_5_.refs_3_ = f32[1024,768]{1,0:T(8,128)S(1)} custom-call(bf16[1024,768]{1,0:T(8,128)(2,1)S(1)} %get-tuple-element.89.cot_ref.refs_2_.refs_3_, bf16[768,768]{1,0:T(8,128)(2,1)S(1)} %get-tuple-element.90.w_ref.refs_1_), custom_call_target="tpu_custom_call" | custom-call | bytes 1 | tf_op jit(solution)/shard_map/act_grad/pallas_call | solution.py:322
  21.0 13.6 %collective-permute-done.1.refs_2_ = bf16[512,768]{1,0:T(8,128)(2,1)S(1)} collective-permute-done((bf16[512,768]{1,0:T(8,128)(2,1)S(1)}, bf16[512,768]{1,0:T(8,128)(2,1)S(1)}, u32[]{:S(2)}, u32[]{:S(2)}) %collective-permute-start.1) | collective-permute-done | bytes 786464 | tf_op jit(solution)/shard_map/ppermute | solution.py:57
  35.4 2.3 %collective-permute-done.2.refs_1_.refs_0_ = bf16[512,768]{1,0:T(8,128)(2,1)S(1)} collective-permute-done((bf16[512,768]{1,0:T(8,128)(2,1)S(1)}, bf16[512,768]{1,0:T(8,128)(2,1)S(1)}, u32[]{:S(2)}, u32[]{:S(2)}) %collective-permute-start.2) | collective-permute-done | bytes 786464 | tf_op jit(solution)/shard_map/ppermute | solution.py:57
  37.7 6.0 %expand.1 = (bf16[512,768]{1,0:T(8,128)(2,1)S(1)}, bf16[512,768]{1,0:T(8,128)(2,1)S(1)}, bf16[1024,768]{1,0:T(8,128)(2,1)S(1)}, bf16[1024,768]{1,0:T(8,128)(2,1)S(1)}, f32[1,768]{1,0:T(1,128)S(1)}) custom-call(s32[152]{0:T(256)S(1)} %concatenate.3.refs_0_.ids.ids_ref, bf16[512,768]{1,0:T(8,128)(2,1)S(1)} %collective-permute-done.2.refs_1_.refs_0_, ...), custom_call_target="tpu_custom_call" | custom-call | flops 1000000000 | bytes 1 | tf_op jit(solution)/shard_map/expand/pallas_call | solution.py:370
  44.0 2.5 %down_grad.1 = (bf16[4,96,768]{2,1,0:T(8,128)(2,1)S(1)}, bf16[4,96,768]{2,1,0:T(8,128)(2,1)S(1)}) custom-call(s32[152]{0:T(256)S(1)} %concatenate.3.refs_0_.ids.ids_ref, bf16[1024,768]{1,0:T(8,128)(2,1)S(1)} %get-tuple-element.94.refs_0_.refs_1_, bf16[1024,768]{1,0:T(8,128)(2,1)S(1)} %get-tuple-element.94.refs_0_.refs_1_, ...), custom_call_target="tpu_custom_call" | custom-call | bytes 1 | tf_op jit(solution)/shard_map/down_grad/pallas_call | solution.py:484
  50.0 2.6 %up_grad.1 = (bf16[4,96,768]{2,1,0:T(8,128)(2,1)S(1)}, bf16[4,96,768]{2,1,0:T(8,128)(2,1)S(1)}) custom-call(s32[152]{0:T(256)S(1)} %concatenate.3.refs_0_.ids.ids_ref, bf16[512,768]{1,0:T(8,128)(2,1)S(1)} %collective-permute-done.2.refs_1_.refs_0_, bf16[512,768]{1,0:T(8,128)(2,1)S(1)} %get-tuple-element.92.refs_2_.refs_1_, ...), custom_call_target="tpu_custom_call" | custom-call | bytes 1 | tf_op jit(solution)/shard_map/up_grad/pallas_call | solution.py:484
  54.2 2.1 %contract_rows.1 = (bf16[512,768]{1,0:T(8,128)(2,1)S(1)}, bf16[512,768]{1,0:T(8,128)(2,1)S(1)}) custom-call(bf16[1024,768]{1,0:T(8,128)(2,1)S(1)} %get-tuple-element.94.refs_0_.refs_1_, bf16[768,768]{1,0:T(8,128)(2,1)S(1)} %get-tuple-element.90.w_ref.refs_1_, bf16[4,96,768]{2,1,0:T(8,128)(2,1)S(1)} %get-tuple-element.99.refs_2_), custom_call_target="tpu_custom_call" | custom-call | bytes 1 | tf_op jit(solution)/shard_map/contract_rows/pallas_call | solution.py:417
  56.4 10.2 %collective-permute-done.7.refs_1_ = bf16[512,768]{1,0:T(8,128)(2,1)S(1)} collective-permute-done((bf16[512,768]{1,0:T(8,128)(2,1)S(1)}, bf16[512,768]{1,0:T(8,128)(2,1)S(1)}, u32[]{:S(2)}, u32[]{:S(2)}) %collective-permute-start.7) | collective-permute-done | bytes 786464 | tf_op jit(solution)/shard_map/ppermute | solution.py:57
  66.6 2.2 %mid_back.1 = (f32[512,768]{1,0:T(8,128)S(1)}, bf16[256,768]{1,0:T(8,128)(2,1)S(1)}, bf16[256,768]{1,0:T(8,128)(2,1)S(1)}, f32[8,768]{1,0:T(8,128)S(1)}) custom-call(s32[152]{0:T(256)S(1)} %concatenate.3.refs_0_.ids.ids_ref, bf16[512,768]{1,0:T(8,128)(2,1)S(1)} %pair_two.1.refs_4_.refs_0_, bf16[512,768]{1,0:T(8,128)(2,1)S(1)} %collective-permute-done.7.refs_1_, ...), custom_call_target="tpu_custom_call" | custom-call | bytes 1 | tf_op jit(solution)/shard_map/mid_back/pallas_call | solution.py:737
  73.1 7.2 %attend_back.1 = (bf16[128,768]{1,0:T(8,128)(2,1)S(1)}, bf16[128,768]{1,0:T(8,128)(2,1)S(1)}, bf16[128,768]{1,0:T(8,128)(2,1)S(1)}, bf16[128,768]{1,0:T(8,128)(2...) custom-call(bf16[256,768]{1,0:T(8,128)(2,1)S(1)} %collective-permute, ...), custom_call_target="tpu_custom_call" | custom-call | bytes 1 | tf_op jit(solution)/shard_map/attend_back/pallas_call | solution.py:820
  83.7 2.6 %collective-permute-start.24 = (bf16[2,2,96,768]{3,2,1,0:T(8,128)(2,1)S(1)}, bf16[2,2,96,768]{3,2,1,0:T(8,128)(2,1)S(1)}, u32[]{:S(2)}, u32[]{:S(2)}) collective-permute-start(bf16[2,2,96,768]{3,2,1,0:T(8,128)(2,1)S(1)} %exchange.9.refs_2_.refs_0_), channel_id=1, source_target_pairs={{0,16},{4,20},{8,24},{12,28},{16,0},{20,4},{24,8},{28,12},{1,17},{... | collective-permute-start | bytes 1769480 | tf_op jit(solution)/shard_map/ppermute | solution.py:57
  91.0 8.5 %collective-permute-done.20.refs_3_ = bf16[4,2,24,768]{3,2,1,0:T(8,128)(2,1)S(1)} collective-permute-done((bf16[4,2,24,768]{3,2,1,0:T(8,128)(2,1)S(1)}, bf16[4,2,24,768]{3,2,1,0:T(8,128)(2,1)S(1)}, u32[]{:S(2)}, u32[]{:S(2)}) %collective-permute-start.20) | collective-permute-done | bytes 294944 | tf_op jit(solution)/shard_map/ppermute | solution.py:57
  102.1 5.0 %collective-permute-done.17.refs_2_ = bf16[256,768]{1,0:T(8,128)(2,1)S(1)} collective-permute-done((bf16[256,768]{1,0:T(8,128)(2,1)S(1)}, bf16[256,768]{1,0:T(8,128)(2,1)S(1)}, u32[]{:S(2)}, u32[]{:S(2)}) %collective-permute-start.17) | collective-permute-done | bytes 393248 | tf_op jit(solution)/shard_map/ppermute | solution.py:57
  108.8 2.0 %collective-permute-start.26 = (bf16[2,2,2,24,768]{4,3,2,1,0:T(8,128)(2,1)S(1)}, bf16[2,2,2,24,768]{4,3,2,1,0:T(8,128)(2,1)S(1)}, u32[]{:S(2)}, u32[]{:S(2)}) collective-permute-start(bf16[2,2,2,24,768]{4,3,2,1,0:T(8,128)(2,1)S(1)} %exchange.11.refs_4_.refs_0_), channel_id=1, source_target_pairs={{0,16},{4,20},{8,24},{12,28},{16,0},{20,4},{24,8},{28,12},{1,17},{... | collective-permute-start | bytes 884744 | tf_op jit(solution)/shard_map/ppermute | solution.py:57
  110.8 9.0 %collective-permute-done.24.refs_1_ = bf16[2,2,96,768]{3,2,1,0:T(8,128)(2,1)S(1)} collective-permute-done((bf16[2,2,96,768]{3,2,1,0:T(8,128)(2,1)S(1)}, bf16[2,2,96,768]{3,2,1,0:T(8,128)(2,1)S(1)}, u32[]{:S(2)}, u32[]{:S(2)}) %collective-permute-start.24) | collective-permute-done | bytes 589856 | tf_op jit(solution)/shard_map/ppermute | solution.py:57
  122.8 5.2 %collective-permute-done.23.refs_1_ = f32[12,768]{1,0:T(8,128)S(1)} collective-permute-done((f32[12,768]{1,0:T(8,128)S(1)}, f32[12,768]{1,0:T(8,128)S(1)}, u32[]{:S(2)}, u32[]{:S(2)}) %collective-permute-start.23) | collective-permute-done | bytes 36896 | tf_op jit(solution)/shard_map/ppermute | solution.py:57
  129.2 3.2 %collective-permute-done.25.refs_1_ = f32[16,768]{1,0:T(8,128)S(1)} collective-permute-done((f32[16,768]{1,0:T(8,128)S(1)}, f32[16,768]{1,0:T(8,128)S(1)}, u32[]{:S(2)}, u32[]{:S(2)}) %collective-permute-start.25) | collective-permute-done | bytes 49184 | tf_op jit(solution)/shard_map/ppermute | solution.py:57
  132.4 4.2 %collective-permute-start.27 = (f32[24,768]{1,0:T(8,128)S(1)}, f32[24,768]{1,0:T(8,128)S(1)}, u32[]{:S(2)}, u32[]{:S(2)}) collective-permute-start(f32[24,768]{1,0:T(8,128)S(1)} %join_sums.4.refs_4_.refs_0_), channel_id=1, source_target_pairs={{0,16},{4,20},{8,24},{12,28},{16,0},{20,4},{24,8},{28,12},{1,17},{... | collective-permute-start | bytes 221192 | tf_op jit(solution)/shard_map/ppermute | solution.py:57
  148.8 4.0 %table_grad.1 = (f32[768]{0:T(1024)}, f32[768]{0:T(1024)}, f32[768]{0:T(1024)}, f32[768]{0:T(1024)}, f32[768]{0:T(1024)}, /*index=5*/f32[768]{0:T(1024)}, f32[192,1000]{1,0:T(8,128)}) custom-call(s32[152]{0:T(256)S(1)} %concatenate.3.refs_0_.ids.ids_ref, f32[40,768]{1,0:T(8,128)S(1)} %join_sums.5.refs_4_.refs_1_, ...), custom_call_target="tpu_custom_call" | custom-call | bytes 1 | tf_op jit(solution)/shard_map/table_grad/pallas_call | solution.py:962
  154.5 3.0 %collective-permute-done.38.value_ref = bf16[4,96,768]{2,1,0:T(8,128)(2,1)S(1)} collective-permute-done((bf16[4,96,768]{2,1,0:T(8,128)(2,1)S(1)}, bf16[4,96,768]{2,1,0:T(8,128)(2,1)S(1)}, u32[]{:S(2)}, u32[]{:S(2)}) %collective-permute-start.38) | collective-permute-done | bytes 589856 | tf_op jit(solution)/shard_map/ppermute | solution.py:57
  160.7 2.5 %collective-permute-done.36.b_ref = bf16[4,2,24,768]{3,2,1,0:T(8,128)(2,1)S(1)} collective-permute-done((bf16[4,2,24,768]{3,2,1,0:T(8,128)(2,1)S(1)}, bf16[4,2,24,768]{3,2,1,0:T(8,128)(2,1)S(1)}, u32[]{:S(2)}, u32[]{:S(2)}) %collective-permute-start.36) | collective-permute-done | bytes 294944 | tf_op jit(solution)/shard_map/ppermute | solution.py:57
  (108 shorter events, 49.9 us)
Async XLA Ops:
  13.8 20.8 %collective-permute-start.1 = (bf16[512,768]{1,0:T(8,128)(2,1)S(1)}, bf16[512,768]{1,0:T(8,128)(2,1)S(1)}, u32[]{:S(2)}, u32[]{:S(2)}) collective-permute-start(bf16[512,768]{1,0:T(8,128)(2,1)S(1)} %pair_one.1.refs_3_.refs_1_), channel_id=1, source_target_pairs={{0,2},{1,3},{2,0},{3,1},{4,6},{5,7},{6,4},{7,5},{8,10},{9,11},{10,... | collective-permute-start | bytes 2359304 | tf_op jit(solution)/shard_map/ppermute | solution.py:57
  46.7 19.9 %collective-permute-start.7 = (bf16[512,768]{1,0:T(8,128)(2,1)S(1)}, bf16[512,768]{1,0:T(8,128)(2,1)S(1)}, u32[]{:S(2)}, u32[]{:S(2)}) collective-permute-start(bf16[512,768]{1,0:T(8,128)(2,1)S(1)} %pair_two.1.refs_4_.refs_0_), channel_id=1, source_target_pairs={{0,2},{1,3},{2,0},{3,1},{4,6},{5,7},{6,4},{7,5},{8,10},{9,11},{10,... | collective-permute-start | bytes 2359304 | tf_op jit(solution)/shard_map/ppermute | solution.py:57
  48.5 20.9 %collective-permute-start.5 = (bf16[4,96,768]{2,1,0:T(8,128)(2,1)S(1)}, bf16[4,96,768]{2,1,0:T(8,128)(2,1)S(1)}, u32[]{:S(2)}, u32[]{:S(2)}) collective-permute-start(bf16[4,96,768]{2,1,0:T(8,128)(2,1)S(1)} %get-tuple-element.102), channel_id=1, source_target_pairs={{0,4},{4,0},{8,12},{12,8},{16,20},{20,16},{24,28},{28,24},{1,5},{5... | collective-permute-start | bytes 1769480 | tf_op jit(solution)/shard_map/ppermute | solution.py:57
  52.6 16.8 %collective-permute-start.6 = (bf16[4,96,768]{2,1,0:T(8,128)(2,1)S(1)}, bf16[4,96,768]{2,1,0:T(8,128)(2,1)S(1)}, u32[]{:S(2)}, u32[]{:S(2)}) collective-permute-start(bf16[4,96,768]{2,1,0:T(8,128)(2,1)S(1)} %get-tuple-element.103), channel_id=1, source_target_pairs={{0,8},{4,12},{8,0},{12,4},{16,24},{20,28},{24,16},{28,20},{1,9},{5... | collective-permute-start | bytes 1769480 | tf_op jit(solution)/shard_map/ppermute | solution.py:57
  56.3 25.2 %collective-permute-start.4 = (bf16[512,768]{1,0:T(8,128)(2,1)S(1)}, bf16[512,768]{1,0:T(8,128)(2,1)S(1)}, u32[]{:S(2)}, u32[]{:S(2)}) collective-permute-start(bf16[512,768]{1,0:T(8,128)(2,1)S(1)} %get-tuple-element.101), channel_id=1, source_target_pairs={{0,1},{1,0},{2,3},{3,2},{4,5},{5,4},{6,7},{7,6},{8,9},{9,8},{10,11... | collective-permute-start | bytes 2359304 | tf_op jit(solution)/shard_map/ppermute | solution.py:57
  69.7 11.1 %collective-permute-start.8 = (bf16[2,96,768]{2,1,0:T(8,128)(2,1)S(1)}, bf16[2,96,768]{2,1,0:T(8,128)(2,1)S(1)}, u32[]{:S(2)}, u32[]{:S(2)}) collective-permute-start(bf16[2,96,768]{2,1,0:T(8,128)(2,1)S(1)} %get-tuple-element.106), channel_id=1, source_target_pairs={{0,8},{4,12},{8,0},{12,4},{16,24},{20,28},{24,16},{28,20},{1,9},{5... | collective-permute-start | bytes 884744 | tf_op jit(solution)/shard_map/ppermute | solution.py:57
  71.6 9.3 %collective-permute-start.9 = (bf16[2,96,768]{2,1,0:T(8,128)(2,1)S(1)}, bf16[2,96,768]{2,1,0:T(8,128)(2,1)S(1)}, u32[]{:S(2)}, u32[]{:S(2)}) collective-permute-start(bf16[2,96,768]{2,1,0:T(8,128)(2,1)S(1)} %get-tuple-element.108), channel_id=1, source_target_pairs={{0,4},{4,0},{8,12},{12,8},{16,20},{20,16},{24,28},{28,24},{1,5},{5... | collective-permute-start | bytes 884744 | tf_op jit(solution)/shard_map/ppermute | solution.py:57
  83.2 16.4 %collective-permute-start.20 = (bf16[4,2,24,768]{3,2,1,0:T(8,128)(2,1)S(1)}, bf16[4,2,24,768]{3,2,1,0:T(8,128)(2,1)S(1)}, u32[]{:S(2)}, u32[]{:S(2)}) collective-permute-start(bf16[4,2,24,768]{3,2,1,0:T(8,128)(2,1)S(1)} %get-tuple-element.131), channel_id=1, source_target_pairs={{0,8},{4,12},{8,0},{12,4},{16,24},{20,28},{24,16},{28,20},{1,9},{5... | collective-permute-start | bytes 884744 | tf_op jit(solution)/shard_map/ppermute | solution.py:57
  83.7 36.1 %collective-permute-start.24 = (bf16[2,2,96,768]{3,2,1,0:T(8,128)(2,1)S(1)}, bf16[2,2,96,768]{3,2,1,0:T(8,128)(2,1)S(1)}, u32[]{:S(2)}, u32[]{:S(2)}) collective-permute-start(bf16[2,2,96,768]{3,2,1,0:T(8,128)(2,1)S(1)} %exchange.9.refs_2_.refs_0_), channel_id=1, source_target_pairs={{0,16},{4,20},{8,24},{12,28},{16,0},{20,4},{24,8},{28,12},{1,17},{... | collective-permute-start | bytes 1769480 | tf_op jit(solution)/shard_map/ppermute | solution.py:57
  86.5 14.8 %collective-permute-start.18 = (bf16[256,768]{1,0:T(8,128)(2,1)S(1)}, bf16[256,768]{1,0:T(8,128)(2,1)S(1)}, u32[]{:S(2)}, u32[]{:S(2)}) collective-permute-start(bf16[256,768]{1,0:T(8,128)(2,1)S(1)} %get-tuple-element.125.refs_1_), channel_id=1, source_target_pairs={{0,2},{1,3},{2,0},{3,1},{4,6},{5,7},{6,4},{7,5},{8,10},{9,11},{10,... | collective-permute-start | bytes 1179656 | tf_op jit(solution)/shard_map/ppermute | solution.py:57
  89.5 11.6 %collective-permute-start.19 = (bf16[4,2,24,768]{3,2,1,0:T(8,128)(2,1)S(1)}, bf16[4,2,24,768]{3,2,1,0:T(8,128)(2,1)S(1)}, u32[]{:S(2)}, u32[]{:S(2)}) collective-permute-start(bf16[4,2,24,768]{3,2,1,0:T(8,128)(2,1)S(1)} %get-tuple-element.130), channel_id=1, source_target_pairs={{0,4},{4,0},{8,12},{12,8},{16,20},{20,16},{24,28},{28,24},{1,5},{5... | collective-permute-start | bytes 884744 | tf_op jit(solution)/shard_map/ppermute | solution.py:57
  90.5 16.5 %collective-permute-start.17 = (bf16[256,768]{1,0:T(8,128)(2,1)S(1)}, bf16[256,768]{1,0:T(8,128)(2,1)S(1)}, u32[]{:S(2)}, u32[]{:S(2)}) collective-permute-start(bf16[256,768]{1,0:T(8,128)(2,1)S(1)} %get-tuple-element.124.refs_4_.refs_0_), channel_id=1, source_target_pairs={{0,2},{1,3},{2,0},{3,1},{4,6},{5,7},{6,4},{7,5},{8,10},{9,11},{10,... | collective-permute-start | bytes 1179656 | tf_op jit(solution)/shard_map/ppermute | solution.py:57
  99.6 40.8 %collective-permute-start.12 = (bf16[512,768]{1,0:T(8,128)(2,1)S(1)}, bf16[512,768]{1,0:T(8,128)(2,1)S(1)}, u32[]{:S(2)}, u32[]{:S(2)}) collective-permute-start(bf16[512,768]{1,0:T(8,128)(2,1)S(1)} %pair_out.1.refs_7_.refs_1_), channel_id=1, source_target_pairs={{0,2},{1,3},{2,0},{3,1},{4,6},{5,7},{6,4},{7,5},{8,10},{9,11},{10,... | collective-permute-start | bytes 2359304 | tf_op jit(solution)/shard_map/ppermute | solution.py:57
  101.3 7.4 %collective-permute-start.21 = (bf16[2,2,24,768]{3,2,1,0:T(8,128)(2,1)S(1)}, bf16[2,2,24,768]{3,2,1,0:T(8,128)(2,1)S(1)}, u32[]{:S(2)}, u32[]{:S(2)}) collective-permute-start(bf16[2,2,24,768]{3,2,1,0:T(8,128)(2,1)S(1)} %get-tuple-element.136), channel_id=1, source_target_pairs={{0,8},{4,12},{8,0},{12,4},{16,24},{20,28},{24,16},{28,20},{1,9},{5... | collective-permute-start | bytes 442376 | tf_op jit(solution)/shard_map/ppermute | solution.py:57
  108.8 19.4 %collective-permute-start.26 = (bf16[2,2,2,24,768]{4,3,2,1,0:T(8,128)(2,1)S(1)}, bf16[2,2,2,24,768]{4,3,2,1,0:T(8,128)(2,1)S(1)}, u32[]{:S(2)}, u32[]{:S(2)}) collective-permute-start(bf16[2,2,2,24,768]{4,3,2,1,0:T(8,128)(2,1)S(1)} %exchange.11.refs_4_.refs_0_), channel_id=1, source_target_pairs={{0,16},{4,20},{8,24},{12,28},{16,0},{20,4},{24,8},{28,12},{1,17},{... | collective-permute-start | bytes 884744 | tf_op jit(solution)/shard_map/ppermute | solution.py:57
  120.0 12.4 %collective-permute-start.29 = (bf16[2,96,768]{2,1,0:T(8,128)(2,1)S(1)}, bf16[2,96,768]{2,1,0:T(8,128)(2,1)S(1)}, u32[]{:S(2)}, u32[]{:S(2)}) collective-permute-start(bf16[2,96,768]{2,1,0:T(8,128)(2,1)S(1)} %get-tuple-element.142.refs_2_), channel_id=1, source_target_pairs={{0,4},{4,0},{8,12},{12,8},{16,20},{20,16},{24,28},{28,24},{1,5},{5... | collective-permute-start | bytes 884744 | tf_op jit(solution)/shard_map/ppermute | solution.py:57
  120.9 11.4 %collective-permute-start.28 = (bf16[2,96,768]{2,1,0:T(8,128)(2,1)S(1)}, bf16[2,96,768]{2,1,0:T(8,128)(2,1)S(1)}, u32[]{:S(2)}, u32[]{:S(2)}) collective-permute-start(bf16[2,96,768]{2,1,0:T(8,128)(2,1)S(1)} %get-tuple-element.140.refs_2_.refs_0_), channel_id=1, source_target_pairs={{0,8},{4,12},{8,0},{12,4},{16,24},{20,28},{24,16},{28,20},{1,9},{5... | collective-permute-start | bytes 884744 | tf_op jit(solution)/shard_map/ppermute | solution.py:57
  128.2 10.1 %collective-permute-start.31 = (bf16[2,2,24,768]{3,2,1,0:T(8,128)(2,1)S(1)}, bf16[2,2,24,768]{3,2,1,0:T(8,128)(2,1)S(1)}, u32[]{:S(2)}, u32[]{:S(2)}) collective-permute-start(bf16[2,2,24,768]{3,2,1,0:T(8,128)(2,1)S(1)} %get-tuple-element.144.refs_2_), channel_id=1, source_target_pairs={{0,4},{4,0},{8,12},{12,8},{16,20},{20,16},{24,28},{28,24},{1,5},{5... | collective-permute-start | bytes 442376 | tf_op jit(solution)/shard_map/ppermute | solution.py:57
  132.4 11.8 %collective-permute-start.33 = (bf16[512,768]{1,0:T(8,128)(2,1)S(1)}, bf16[512,768]{1,0:T(8,128)(2,1)S(1)}, u32[]{:S(2)}, u32[]{:S(2)}) collective-permute-start(bf16[512,768]{1,0:T(8,128)(2,1)S(1)} %get-tuple-element.139.refs_4_.own_ref), channel_id=1, source_target_pairs={{0,1},{1,0},{2,3},{3,2},{4,5},{5,4},{6,7},{7,6},{8,9},{9,8},{10,11... | collective-permute-start | bytes 2359304 | tf_op jit(solution)/shard_map/ppermute | solution.py:57
  132.4 7.9 %collective-permute-start.27 = (f32[24,768]{1,0:T(8,128)S(1)}, f32[24,768]{1,0:T(8,128)S(1)}, u32[]{:S(2)}, u32[]{:S(2)}) collective-permute-start(f32[24,768]{1,0:T(8,128)S(1)} %join_sums.4.refs_4_.refs_0_), channel_id=1, source_target_pairs={{0,16},{4,20},{8,24},{12,28},{16,0},{20,4},{24,8},{28,12},{1,17},{... | collective-permute-start | bytes 221192 | tf_op jit(solution)/shard_map/ppermute | solution.py:57
  141.3 16.1 %collective-permute-start.38 = (bf16[4,96,768]{2,1,0:T(8,128)(2,1)S(1)}, bf16[4,96,768]{2,1,0:T(8,128)(2,1)S(1)}, u32[]{:S(2)}, u32[]{:S(2)}) collective-permute-start(bf16[4,96,768]{2,1,0:T(8,128)(2,1)S(1)} %get-tuple-element.143.value_ref), channel_id=1, source_target_pairs={{0,8},{4,12},{8,0},{12,4},{16,24},{20,28},{24,16},{28,20},{1,9},{5... | collective-permute-start | bytes 1769480 | tf_op jit(solution)/shard_map/ppermute | solution.py:57
  142.3 16.8 %collective-permute-start.37 = (bf16[4,96,768]{2,1,0:T(8,128)(2,1)S(1)}, bf16[4,96,768]{2,1,0:T(8,128)(2,1)S(1)}, u32[]{:S(2)}, u32[]{:S(2)}) collective-permute-start(bf16[4,96,768]{2,1,0:T(8,128)(2,1)S(1)} %get-tuple-element.145.value_ref.refs_0_), channel_id=1, source_target_pairs={{0,4},{4,0},{8,12},{12,8},{16,20},{20,16},{24,28},{28,24},{1,5},{5... | collective-permute-start | bytes 1769480 | tf_op jit(solution)/shard_map/ppermute | solution.py:57
  143.1 20.1 %collective-permute-start.36 = (bf16[4,2,24,768]{3,2,1,0:T(8,128)(2,1)S(1)}, bf16[4,2,24,768]{3,2,1,0:T(8,128)(2,1)S(1)}, u32[]{:S(2)}, u32[]{:S(2)}) collective-permute-start(bf16[4,2,24,768]{3,2,1,0:T(8,128)(2,1)S(1)} %get-tuple-element.150.b_ref), channel_id=1, source_target_pairs={{0,8},{4,12},{8,0},{12,4},{16,24},{20,28},{24,16},{28,20},{1,9},{5... | collective-permute-start | bytes 884744 | tf_op jit(solution)/shard_map/ppermute | solution.py:57
  144.2 19.9 %collective-permute-start.35 = (bf16[4,2,24,768]{3,2,1,0:T(8,128)(2,1)S(1)}, bf16[4,2,24,768]{3,2,1,0:T(8,128)(2,1)S(1)}, u32[]{:S(2)}, u32[]{:S(2)}) collective-permute-start(bf16[4,2,24,768]{3,2,1,0:T(8,128)(2,1)S(1)} %get-tuple-element.146.refs_0_.a_ref), channel_id=1, source_target_pairs={{0,4},{4,0},{8,12},{12,8},{16,20},{20,16},{24,28},{28,24},{1,5},{5... | collective-permute-start | bytes 884744 | tf_op jit(solution)/shard_map/ppermute | solution.py:57
  (22 other events, 130.8 us)

commit v4 on v3

--- a/solution.py
+++ b/solution.py
@@ -37,7 +37,7 @@
     )
 
 
-COSTS = {"expand": 1, "finish": 0.5, "order_input": 0.5}
+COSTS = {"finish": 0.5, "up_grad": 1}
 
 
 def cost(name):
@@ -1034,7 +1034,8 @@
     part = lax.axis_index("tensor")
     core = lax.rem(part, 2)
     direct = n_dp == 8
-    low_bit, mid_bit, top_bit = dp & 1, (dp >> 1) & 1, (dp >> 2) & 1
+    low_bit, top_bit = dp & 1, (dp >> 2) & 1
+    mid_bit = ((dp >> 1) & 1) ^ top_bit
     if direct:
         orders = [low_bit, 2 * mid_bit + top_bit, mid_bit, 2 * low_bit + top_bit]
     else:
@@ -1043,7 +1044,7 @@
     ids = jnp.concatenate([own, row_length, row_group, row_step])
     scalars = ids
     order_a, order_b = 3, 5
-    bits = ((1, 2, 4), (2, 1, 4))
+    bits = ((1, 2, 6), (2, 1, 6))
     local = w_out.shape[0]
     slots = count // SHORT
     heads = jnp.transpose(w_qkv, (1, 2, 0))
@@ -1197,10 +1198,11 @@
         return lambda after: group.step(after[0])
 
     order = (
-        down_grad, pair_two, up_grad, contract, mid, sum_step(mlp), attend_grad, sum_step(mlp), pair_out,
-        vo_grad, pair_three, qk_grad, sum_step(heads_sum), last, sum_step(heads_sum), pack, sum_step(mlp),
-        join(0), sum_step(heads_sum), join(1), sum_step(mlp), place(0, 0), sum_step(heads_sum), place(1, 0),
-        join(2), final, input_rows, output_rows, table, place_attn(0), place(1, 1), place(0, 1), place_attn(1),
+        down_grad, pair_two, up_grad, contract, mid, sum_step(mlp), attend_grad, sum_step(mlp), vo_grad,
+        pair_out, pair_three, qk_grad, sum_step(heads_sum), last, sum_step(heads_sum), pack, sum_step(mlp),
+        sum_step(heads_sum), join(0), join(1), sum_step(mlp), sum_step(heads_sum), place_attn(0), join(2),
+        final, place(0, 0), place(1, 0), input_rows, output_rows, table, place(1, 1), place(0, 1),
+        place_attn(1),
     )
     mark = first_keep
     for step in order:

time: 166 us -> 160 us (0.964)
  waiting for transfers between devices: 65.5 us -> 54.1 us
  starting transfers between devices: 36.9 us -> 42.6 us
    ppermute x39, waiting for transfers between devices: 65.5 us -> 54.1 us  [swap(): lax.ppermute(value, axis, [(i, i ^ bit) for i in range(lax.axis_size(axis...]
    ppermute x39, starting transfers between devices: 36.9 us -> 42.6 us  [swap(): lax.ppermute(value, axis, [(i, i ^ bit) for i in range(lax.axis_size(axis...]
  transfers between devices with their start and end apart: 39 -> 39, of which waited for: 13 -> 15; matrix products, arithmetic and copies ran while one was open for 0% -> 0% of each run, Pallas kernels for 26% -> 27%
where the time goes in v4:
time: 160 us
  Pallas kernels  61.2 us (38%)
  waiting for transfers between devices  54.1 us (34%)
  starting transfers between devices  42.6 us (27%)
    ppermute x39, waiting for transfers between devices, swap(): lax.ppermute(value, axis, [(i, i ^ bit) for i in range(lax.axis_size(axis...  54.1 us
    ppermute x39, starting transfers between devices, swap(): lax.ppermute(value, axis, [(i, i ^ bit) for i in range(lax.axis_size(axis...  42.6 us
    pallas_call x1, Pallas kernels, attend(): pl.pallas_call(lambda *refs: attend_kernel(chunk, half, chunks, slots, *r...  9.79 us
    pallas_call x1, Pallas kernels, attend_back(): pl.pallas_call(lambda *refs: attend_back_kernel(count, blocks, *refs[:ins...  7.18 us
    pallas_call x4, Pallas kernels, place_half(): pl.pallas_call(kernel, grid_spec=pltpu.PrefetchScalarGridSpec(num_scalar_...  6.43 us
    pallas_call x1, Pallas kernels, expand(): pl.pallas_call(lambda *refs: expand_kernel(half, *refs[:6], *refs[6 + len...  6.04 us
    pallas_call x2, Pallas kernels, weight_grad(): pl.pallas_call(lambda ids, *refs: kernel(ids, *refs[:2 * total], *refs[2...  5.1 us
    pallas_call x1, Pallas kernels, table_grad(): pl.pallas_call(lambda *refs: table_kernel(slots, steps, *refs[:3], *refs[...  3.98 us
  transfers between devices with their start and end apart: 39, of which 15 were waited for; matrix products, arithmetic and copies ran while one was open for 0% of the time, Pallas kernels for 27%

profile of v4, /device:TPU:0, one launch (start us, length us, event | category | flops | bytes accessed | tf_op | source)
XLA Modules:
  0.0 160.0 jit_solution(4831172646263317590)
XLA Ops:
  1.4 9.8 %attend.1 = (bf16[512,768]{1,0:T(8,128)(2,1)S(1)}, bf16[512,768]{1,0:T(8,128)(2,1)S(1)}, f32[512,768]{1,0:T(8,128)S(1)}, bf16[1024,768]{1,0:T(8,128)(2,1)S(1)}, ...) custom-call(s32[152]{0:T(256)S(1)} %concatenate.3.refs_0_.ids.ids_re, ...), custom_call_target="tpu_custom_call" | custom-call | bytes 1 | tf_op jit(solution)/shard_map/attend/pallas_call | solution.py:255
  13.8 3.0 %collective-permute-start.1 = (bf16[512,768]{1,0:T(8,128)(2,1)S(1)}, bf16[512,768]{1,0:T(8,128)(2,1)S(1)}, u32[]{:S(2)}, u32[]{:S(2)}) collective-permute-start(bf16[512,768]{1,0:T(8,128)(2,1)S(1)} %pair_one.1.refs_3_.refs_1_), channel_id=1, source_target_pairs={{0,2},{1,3},{2,0},{3,1},{4,6},{5,7},{6,4},{7,5},{8,10},{9,11},{10,... | collective-permute-start | bytes 2359304 | tf_op jit(solution)/shard_map/ppermute | solution.py:57
  16.8 2.1 %stage.1 = (bf16[768,768]{1,0:T(8,128)(2,1)S(1)}, bf16[768,768]{1,0:T(8,128)(2,1)S(1)}, bf16[1024,768]{1,0:T(8,128)(2,1)S(1)}) custom-call(bf16[768,768]{1,0:T(8,128)(2,1)} %refs_0_.1, bf16[768,768]{1,0:T(8,128)(2,1)} %refs_1_.3, bf16[1024,768]{1,0:T(8,128)(2,1)} %refs_2_.3, bf16[512,768]{1,0:T(8,128)(2,1)S(1)} %pair_one.1.refs_3_.refs_1_), custom_call_target="tpu_custom_call" | custom-call | bytes 1 | tf_op jit(solution)/shard_map/stage/pallas_call | solution.py:150
  19.0 2.1 %act_grad.1.refs_5_.refs_3_ = f32[1024,768]{1,0:T(8,128)S(1)} custom-call(bf16[1024,768]{1,0:T(8,128)(2,1)S(1)} %get-tuple-element.89.cot_ref.refs_2_.refs_3_, bf16[768,768]{1,0:T(8,128)(2,1)S(1)} %get-tuple-element.90.w_ref.refs_1_), custom_call_target="tpu_custom_call" | custom-call | bytes 1 | tf_op jit(solution)/shard_map/act_grad/pallas_call | solution.py:322
  21.0 13.6 %collective-permute-done.1.refs_2_ = bf16[512,768]{1,0:T(8,128)(2,1)S(1)} collective-permute-done((bf16[512,768]{1,0:T(8,128)(2,1)S(1)}, bf16[512,768]{1,0:T(8,128)(2,1)S(1)}, u32[]{:S(2)}, u32[]{:S(2)}) %collective-permute-start.1) | collective-permute-done | bytes 786464 | tf_op jit(solution)/shard_map/ppermute | solution.py:57
  35.4 2.3 %collective-permute-done.2.refs_1_.refs_0_ = bf16[512,768]{1,0:T(8,128)(2,1)S(1)} collective-permute-done((bf16[512,768]{1,0:T(8,128)(2,1)S(1)}, bf16[512,768]{1,0:T(8,128)(2,1)S(1)}, u32[]{:S(2)}, u32[]{:S(2)}) %collective-permute-start.2) | collective-permute-done | bytes 786464 | tf_op jit(solution)/shard_map/ppermute | solution.py:57
  37.7 6.0 %expand.1 = (bf16[512,768]{1,0:T(8,128)(2,1)S(1)}, bf16[512,768]{1,0:T(8,128)(2,1)S(1)}, bf16[1024,768]{1,0:T(8,128)(2,1)S(1)}, bf16[1024,768]{1,0:T(8,128)(2,1)S(1)}, f32[1,768]{1,0:T(1,128)S(1)}) custom-call(s32[152]{0:T(256)S(1)} %concatenate.3.refs_0_.ids.ids_ref, bf16[512,768]{1,0:T(8,128)(2,1)S(1)} %collective-permute-done.2.refs_1_.refs_0_, ...), custom_call_target="tpu_custom_call" | custom-call | bytes 1 | tf_op jit(solution)/shard_map/expand/pallas_call | solution.py:370
  44.0 2.5 %down_grad.1 = (bf16[4,96,768]{2,1,0:T(8,128)(2,1)S(1)}, bf16[4,96,768]{2,1,0:T(8,128)(2,1)S(1)}) custom-call(s32[152]{0:T(256)S(1)} %concatenate.3.refs_0_.ids.ids_ref, bf16[1024,768]{1,0:T(8,128)(2,1)S(1)} %get-tuple-element.94.refs_0_.refs_1_, bf16[1024,768]{1,0:T(8,128)(2,1)S(1)} %get-tuple-element.94.refs_0_.refs_1_, ...), custom_call_target="tpu_custom_call" | custom-call | bytes 1 | tf_op jit(solution)/shard_map/down_grad/pallas_call | solution.py:484
  50.0 2.6 %up_grad.1 = (bf16[4,96,768]{2,1,0:T(8,128)(2,1)S(1)}, bf16[4,96,768]{2,1,0:T(8,128)(2,1)S(1)}) custom-call(s32[152]{0:T(256)S(1)} %concatenate.3.refs_0_.ids.ids_ref, bf16[512,768]{1,0:T(8,128)(2,1)S(1)} %collective-permute-done.2.refs_1_.refs_0_, bf16[512,768]{1,0:T(8,128)(2,1)S(1)} %get-tuple-element.92.refs_2_.refs_1_, ...), custom_call_target="tpu_custom_call" | custom-call | flops 1000000000 | bytes 1 | tf_op jit(solution)/shard_map/up_grad/pallas_call | solution.py:484
  54.2 2.1 %contract_rows.1 = (bf16[512,768]{1,0:T(8,128)(2,1)S(1)}, bf16[512,768]{1,0:T(8,128)(2,1)S(1)}) custom-call(bf16[1024,768]{1,0:T(8,128)(2,1)S(1)} %get-tuple-element.94.refs_0_.refs_1_, bf16[768,768]{1,0:T(8,128)(2,1)S(1)} %get-tuple-element.90.w_ref.refs_1_, bf16[4,96,768]{2,1,0:T(8,128)(2,1)S(1)} %get-tuple-element.99.refs_2_), custom_call_target="tpu_custom_call" | custom-call | bytes 1 | tf_op jit(solution)/shard_map/contract_rows/pallas_call | solution.py:417
  56.4 10.2 %collective-permute-done.5.refs_1_ = bf16[512,768]{1,0:T(8,128)(2,1)S(1)} collective-permute-done((bf16[512,768]{1,0:T(8,128)(2,1)S(1)}, bf16[512,768]{1,0:T(8,128)(2,1)S(1)}, u32[]{:S(2)}, u32[]{:S(2)}) %collective-permute-start.5) | collective-permute-done | bytes 786464 | tf_op jit(solution)/shard_map/ppermute | solution.py:57
  66.6 2.2 %mid_back.1 = (f32[512,768]{1,0:T(8,128)S(1)}, bf16[256,768]{1,0:T(8,128)(2,1)S(1)}, bf16[256,768]{1,0:T(8,128)(2,1)S(1)}, f32[8,768]{1,0:T(8,128)S(1)}) custom-call(s32[152]{0:T(256)S(1)} %concatenate.3.refs_0_.ids.ids_ref, bf16[512,768]{1,0:T(8,128)(2,1)S(1)} %pair_two.1.refs_4_.refs_0_, bf16[512,768]{1,0:T(8,128)(2,1)S(1)} %collective-permute-done.5.refs_1_, ...), custom_call_target="tpu_custom_call" | custom-call | bytes 1 | tf_op jit(solution)/shard_map/mid_back/pallas_call | solution.py:737
  73.1 7.2 %attend_back.1 = (bf16[128,768]{1,0:T(8,128)(2,1)S(1)}, bf16[128,768]{1,0:T(8,128)(2,1)S(1)}, bf16[128,768]{1,0:T(8,128)(2,1)S(1)}, bf16[128,768]{1,0:T(8,128)(2...) custom-call(bf16[256,768]{1,0:T(8,128)(2,1)S(1)} %collective-permute, ...), custom_call_target="tpu_custom_call" | custom-call | bytes 1 | tf_op jit(solution)/shard_map/attend_back/pallas_call | solution.py:820
  83.5 3.6 %collective-permute-start.25 = (bf16[2,2,96,768]{3,2,1,0:T(8,128)(2,1)S(1)}, bf16[2,2,96,768]{3,2,1,0:T(8,128)(2,1)S(1)}, u32[]{:S(2)}, u32[]{:S(2)}) collective-permute-start(bf16[2,2,96,768]{3,2,1,0:T(8,128)(2,1)S(1)} %exchange.9.refs_7_.refs_0_), channel_id=1, source_target_pairs={{0,24},{4,28},{8,16},{12,20},{16,8},{20,12},{24,0},{28,4},{1,25},{... | collective-permute-start | bytes 1769480 | tf_op jit(solution)/shard_map/ppermute | solution.py:57
  93.6 5.2 %collective-permute-done.19.refs_1_ = bf16[4,2,24,768]{3,2,1,0:T(8,128)(2,1)S(1)} collective-permute-done((bf16[4,2,24,768]{3,2,1,0:T(8,128)(2,1)S(1)}, bf16[4,2,24,768]{3,2,1,0:T(8,128)(2,1)S(1)}, u32[]{:S(2)}, u32[]{:S(2)}) %collective-permute-start.19) | collective-permute-done | bytes 294944 | tf_op jit(solution)/shard_map/ppermute | solution.py:57
  100.2 7.9 %collective-permute-done.17.refs_2_ = bf16[256,768]{1,0:T(8,128)(2,1)S(1)} collective-permute-done((bf16[256,768]{1,0:T(8,128)(2,1)S(1)}, bf16[256,768]{1,0:T(8,128)(2,1)S(1)}, u32[]{:S(2)}, u32[]{:S(2)}) %collective-permute-start.17) | collective-permute-done | bytes 393248 | tf_op jit(solution)/shard_map/ppermute | solution.py:57
  110.1 3.5 %collective-permute-start.24 = (bf16[2,2,2,24,768]{4,3,2,1,0:T(8,128)(2,1)S(1)}, bf16[2,2,2,24,768]{4,3,2,1,0:T(8,128)(2,1)S(1)}, u32[]{:S(2)}, u32[]{:S(2)}) collective-permute-start(bf16[2,2,2,24,768]{4,3,2,1,0:T(8,128)(2,1)S(1)} %exchange.11.refs_4_.refs_0_), channel_id=1, source_target_pairs={{0,24},{4,28},{8,16},{12,20},{16,8},{20,12},{24,0},{28,4},{1,25},{... | collective-permute-start | bytes 884744 | tf_op jit(solution)/shard_map/ppermute | solution.py:57
  114.9 2.5 %collective-permute-start.30 = (bf16[2,96,768]{2,1,0:T(8,128)(2,1)S(1)}, bf16[2,96,768]{2,1,0:T(8,128)(2,1)S(1)}, u32[]{:S(2)}, u32[]{:S(2)}) collective-permute-start(bf16[2,96,768]{2,1,0:T(8,128)(2,1)S(1)} %get-tuple-element.140.refs_2_.refs_0_), channel_id=1, source_target_pairs={{0,8},{4,12},{8,0},{12,4},{16,24},{20,28},{24,16},{28,20},{1,9},{5... | collective-permute-start | bytes 884744 | tf_op jit(solution)/shard_map/ppermute | solution.py:57
  118.5 3.4 %collective-permute-done.24.refs_1_ = bf16[2,2,2,24,768]{4,3,2,1,0:T(8,128)(2,1)S(1)} collective-permute-done((bf16[2,2,2,24,768]{4,3,2,1,0:T(8,128)(2,1)S(1)}, bf16[2,2,2,24,768]{4,3,2,1,0:T(8,128)(2,1)S(1)}, u32[]{:S(2)}, u32[]{:S(2)}) %collective-permute-start.24) | collective-permute-done | bytes 294944 | tf_op jit(solution)/shard_map/ppermute | solution.py:57
  121.9 3.6 %collective-permute-start.26 = (f32[16,768]{1,0:T(8,128)S(1)}, f32[16,768]{1,0:T(8,128)S(1)}, u32[]{:S(2)}, u32[]{:S(2)}) collective-permute-start(f32[16,768]{1,0:T(8,128)S(1)} %join_sums.3.refs_0_.refs_2_), channel_id=1, source_target_pairs={{0,8},{4,12},{8,0},{12,4},{16,24},{20,28},{24,16},{28,20},{1,9},{5... | collective-permute-start | bytes 147464 | tf_op jit(solution)/shard_map/ppermute | solution.py:57
  128.2 3.0 %collective-permute-start.27 = (f32[24,768]{1,0:T(8,128)S(1)}, f32[24,768]{1,0:T(8,128)S(1)}, u32[]{:S(2)}, u32[]{:S(2)}) collective-permute-start(f32[24,768]{1,0:T(8,128)S(1)} %join_sums.4.refs_4_.refs_0_), channel_id=1, source_target_pairs={{0,16},{4,20},{8,24},{12,28},{16,0},{20,4},{24,8},{28,12},{1,17},{... | collective-permute-start | bytes 221192 | tf_op jit(solution)/shard_map/ppermute | solution.py:57
  133.3 2.4 %collective-permute-done.27.refs_1_ = f32[24,768]{1,0:T(8,128)S(1)} collective-permute-done((f32[24,768]{1,0:T(8,128)S(1)}, f32[24,768]{1,0:T(8,128)S(1)}, u32[]{:S(2)}, u32[]{:S(2)}) %collective-permute-start.27) | collective-permute-done | bytes 73760 | tf_op jit(solution)/shard_map/ppermute | solution.py:57
  146.9 4.0 %table_grad.1 = (f32[768]{0:T(1024)}, f32[768]{0:T(1024)}, f32[768]{0:T(1024)}, f32[768]{0:T(1024)}, f32[768]{0:T(1024)}, /*index=5*/f32[768]{0:T(1024)}, f32[192,1000]{1,0:T(8,128)}) custom-call(s32[152]{0:T(256)S(1)} %concatenate.3.refs_0_.ids.ids_ref, f32[40,768]{1,0:T(8,128)S(1)} %join_sums.5.refs_4_.refs_1_, ...), custom_call_target="tpu_custom_call" | custom-call | bytes 1 | tf_op jit(solution)/shard_map/table_grad/pallas_call | solution.py:962
  155.6 2.6 %collective-permute-done.35.a_ref = bf16[4,2,24,768]{3,2,1,0:T(8,128)(2,1)S(1)} collective-permute-done((bf16[4,2,24,768]{3,2,1,0:T(8,128)(2,1)S(1)}, bf16[4,2,24,768]{3,2,1,0:T(8,128)(2,1)S(1)}, u32[]{:S(2)}, u32[]{:S(2)}) %collective-permute-start.35) | collective-permute-done | bytes 294944 | tf_op jit(solution)/shard_map/ppermute | solution.py:57
  (108 shorter events, 51.5 us)
Async XLA Ops:
  13.8 20.8 %collective-permute-start.1 = (bf16[512,768]{1,0:T(8,128)(2,1)S(1)}, bf16[512,768]{1,0:T(8,128)(2,1)S(1)}, u32[]{:S(2)}, u32[]{:S(2)}) collective-permute-start(bf16[512,768]{1,0:T(8,128)(2,1)S(1)} %pair_one.1.refs_3_.refs_1_), channel_id=1, source_target_pairs={{0,2},{1,3},{2,0},{3,1},{4,6},{5,7},{6,4},{7,5},{8,10},{9,11},{10,... | collective-permute-start | bytes 2359304 | tf_op jit(solution)/shard_map/ppermute | solution.py:57
  46.7 19.9 %collective-permute-start.5 = (bf16[512,768]{1,0:T(8,128)(2,1)S(1)}, bf16[512,768]{1,0:T(8,128)(2,1)S(1)}, u32[]{:S(2)}, u32[]{:S(2)}) collective-permute-start(bf16[512,768]{1,0:T(8,128)(2,1)S(1)} %pair_two.1.refs_4_.refs_0_), channel_id=1, source_target_pairs={{0,2},{1,3},{2,0},{3,1},{4,6},{5,7},{6,4},{7,5},{8,10},{9,11},{10,... | collective-permute-start | bytes 2359304 | tf_op jit(solution)/shard_map/ppermute | solution.py:57
  48.5 20.9 %collective-permute-start.8 = (bf16[4,96,768]{2,1,0:T(8,128)(2,1)S(1)}, bf16[4,96,768]{2,1,0:T(8,128)(2,1)S(1)}, u32[]{:S(2)}, u32[]{:S(2)}) collective-permute-start(bf16[4,96,768]{2,1,0:T(8,128)(2,1)S(1)} %get-tuple-element.108), channel_id=1, source_target_pairs={{0,4},{4,0},{8,12},{12,8},{16,20},{20,16},{24,28},{28,24},{1,5},{5... | collective-permute-start | bytes 1769480 | tf_op jit(solution)/shard_map/ppermute | solution.py:57
  52.6 16.8 %collective-permute-start.9 = (bf16[4,96,768]{2,1,0:T(8,128)(2,1)S(1)}, bf16[4,96,768]{2,1,0:T(8,128)(2,1)S(1)}, u32[]{:S(2)}, u32[]{:S(2)}) collective-permute-start(bf16[4,96,768]{2,1,0:T(8,128)(2,1)S(1)} %get-tuple-element.109), channel_id=1, source_target_pairs={{0,8},{4,12},{8,0},{12,4},{16,24},{20,28},{24,16},{28,20},{1,9},{5... | collective-permute-start | bytes 1769480 | tf_op jit(solution)/shard_map/ppermute | solution.py:57
  56.3 26.6 %collective-permute-start.4 = (bf16[512,768]{1,0:T(8,128)(2,1)S(1)}, bf16[512,768]{1,0:T(8,128)(2,1)S(1)}, u32[]{:S(2)}, u32[]{:S(2)}) collective-permute-start(bf16[512,768]{1,0:T(8,128)(2,1)S(1)} %get-tuple-element.101), channel_id=1, source_target_pairs={{0,1},{1,0},{2,3},{3,2},{4,5},{5,4},{6,7},{7,6},{8,9},{9,8},{10,11... | collective-permute-start | bytes 2359304 | tf_op jit(solution)/shard_map/ppermute | solution.py:57
  69.7 11.1 %collective-permute-start.10 = (bf16[2,96,768]{2,1,0:T(8,128)(2,1)S(1)}, bf16[2,96,768]{2,1,0:T(8,128)(2,1)S(1)}, u32[]{:S(2)}, u32[]{:S(2)}) collective-permute-start(bf16[2,96,768]{2,1,0:T(8,128)(2,1)S(1)} %get-tuple-element.114), channel_id=1, source_target_pairs={{0,8},{4,12},{8,0},{12,4},{16,24},{20,28},{24,16},{28,20},{1,9},{5... | collective-permute-start | bytes 884744 | tf_op jit(solution)/shard_map/ppermute | solution.py:57
  71.6 9.4 %collective-permute-start.11 = (bf16[2,96,768]{2,1,0:T(8,128)(2,1)S(1)}, bf16[2,96,768]{2,1,0:T(8,128)(2,1)S(1)}, u32[]{:S(2)}, u32[]{:S(2)}) collective-permute-start(bf16[2,96,768]{2,1,0:T(8,128)(2,1)S(1)} %get-tuple-element.116), channel_id=1, source_target_pairs={{0,4},{4,0},{8,12},{12,8},{16,20},{20,16},{24,28},{28,24},{1,5},{5... | collective-permute-start | bytes 884744 | tf_op jit(solution)/shard_map/ppermute | solution.py:57
  83.0 9.1 %collective-permute-start.20 = (bf16[4,2,24,768]{3,2,1,0:T(8,128)(2,1)S(1)}, bf16[4,2,24,768]{3,2,1,0:T(8,128)(2,1)S(1)}, u32[]{:S(2)}, u32[]{:S(2)}) collective-permute-start(bf16[4,2,24,768]{3,2,1,0:T(8,128)(2,1)S(1)} %get-tuple-element.131), channel_id=1, source_target_pairs={{0,8},{4,12},{8,0},{12,4},{16,24},{20,28},{24,16},{28,20},{1,9},{5... | collective-permute-start | bytes 884744 | tf_op jit(solution)/shard_map/ppermute | solution.py:57
  83.5 30.1 %collective-permute-start.25 = (bf16[2,2,96,768]{3,2,1,0:T(8,128)(2,1)S(1)}, bf16[2,2,96,768]{3,2,1,0:T(8,128)(2,1)S(1)}, u32[]{:S(2)}, u32[]{:S(2)}) collective-permute-start(bf16[2,2,96,768]{3,2,1,0:T(8,128)(2,1)S(1)} %exchange.9.refs_7_.refs_0_), channel_id=1, source_target_pairs={{0,24},{4,28},{8,16},{12,20},{16,8},{20,12},{24,0},{28,4},{1,25},{... | collective-permute-start | bytes 1769480 | tf_op jit(solution)/shard_map/ppermute | solution.py:57
  87.6 12.1 %collective-permute-start.18 = (bf16[256,768]{1,0:T(8,128)(2,1)S(1)}, bf16[256,768]{1,0:T(8,128)(2,1)S(1)}, u32[]{:S(2)}, u32[]{:S(2)}) collective-permute-start(bf16[256,768]{1,0:T(8,128)(2,1)S(1)} %get-tuple-element.125.refs_1_), channel_id=1, source_target_pairs={{0,2},{1,3},{2,0},{3,1},{4,6},{5,7},{6,4},{7,5},{8,10},{9,11},{10,... | collective-permute-start | bytes 1179656 | tf_op jit(solution)/shard_map/ppermute | solution.py:57
  90.6 8.2 %collective-permute-start.19 = (bf16[4,2,24,768]{3,2,1,0:T(8,128)(2,1)S(1)}, bf16[4,2,24,768]{3,2,1,0:T(8,128)(2,1)S(1)}, u32[]{:S(2)}, u32[]{:S(2)}) collective-permute-start(bf16[4,2,24,768]{3,2,1,0:T(8,128)(2,1)S(1)} %get-tuple-element.130), channel_id=1, source_target_pairs={{0,4},{4,0},{8,12},{12,8},{16,20},{20,16},{24,28},{28,24},{1,5},{5... | collective-permute-start | bytes 884744 | tf_op jit(solution)/shard_map/ppermute | solution.py:57
  91.2 16.9 %collective-permute-start.17 = (bf16[256,768]{1,0:T(8,128)(2,1)S(1)}, bf16[256,768]{1,0:T(8,128)(2,1)S(1)}, u32[]{:S(2)}, u32[]{:S(2)}) collective-permute-start(bf16[256,768]{1,0:T(8,128)(2,1)S(1)} %get-tuple-element.124.refs_4_.refs_0_), channel_id=1, source_target_pairs={{0,2},{1,3},{2,0},{3,1},{4,6},{5,7},{6,4},{7,5},{8,10},{9,11},{10,... | collective-permute-start | bytes 1179656 | tf_op jit(solution)/shard_map/ppermute | solution.py:57
  92.0 43.6 %collective-permute-start.12 = (bf16[512,768]{1,0:T(8,128)(2,1)S(1)}, bf16[512,768]{1,0:T(8,128)(2,1)S(1)}, u32[]{:S(2)}, u32[]{:S(2)}) collective-permute-start(bf16[512,768]{1,0:T(8,128)(2,1)S(1)} %pair_out.1.refs_5_.refs_1_), channel_id=1, source_target_pairs={{0,2},{1,3},{2,0},{3,1},{4,6},{5,7},{6,4},{7,5},{8,10},{9,11},{10,... | collective-permute-start | bytes 2359304 | tf_op jit(solution)/shard_map/ppermute | solution.py:57
  98.9 11.0 %collective-permute-start.21 = (bf16[2,2,24,768]{3,2,1,0:T(8,128)(2,1)S(1)}, bf16[2,2,24,768]{3,2,1,0:T(8,128)(2,1)S(1)}, u32[]{:S(2)}, u32[]{:S(2)}) collective-permute-start(bf16[2,2,24,768]{3,2,1,0:T(8,128)(2,1)S(1)} %get-tuple-element.136), channel_id=1, source_target_pairs={{0,8},{4,12},{8,0},{12,4},{16,24},{20,28},{24,16},{28,20},{1,9},{5... | collective-permute-start | bytes 442376 | tf_op jit(solution)/shard_map/ppermute | solution.py:57
  99.7 10.3 %collective-permute-start.22 = (bf16[2,2,24,768]{3,2,1,0:T(8,128)(2,1)S(1)}, bf16[2,2,24,768]{3,2,1,0:T(8,128)(2,1)S(1)}, u32[]{:S(2)}, u32[]{:S(2)}) collective-permute-start(bf16[2,2,24,768]{3,2,1,0:T(8,128)(2,1)S(1)} %get-tuple-element.138), channel_id=1, source_target_pairs={{0,4},{4,0},{8,12},{12,8},{16,20},{20,16},{24,28},{28,24},{1,5},{5... | collective-permute-start | bytes 442376 | tf_op jit(solution)/shard_map/ppermute | solution.py:57
  110.1 11.8 %collective-permute-start.24 = (bf16[2,2,2,24,768]{4,3,2,1,0:T(8,128)(2,1)S(1)}, bf16[2,2,2,24,768]{4,3,2,1,0:T(8,128)(2,1)S(1)}, u32[]{:S(2)}, u32[]{:S(2)}) collective-permute-start(bf16[2,2,2,24,768]{4,3,2,1,0:T(8,128)(2,1)S(1)} %exchange.11.refs_4_.refs_0_), channel_id=1, source_target_pairs={{0,24},{4,28},{8,16},{12,20},{16,8},{20,12},{24,0},{28,4},{1,25},{... | collective-permute-start | bytes 884744 | tf_op jit(solution)/shard_map/ppermute | solution.py:57
  113.8 12.6 %collective-permute-start.31 = (bf16[2,96,768]{2,1,0:T(8,128)(2,1)S(1)}, bf16[2,96,768]{2,1,0:T(8,128)(2,1)S(1)}, u32[]{:S(2)}, u32[]{:S(2)}) collective-permute-start(bf16[2,96,768]{2,1,0:T(8,128)(2,1)S(1)} %get-tuple-element.143.refs_2_), channel_id=1, source_target_pairs={{0,4},{4,0},{8,12},{12,8},{16,20},{20,16},{24,28},{28,24},{1,5},{5... | collective-permute-start | bytes 884744 | tf_op jit(solution)/shard_map/ppermute | solution.py:57
  114.9 13.3 %collective-permute-start.30 = (bf16[2,96,768]{2,1,0:T(8,128)(2,1)S(1)}, bf16[2,96,768]{2,1,0:T(8,128)(2,1)S(1)}, u32[]{:S(2)}, u32[]{:S(2)}) collective-permute-start(bf16[2,96,768]{2,1,0:T(8,128)(2,1)S(1)} %get-tuple-element.140.refs_2_.refs_0_), channel_id=1, source_target_pairs={{0,8},{4,12},{8,0},{12,4},{16,24},{20,28},{24,16},{28,20},{1,9},{5... | collective-permute-start | bytes 884744 | tf_op jit(solution)/shard_map/ppermute | solution.py:57
  128.2 10.1 %collective-permute-start.33 = (bf16[512,768]{1,0:T(8,128)(2,1)S(1)}, bf16[512,768]{1,0:T(8,128)(2,1)S(1)}, u32[]{:S(2)}, u32[]{:S(2)}) collective-permute-start(bf16[512,768]{1,0:T(8,128)(2,1)S(1)} %get-tuple-element.139.refs_4_.own_ref), channel_id=1, source_target_pairs={{0,1},{1,0},{2,3},{3,2},{4,5},{5,4},{6,7},{7,6},{8,9},{9,8},{10,11... | collective-permute-start | bytes 2359304 | tf_op jit(solution)/shard_map/ppermute | solution.py:57
  128.2 7.5 %collective-permute-start.27 = (f32[24,768]{1,0:T(8,128)S(1)}, f32[24,768]{1,0:T(8,128)S(1)}, u32[]{:S(2)}, u32[]{:S(2)}) collective-permute-start(f32[24,768]{1,0:T(8,128)S(1)} %join_sums.4.refs_4_.refs_0_), channel_id=1, source_target_pairs={{0,16},{4,20},{8,24},{12,28},{16,0},{20,4},{24,8},{28,12},{1,17},{... | collective-permute-start | bytes 221192 | tf_op jit(solution)/shard_map/ppermute | solution.py:57
  136.1 16.2 %collective-permute-start.38 = (bf16[4,96,768]{2,1,0:T(8,128)(2,1)S(1)}, bf16[4,96,768]{2,1,0:T(8,128)(2,1)S(1)}, u32[]{:S(2)}, u32[]{:S(2)}) collective-permute-start(bf16[4,96,768]{2,1,0:T(8,128)(2,1)S(1)} %get-tuple-element.148.value_ref), channel_id=1, source_target_pairs={{0,8},{4,12},{8,0},{12,4},{16,24},{20,28},{24,16},{28,20},{1,9},{5... | collective-permute-start | bytes 1769480 | tf_op jit(solution)/shard_map/ppermute | solution.py:57
  136.2 17.7 %collective-permute-start.37 = (bf16[4,96,768]{2,1,0:T(8,128)(2,1)S(1)}, bf16[4,96,768]{2,1,0:T(8,128)(2,1)S(1)}, u32[]{:S(2)}, u32[]{:S(2)}) collective-permute-start(bf16[4,96,768]{2,1,0:T(8,128)(2,1)S(1)} %get-tuple-element.144.refs_4_.value_ref), channel_id=1, source_target_pairs={{0,4},{4,0},{8,12},{12,8},{16,20},{20,16},{24,28},{28,24},{1,5},{5... | collective-permute-start | bytes 1769480 | tf_op jit(solution)/shard_map/ppermute | solution.py:57
  137.3 20.9 %collective-permute-start.35 = (bf16[4,2,24,768]{3,2,1,0:T(8,128)(2,1)S(1)}, bf16[4,2,24,768]{3,2,1,0:T(8,128)(2,1)S(1)}, u32[]{:S(2)}, u32[]{:S(2)}) collective-permute-start(bf16[4,2,24,768]{3,2,1,0:T(8,128)(2,1)S(1)} %get-tuple-element.145.a_ref.refs_0_), channel_id=1, source_target_pairs={{0,4},{4,0},{8,12},{12,8},{16,20},{20,16},{24,28},{28,24},{1,5},{5... | collective-permute-start | bytes 884744 | tf_op jit(solution)/shard_map/ppermute | solution.py:57
  138.3 19.9 %collective-permute-start.36 = (bf16[4,2,24,768]{3,2,1,0:T(8,128)(2,1)S(1)}, bf16[4,2,24,768]{3,2,1,0:T(8,128)(2,1)S(1)}, u32[]{:S(2)}, u32[]{:S(2)}) collective-permute-start(bf16[4,2,24,768]{3,2,1,0:T(8,128)(2,1)S(1)} %get-tuple-element.146.b_ref), channel_id=1, source_target_pairs={{0,8},{4,12},{8,0},{12,4},{16,24},{20,28},{24,16},{28,20},{1,9},{5... | collective-permute-start | bytes 884744 | tf_op jit(solution)/shard_map/ppermute | solution.py:57
  (22 other events, 137.8 us)

commit v5 on v4

--- a/solution.py
+++ b/solution.py
@@ -331,76 +331,57 @@
     )(cot, w_down)
 
 
-def expand_kernel(half, ids, peer, own, grad_act, w_up, up_bias, send, keep, act_out, low_out, bias_out):
-    i = pl.program_id(0)
-    normed = jnp.where(i < half, peer[...], own[...])
-    pre = mm(normed, w_up[...], 1, 0) + row_vector(up_bias)
+def expand_kernel(ids, normed, grad_act, w_up, up_bias, part_out, act_out, low_out, bias_out):
+    pre = mm(normed[...], w_up[...], 1, 0) + row_vector(up_bias)
     cdf = 0.5 * (1.0 + lax.erf(pre * SQRT_HALF))
     act_out[...] = (pre * cdf).astype(BF16)
     slope = cdf + pre * (PHI_ZERO * jnp.exp(-0.5 * (pre * pre)))
     grad_pre = grad_act[...] * slope
 
-    @pl.when(i == 0)
+    @pl.when(pl.program_id(0) == 0)
     def _():
         bias_out[...] = jnp.zeros_like(bias_out)
 
     bias_out[...] += jnp.sum(grad_pre, axis=0, keepdims=True)
     low = grad_pre.astype(BF16)
     low_out[...] = low
-    part = mm(low, w_up[...], 1, 1).astype(BF16)
-
-    @pl.when(i < half)
-    def _():
-        send[...] = part
-
-    @pl.when(i >= half)
-    def _():
-        keep[...] = part
-
-
-def expand(chunk, chunks, ids, peer, own, grad_act, w_up, up_bias, after):
-    count, width = grad_act.shape[0], peer.shape[1]
+    part_out[...] = mm(low, w_up[...], 1, 1).astype(BF16)
+
+
+def expand(ids, own, normed, grad_act, w_up, up_bias, after):
+    rows, width = normed.shape
     local = w_up.shape[1]
-    blocks = count // PAIR // chunks
-    half = blocks // 2
-    rows = blocks * PAIR
-    first = lambda i, *_: (jnp.minimum(i, half - 1), 0)
-    second = lambda i, *_: (jnp.maximum(i - half, 0), 0)
-    step = lambda i, *_: (i, 0)
-    return pl.pallas_call(
-        lambda *refs: expand_kernel(half, *refs[:6], *refs[6 + len(after) :]),
+    blocks = rows // PAIR
+    side = 0 if own else 1
+    row = pl.BlockSpec((PAIR, width), lambda i, *_: (i, 0))
+    thin = pl.BlockSpec((PAIR, local), lambda i, *_: (i, 0))
+    return pl.pallas_call(
+        lambda *refs: expand_kernel(*refs[:5], *refs[5 + len(after) :]),
         grid_spec=pltpu.PrefetchScalarGridSpec(
             num_scalar_prefetch=1,
             grid=(blocks,),
             in_specs=[
-                pl.BlockSpec((PAIR, width), first),
-                pl.BlockSpec((PAIR, width), second),
-                pl.BlockSpec((PAIR, local), lambda i, ids: (block_of(i, ids, chunk, half, chunks), 0)),
+                row,
+                pl.BlockSpec((PAIR, local), lambda i, ids: ((ids[0] ^ side) * blocks + i, 0)),
                 VM, whole(up_bias),
             ]
             + [ANY] * len(after),
-            out_specs=[
-                pl.BlockSpec((PAIR, width), first),
-                pl.BlockSpec((PAIR, width), second),
-                pl.BlockSpec((PAIR, local), step),
-                pl.BlockSpec((PAIR, local), step),
-                pl.BlockSpec((1, local), lambda i, *_: (0, 0)),
-            ],
+            out_specs=[row, thin, thin, pl.BlockSpec((1, local), lambda i, *_: (0, 0))],
         ),
         out_shape=[
-            shape((rows // 2, width), BF16), shape((rows // 2, width), BF16),
-            shape((rows, local), BF16), shape((rows, local), BF16),
+            shape((rows, width), BF16), shape((rows, local), BF16), shape((rows, local), BF16),
             shape((1, local), F32),
         ],
         compiler_params=params(),
         cost_estimate=cost("expand"),
         name="expand",
-    )(ids, peer, own, grad_act, w_up, up_bias, *after)
-
-
-def contract_kernel(act, w_down, send, keep):
+    )(ids, normed, grad_act, w_up, up_bias, *after)
+
+
+def contract_kernel(a, b, w_down, send, keep):
     i = pl.program_id(0)
-    part = mm(act[...], w_down[...], 1, 0).astype(BF16)
+    act = jnp.where(i < 2, a[...], b[...])
+    part = mm(act, w_down[...], 1, 0).astype(BF16)
 
     @pl.when(i < 2)
     def _():
@@ -411,22 +392,21 @@
         keep[...] = part
 
 
-def contract_rows(act, w_down, after):
-    rows, local = act.shape
+def contract_rows(peer, own, w_down, after):
+    rows, local = peer.shape
     width = w_down.shape[1]
-    return pl.pallas_call(
-        lambda *refs: contract_kernel(*refs[:2], *refs[2 + len(after) :]),
-        grid=(rows // PAIR,),
-        in_specs=[pl.BlockSpec((PAIR, local), lambda i: (i, 0)), VM] + [ANY] * len(after),
-        out_specs=[
-            pl.BlockSpec((PAIR, width), lambda i: (jnp.minimum(i, 1), 0)),
-            pl.BlockSpec((PAIR, width), lambda i: (jnp.maximum(i - 2, 0), 0)),
-        ],
-        out_shape=[shape((rows // 2, width), BF16), shape((rows // 2, width), BF16)],
+    first = lambda i: (jnp.minimum(i, 1), 0)
+    second = lambda i: (jnp.maximum(i - 2, 0), 0)
+    return pl.pallas_call(
+        lambda *refs: contract_kernel(*refs[:3], *refs[3 + len(after) :]),
+        grid=(2 * rows // PAIR,),
+        in_specs=[pl.BlockSpec((PAIR, local), first), pl.BlockSpec((PAIR, local), second), VM] + [ANY] * len(after),
+        out_specs=[pl.BlockSpec((PAIR, width), first), pl.BlockSpec((PAIR, width), second)],
+        out_shape=[shape((rows, width), BF16), shape((rows, width), BF16)],
         compiler_params=params(),
         cost_estimate=cost("contract_rows"),
         name="contract_rows",
-    )(act, w_down, *after)
+    )(peer, own, w_down, *after)
 
 
 def weight_kernel(order, groups, ids, *refs):
@@ -882,18 +862,18 @@
     )(*pair, *other, hidden, grad_residual, gain, *after)
 
 
-def pack_sums(vec2, vec1, up, times, after):
+def pack_sums(vec2, vec1, up_a, up_b, times, after):
     pairs, _, width = times.shape
 
-    def kernel(v2, v1, u, t, out):
+    def kernel(v2, v1, ua, ub, t, out):
         out[0:3] = v2[0:3]
         out[3:5] = v1[0:2]
-        out[5:6] = u[...]
+        out[5:6] = ua[...] + ub[...]
         out[6:8] = jnp.zeros((2, width), F32)
         for n in range(pairs):
             out[8 + 2 * n : 10 + 2 * n] = t[n]
 
-    return small_call(kernel, [shape((8 + 2 * pairs, width), F32)], [vec2, vec1, up, times], after, "pack_sums")[0]
+    return small_call(kernel, [shape((8 + 2 * pairs, width), F32)], [vec2, vec1, up_a, up_b, times], after, "pack_sums")[0]
 
 
 def join_sums(a, b, after, name):
@@ -1053,7 +1033,6 @@
     peer_rows = lambda ids: 1 - ids[0]
     own_rows = lambda ids: ids[0]
     zero = lambda ids: 0
-    one = lambda ids: 1
 
     send, keep, hidden, normed, q, k, v, p, ctx = attend(
         0, 1, scalars, *[far(x) for x in (tokens, time_table, norm1_gain, norm1_bias, heads, w_out)], []
@@ -1064,12 +1043,14 @@
     grad_act = act_grad(cotangent, w_down)
     residual, own2 = mid_forward(hidden, pair, other, norm2_gain, norm2_bias, [grad_act])
     peer2 = core_swap(own2)
-    send, keep, act, low, up_sum = expand(0, 1, ids, peer2, own2, grad_act, w_up, up_bias, [])
+    keep, act_own, low_rows_own, up_own = expand(ids, True, own2, grad_act, w_up, up_bias, [])
+    send, act_peer, low_rows_peer, up_peer = expand(ids, False, peer2, grad_act, w_up, up_bias, [keep])
     got_two = core_swap(send)
     first_keep = keep
+    start = send
     cots = [(cotangent, size, f) for f in (peer_rows, own_rows)]
-    acts = [(act, size, f) for f in (zero, one)]
-    lows = [(low, size, f) for f in (zero, one)]
+    acts = [(act_peer, size, zero), (act_own, size, zero)]
+    lows = [(low_rows_peer, size, zero), (low_rows_own, size, zero)]
     norms = [(peer2, size, zero), (own2, size, zero)]
     mlp = Dual(bits, direct)
     heads_sum = Dual(bits, direct)
@@ -1092,7 +1073,7 @@
         return it.pair2
 
     def contract(after):
-        send, it.keep_e = contract_rows(act, w_down, after)
+        send, it.keep_e = contract_rows(act_peer, act_own, w_down, after)
         it.got_e = core_swap(send)
         return it.keep_e
 
@@ -1139,7 +1120,7 @@
         return it.low_in
 
     def pack(after):
-        it.sums = pack_sums(it.vec2, it.vec1, up_sum, it.times, after)
+        it.sums = pack_sums(it.vec2, it.vec1, up_own, up_peer, it.times, after)
         it.sums_got = dp_swap(it.sums, 1)
         return it.sums
 

time: 160 us -> 158 us (0.988)
  waiting for transfers between devices: 54.1 us -> 51.5 us
    ppermute x39, waiting for transfers between devices: 54.1 us -> 51.5 us  [swap(): lax.ppermute(value, axis, [(i, i ^ bit) for i in range(lax.axis_size(axis...]
    pallas_call x2 -> x3, Pallas kernels: 8.13 us -> 8.5 us  [the longest x2 6.38 us: expand(): pl.pallas_call(lambda *refs: expand_kernel(*refs[:5], *refs[5 + len(after...]
  transfers between devices with their start and end apart: 39 -> 39, of which waited for: 15 -> 14; matrix products, arithmetic and copies ran while one was open for 0% -> 0% of each run, Pallas kernels for 27% -> 29%
where the time goes in v5:
time: 158 us
  Pallas kernels  61.5 us (39%)
  waiting for transfers between devices  51.5 us (33%)
  starting transfers between devices  43 us (27%)
    ppermute x39, waiting for transfers between devices, swap(): lax.ppermute(value, axis, [(i, i ^ bit) for i in range(lax.axis_size(axis...  51.5 us
    ppermute x39, starting transfers between devices, swap(): lax.ppermute(value, axis, [(i, i ^ bit) for i in range(lax.axis_size(axis...  43 us
    pallas_call x1, Pallas kernels, attend(): pl.pallas_call(lambda *refs: attend_kernel(chunk, half, chunks, slots, *r...  9.79 us
    pallas_call x1, Pallas kernels, attend_back(): pl.pallas_call(lambda *refs: attend_back_kernel(count, blocks, *refs[:ins...  7.19 us
    pallas_call x4, Pallas kernels, place_half(): pl.pallas_call(kernel, grid_spec=pltpu.PrefetchScalarGridSpec(num_scalar_...  6.43 us
    pallas_call x2, Pallas kernels, expand(): pl.pallas_call(lambda *refs: expand_kernel(*refs[:5], *refs[5 + len(after...  6.38 us
    pallas_call x2, Pallas kernels, weight_grad(): pl.pallas_call(lambda ids, *refs: kernel(ids, *refs[:2 * total], *refs[2...  5.12 us
    pallas_call x1, Pallas kernels, table_grad(): pl.pallas_call(lambda *refs: table_kernel(slots, steps, *refs[:3], *refs[...  3.98 us
  transfers between devices with their start and end apart: 39, of which 14 were waited for; matrix products, arithmetic and copies ran while one was open for 0% of the time, Pallas kernels for 29%

profile of v5, /device:TPU:0, one launch (start us, length us, event | category | flops | bytes accessed | tf_op | source)
XLA Modules:
  0.0 158.1 jit_solution(6233703498208275463)
XLA Ops:
  1.4 9.8 %attend.1 = (bf16[512,768]{1,0:T(8,128)(2,1)S(1)}, bf16[512,768]{1,0:T(8,128)(2,1)S(1)}, f32[512,768]{1,0:T(8,128)S(1)}, bf16[1024,768]{1,0:T(8,128)(2,1)S(1)}, ...) custom-call(s32[152]{0:T(256)S(1)} %concatenate.3.refs_0_.ids.ids_re, ...), custom_call_target="tpu_custom_call" | custom-call | bytes 1 | tf_op jit(solution)/shard_map/attend/pallas_call | solution.py:255
  13.8 3.0 %collective-permute-start.1 = (bf16[512,768]{1,0:T(8,128)(2,1)S(1)}, bf16[512,768]{1,0:T(8,128)(2,1)S(1)}, u32[]{:S(2)}, u32[]{:S(2)}) collective-permute-start(bf16[512,768]{1,0:T(8,128)(2,1)S(1)} %pair_one.1.refs_3_.refs_1_), channel_id=1, source_target_pairs={{0,2},{1,3},{2,0},{3,1},{4,6},{5,7},{6,4},{7,5},{8,10},{9,11},{10,... | collective-permute-start | bytes 2359304 | tf_op jit(solution)/shard_map/ppermute | solution.py:57
  16.8 2.1 %stage.1 = (bf16[768,768]{1,0:T(8,128)(2,1)S(1)}, bf16[768,768]{1,0:T(8,128)(2,1)S(1)}, bf16[1024,768]{1,0:T(8,128)(2,1)S(1)}) custom-call(bf16[768,768]{1,0:T(8,128)(2,1)} %refs_0_.1, bf16[768,768]{1,0:T(8,128)(2,1)} %refs_1_.3, bf16[1024,768]{1,0:T(8,128)(2,1)} %refs_2_.3, bf16[512,768]{1,0:T(8,128)(2,1)S(1)} %pair_one.1.refs_3_.refs_1_), custom_call_target="tpu_custom_call" | custom-call | bytes 1 | tf_op jit(solution)/shard_map/stage/pallas_call | solution.py:150
  19.0 2.1 %act_grad.1.refs_5_.refs_2_ = f32[1024,768]{1,0:T(8,128)S(1)} custom-call(bf16[1024,768]{1,0:T(8,128)(2,1)S(1)} %get-tuple-element.92.cot_ref.refs_2_.refs_3_, bf16[768,768]{1,0:T(8,128)(2,1)S(1)} %get-tuple-element.93.w_ref.refs_2_), custom_call_target="tpu_custom_call" | custom-call | bytes 1 | tf_op jit(solution)/shard_map/act_grad/pallas_call | solution.py:322
  21.0 13.6 %collective-permute-done.1.refs_2_ = bf16[512,768]{1,0:T(8,128)(2,1)S(1)} collective-permute-done((bf16[512,768]{1,0:T(8,128)(2,1)S(1)}, bf16[512,768]{1,0:T(8,128)(2,1)S(1)}, u32[]{:S(2)}, u32[]{:S(2)}) %collective-permute-start.1) | collective-permute-done | bytes 786464 | tf_op jit(solution)/shard_map/ppermute | solution.py:57
  35.5 3.2 %expand.2 = (bf16[512,768]{1,0:T(8,128)(2,1)S(1)}, bf16[512,768]{1,0:T(8,128)(2,1)S(1)}, bf16[512,768]{1,0:T(8,128)(2,1)S(1)}, f32[1,768]{1,0:T(1,128)S(1)}) custom-call(s32[152]{0:T(256)S(1)} %concatenate.3.refs_0_.ids.ids_ref, bf16[512,768]{1,0:T(8,128)(2,1)S(1)} %get-tuple-element.95.refs_1_, f32[1024,768]{1,0:T(8,128)S(1)} %act_grad.1.refs_5_.refs_2_, ...), custom_call_target="tpu_custom_call" | custom-call | bytes 1 | tf_op jit(solution)/shard_map/expand/pallas_call | solution.py:358
  38.7 3.2 %expand.3 = (bf16[512,768]{1,0:T(8,128)(2,1)S(1)}, bf16[512,768]{1,0:T(8,128)(2,1)S(1)}, bf16[512,768]{1,0:T(8,128)(2,1)S(1)}, f32[1,768]{1,0:T(1,128)S(1)}) custom-call(s32[152]{0:T(256)S(1)} %concatenate.3.refs_0_.ids.ids_ref, bf16[512,768]{1,0:T(8,128)(2,1)S(1)} %collective-permute-done.2.refs_1_.refs_0_, f32[1024,768]{1,0:T(8,128)S(1)} %act_grad.1.refs_5_.refs_2_, ...), custom_call_target="tpu_custom_call" | custom-call | bytes 1 | tf_op jit(solution)/shard_map/expand/pallas_call | solution.py:358
  42.4 2.6 %down_grad.1 = (bf16[4,96,768]{2,1,0:T(8,128)(2,1)S(1)}, bf16[4,96,768]{2,1,0:T(8,128)(2,1)S(1)}) custom-call(s32[152]{0:T(256)S(1)} %concatenate.3.refs_0_.ids.ids_ref, bf16[512,768]{1,0:T(8,128)(2,1)S(1)} %get-tuple-element.98.refs_0_, bf16[512,768]{1,0:T(8,128)(2,1)S(1)} %get-tuple-element.99.refs_1_, ...), custom_call_target="tpu_custom_call" | custom-call | bytes 1 | tf_op jit(solution)/shard_map/down_grad/pallas_call | solution.py:464
  48.5 2.6 %up_grad.1 = (bf16[4,96,768]{2,1,0:T(8,128)(2,1)S(1)}, bf16[4,96,768]{2,1,0:T(8,128)(2,1)S(1)}) custom-call(s32[152]{0:T(256)S(1)} %concatenate.3.refs_0_.ids.ids_ref, bf16[512,768]{1,0:T(8,128)(2,1)S(1)} %collective-permute-done.2.refs_1_.refs_0_, bf16[512,768]{1,0:T(8,128)(2,1)S(1)} %get-tuple-element.95.refs_1_, ...), custom_call_target="tpu_custom_call" | custom-call | flops 1000000000 | bytes 1 | tf_op jit(solution)/shard_map/up_grad/pallas_call | solution.py:464
  52.7 2.1 %contract_rows.1 = (bf16[512,768]{1,0:T(8,128)(2,1)S(1)}, bf16[512,768]{1,0:T(8,128)(2,1)S(1)}) custom-call(bf16[512,768]{1,0:T(8,128)(2,1)S(1)} %get-tuple-element.98.refs_0_, bf16[512,768]{1,0:T(8,128)(2,1)S(1)} %get-tuple-element.99.refs_1_, bf16[768,768]{1,0:T(8,128)(2,1)S(1)} %get-tuple-element.93.w_ref.refs_2_, ...), custom_call_target="tpu_custom_call" | custom-call | bytes 1 | tf_op jit(solution)/shard_map/contract_rows/pallas_call | solution.py:400
  54.9 9.8 %collective-permute-done.5.refs_1_ = bf16[512,768]{1,0:T(8,128)(2,1)S(1)} collective-permute-done((bf16[512,768]{1,0:T(8,128)(2,1)S(1)}, bf16[512,768]{1,0:T(8,128)(2,1)S(1)}, u32[]{:S(2)}, u32[]{:S(2)}) %collective-permute-start.5) | collective-permute-done | bytes 786464 | tf_op jit(solution)/shard_map/ppermute | solution.py:57
  64.7 2.2 %mid_back.1 = (f32[512,768]{1,0:T(8,128)S(1)}, bf16[256,768]{1,0:T(8,128)(2,1)S(1)}, bf16[256,768]{1,0:T(8,128)(2,1)S(1)}, f32[8,768]{1,0:T(8,128)S(1)}) custom-call(s32[152]{0:T(256)S(1)} %concatenate.3.refs_0_.ids.ids_ref, bf16[512,768]{1,0:T(8,128)(2,1)S(1)} %pair_two.1.refs_4_.refs_0_, bf16[512,768]{1,0:T(8,128)(2,1)S(1)} %collective-permute-done.5.refs_1_, ...), custom_call_target="tpu_custom_call" | custom-call | bytes 1 | tf_op jit(solution)/shard_map/mid_back/pallas_call | solution.py:717
  71.2 7.2 %attend_back.1 = (bf16[128,768]{1,0:T(8,128)(2,1)S(1)}, bf16[128,768]{1,0:T(8,128)(2,1)S(1)}, bf16[128,768]{1,0:T(8,128)(2,1)S(1)}, bf16[128,768]{1,0:T(8,128)(2...) custom-call(bf16[256,768]{1,0:T(8,128)(2,1)S(1)} %collective-permute, ...), custom_call_target="tpu_custom_call" | custom-call | bytes 1 | tf_op jit(solution)/shard_map/attend_back/pallas_call | solution.py:800
  81.6 3.6 %collective-permute-start.25 = (bf16[2,2,96,768]{3,2,1,0:T(8,128)(2,1)S(1)}, bf16[2,2,96,768]{3,2,1,0:T(8,128)(2,1)S(1)}, u32[]{:S(2)}, u32[]{:S(2)}) collective-permute-start(bf16[2,2,96,768]{3,2,1,0:T(8,128)(2,1)S(1)} %exchange.9.refs_7_.refs_0_), channel_id=1, source_target_pairs={{0,24},{4,28},{8,16},{12,20},{16,8},{20,12},{24,0},{28,4},{1,25},{... | collective-permute-start | bytes 1769480 | tf_op jit(solution)/shard_map/ppermute | solution.py:57
  91.7 5.2 %collective-permute-done.19.refs_1_ = bf16[4,2,24,768]{3,2,1,0:T(8,128)(2,1)S(1)} collective-permute-done((bf16[4,2,24,768]{3,2,1,0:T(8,128)(2,1)S(1)}, bf16[4,2,24,768]{3,2,1,0:T(8,128)(2,1)S(1)}, u32[]{:S(2)}, u32[]{:S(2)}) %collective-permute-start.19) | collective-permute-done | bytes 294944 | tf_op jit(solution)/shard_map/ppermute | solution.py:57
  98.3 7.9 %collective-permute-done.17.refs_2_ = bf16[256,768]{1,0:T(8,128)(2,1)S(1)} collective-permute-done((bf16[256,768]{1,0:T(8,128)(2,1)S(1)}, bf16[256,768]{1,0:T(8,128)(2,1)S(1)}, u32[]{:S(2)}, u32[]{:S(2)}) %collective-permute-start.17) | collective-permute-done | bytes 393248 | tf_op jit(solution)/shard_map/ppermute | solution.py:57
  108.2 3.7 %collective-permute-start.24 = (bf16[2,2,2,24,768]{4,3,2,1,0:T(8,128)(2,1)S(1)}, bf16[2,2,2,24,768]{4,3,2,1,0:T(8,128)(2,1)S(1)}, u32[]{:S(2)}, u32[]{:S(2)}) collective-permute-start(bf16[2,2,2,24,768]{4,3,2,1,0:T(8,128)(2,1)S(1)} %exchange.11.refs_5_.refs_0_), channel_id=1, source_target_pairs={{0,24},{4,28},{8,16},{12,20},{16,8},{20,12},{24,0},{28,4},{1,25},{... | collective-permute-start | bytes 884744 | tf_op jit(solution)/shard_map/ppermute | solution.py:57
  113.0 2.4 %collective-permute-start.30 = (bf16[2,96,768]{2,1,0:T(8,128)(2,1)S(1)}, bf16[2,96,768]{2,1,0:T(8,128)(2,1)S(1)}, u32[]{:S(2)}, u32[]{:S(2)}) collective-permute-start(bf16[2,96,768]{2,1,0:T(8,128)(2,1)S(1)} %get-tuple-element.146.refs_2_.refs_0_), channel_id=1, source_target_pairs={{0,8},{4,12},{8,0},{12,4},{16,24},{20,28},{24,16},{28,20},{1,9},{5... | collective-permute-start | bytes 884744 | tf_op jit(solution)/shard_map/ppermute | solution.py:57
  116.6 3.4 %collective-permute-done.24.refs_1_ = bf16[2,2,2,24,768]{4,3,2,1,0:T(8,128)(2,1)S(1)} collective-permute-done((bf16[2,2,2,24,768]{4,3,2,1,0:T(8,128)(2,1)S(1)}, bf16[2,2,2,24,768]{4,3,2,1,0:T(8,128)(2,1)S(1)}, u32[]{:S(2)}, u32[]{:S(2)}) %collective-permute-start.24) | collective-permute-done | bytes 294944 | tf_op jit(solution)/shard_map/ppermute | solution.py:57
  120.1 3.6 %collective-permute-start.26 = (f32[16,768]{1,0:T(8,128)S(1)}, f32[16,768]{1,0:T(8,128)S(1)}, u32[]{:S(2)}, u32[]{:S(2)}) collective-permute-start(f32[16,768]{1,0:T(8,128)S(1)} %join_sums.3.refs_0_.refs_2_), channel_id=1, source_target_pairs={{0,8},{4,12},{8,0},{12,4},{16,24},{20,28},{24,16},{28,20},{1,9},{5... | collective-permute-start | bytes 147464 | tf_op jit(solution)/shard_map/ppermute | solution.py:57
  126.3 3.0 %collective-permute-start.27 = (f32[24,768]{1,0:T(8,128)S(1)}, f32[24,768]{1,0:T(8,128)S(1)}, u32[]{:S(2)}, u32[]{:S(2)}) collective-permute-start(f32[24,768]{1,0:T(8,128)S(1)} %join_sums.4.refs_4_.refs_0_), channel_id=1, source_target_pairs={{0,16},{4,20},{8,24},{12,28},{16,0},{20,4},{24,8},{28,12},{1,17},{... | collective-permute-start | bytes 221192 | tf_op jit(solution)/shard_map/ppermute | solution.py:57
  131.4 2.4 %collective-permute-done.27.refs_1_ = f32[24,768]{1,0:T(8,128)S(1)} collective-permute-done((f32[24,768]{1,0:T(8,128)S(1)}, f32[24,768]{1,0:T(8,128)S(1)}, u32[]{:S(2)}, u32[]{:S(2)}) %collective-permute-start.27) | collective-permute-done | bytes 73760 | tf_op jit(solution)/shard_map/ppermute | solution.py:57
  145.0 4.0 %table_grad.1 = (f32[768]{0:T(1024)}, f32[768]{0:T(1024)}, f32[768]{0:T(1024)}, f32[768]{0:T(1024)}, f32[768]{0:T(1024)}, /*index=5*/f32[768]{0:T(1024)}, f32[192,1000]{1,0:T(8,128)}) custom-call(s32[152]{0:T(256)S(1)} %concatenate.3.refs_0_.ids.ids_ref, f32[40,768]{1,0:T(8,128)S(1)} %join_sums.5.refs_4_.refs_1_, ...), custom_call_target="tpu_custom_call" | custom-call | bytes 1 | tf_op jit(solution)/shard_map/table_grad/pallas_call | solution.py:942
  153.7 2.6 %collective-permute-done.35.a_ref = bf16[4,2,24,768]{3,2,1,0:T(8,128)(2,1)S(1)} collective-permute-done((bf16[4,2,24,768]{3,2,1,0:T(8,128)(2,1)S(1)}, bf16[4,2,24,768]{3,2,1,0:T(8,128)(2,1)S(1)}, u32[]{:S(2)}, u32[]{:S(2)}) %collective-permute-start.35) | collective-permute-done | bytes 294944 | tf_op jit(solution)/shard_map/ppermute | solution.py:57
  (109 shorter events, 51.7 us)
Async XLA Ops:
  13.8 20.8 %collective-permute-start.1 = (bf16[512,768]{1,0:T(8,128)(2,1)S(1)}, bf16[512,768]{1,0:T(8,128)(2,1)S(1)}, u32[]{:S(2)}, u32[]{:S(2)}) collective-permute-start(bf16[512,768]{1,0:T(8,128)(2,1)S(1)} %pair_one.1.refs_3_.refs_1_), channel_id=1, source_target_pairs={{0,2},{1,3},{2,0},{3,1},{4,6},{5,7},{6,4},{7,5},{8,10},{9,11},{10,... | collective-permute-start | bytes 2359304 | tf_op jit(solution)/shard_map/ppermute | solution.py:57
  45.2 19.5 %collective-permute-start.5 = (bf16[512,768]{1,0:T(8,128)(2,1)S(1)}, bf16[512,768]{1,0:T(8,128)(2,1)S(1)}, u32[]{:S(2)}, u32[]{:S(2)}) collective-permute-start(bf16[512,768]{1,0:T(8,128)(2,1)S(1)} %pair_two.1.refs_4_.refs_0_), channel_id=1, source_target_pairs={{0,2},{1,3},{2,0},{3,1},{4,6},{5,7},{6,4},{7,5},{8,10},{9,11},{10,... | collective-permute-start | bytes 2359304 | tf_op jit(solution)/shard_map/ppermute | solution.py:57
  47.0 20.6 %collective-permute-start.8 = (bf16[4,96,768]{2,1,0:T(8,128)(2,1)S(1)}, bf16[4,96,768]{2,1,0:T(8,128)(2,1)S(1)}, u32[]{:S(2)}, u32[]{:S(2)}) collective-permute-start(bf16[4,96,768]{2,1,0:T(8,128)(2,1)S(1)} %get-tuple-element.113), channel_id=1, source_target_pairs={{0,4},{4,0},{8,12},{12,8},{16,20},{20,16},{24,28},{28,24},{1,5},{5... | collective-permute-start | bytes 1769480 | tf_op jit(solution)/shard_map/ppermute | solution.py:57
  51.1 16.5 %collective-permute-start.9 = (bf16[4,96,768]{2,1,0:T(8,128)(2,1)S(1)}, bf16[4,96,768]{2,1,0:T(8,128)(2,1)S(1)}, u32[]{:S(2)}, u32[]{:S(2)}) collective-permute-start(bf16[4,96,768]{2,1,0:T(8,128)(2,1)S(1)} %get-tuple-element.114), channel_id=1, source_target_pairs={{0,8},{4,12},{8,0},{12,4},{16,24},{20,28},{24,16},{28,20},{1,9},{5... | collective-permute-start | bytes 1769480 | tf_op jit(solution)/shard_map/ppermute | solution.py:57
  54.8 26.3 %collective-permute-start.4 = (bf16[512,768]{1,0:T(8,128)(2,1)S(1)}, bf16[512,768]{1,0:T(8,128)(2,1)S(1)}, u32[]{:S(2)}, u32[]{:S(2)}) collective-permute-start(bf16[512,768]{1,0:T(8,128)(2,1)S(1)} %get-tuple-element.106), channel_id=1, source_target_pairs={{0,1},{1,0},{2,3},{3,2},{4,5},{5,4},{6,7},{7,6},{8,9},{9,8},{10,11... | collective-permute-start | bytes 2359304 | tf_op jit(solution)/shard_map/ppermute | solution.py:57
  67.8 11.1 %collective-permute-start.10 = (bf16[2,96,768]{2,1,0:T(8,128)(2,1)S(1)}, bf16[2,96,768]{2,1,0:T(8,128)(2,1)S(1)}, u32[]{:S(2)}, u32[]{:S(2)}) collective-permute-start(bf16[2,96,768]{2,1,0:T(8,128)(2,1)S(1)} %get-tuple-element.119), channel_id=1, source_target_pairs={{0,8},{4,12},{8,0},{12,4},{16,24},{20,28},{24,16},{28,20},{1,9},{5... | collective-permute-start | bytes 884744 | tf_op jit(solution)/shard_map/ppermute | solution.py:57
  69.7 9.4 %collective-permute-start.11 = (bf16[2,96,768]{2,1,0:T(8,128)(2,1)S(1)}, bf16[2,96,768]{2,1,0:T(8,128)(2,1)S(1)}, u32[]{:S(2)}, u32[]{:S(2)}) collective-permute-start(bf16[2,96,768]{2,1,0:T(8,128)(2,1)S(1)} %get-tuple-element.121), channel_id=1, source_target_pairs={{0,4},{4,0},{8,12},{12,8},{16,20},{20,16},{24,28},{28,24},{1,5},{5... | collective-permute-start | bytes 884744 | tf_op jit(solution)/shard_map/ppermute | solution.py:57
  81.1 9.1 %collective-permute-start.20 = (bf16[4,2,24,768]{3,2,1,0:T(8,128)(2,1)S(1)}, bf16[4,2,24,768]{3,2,1,0:T(8,128)(2,1)S(1)}, u32[]{:S(2)}, u32[]{:S(2)}) collective-permute-start(bf16[4,2,24,768]{3,2,1,0:T(8,128)(2,1)S(1)} %get-tuple-element.136), channel_id=1, source_target_pairs={{0,8},{4,12},{8,0},{12,4},{16,24},{20,28},{24,16},{28,20},{1,9},{5... | collective-permute-start | bytes 884744 | tf_op jit(solution)/shard_map/ppermute | solution.py:57
  81.6 30.2 %collective-permute-start.25 = (bf16[2,2,96,768]{3,2,1,0:T(8,128)(2,1)S(1)}, bf16[2,2,96,768]{3,2,1,0:T(8,128)(2,1)S(1)}, u32[]{:S(2)}, u32[]{:S(2)}) collective-permute-start(bf16[2,2,96,768]{3,2,1,0:T(8,128)(2,1)S(1)} %exchange.9.refs_7_.refs_0_), channel_id=1, source_target_pairs={{0,24},{4,28},{8,16},{12,20},{16,8},{20,12},{24,0},{28,4},{1,25},{... | collective-permute-start | bytes 1769480 | tf_op jit(solution)/shard_map/ppermute | solution.py:57
  85.6 12.1 %collective-permute-start.18 = (bf16[256,768]{1,0:T(8,128)(2,1)S(1)}, bf16[256,768]{1,0:T(8,128)(2,1)S(1)}, u32[]{:S(2)}, u32[]{:S(2)}) collective-permute-start(bf16[256,768]{1,0:T(8,128)(2,1)S(1)} %get-tuple-element.130.refs_1_), channel_id=1, source_target_pairs={{0,2},{1,3},{2,0},{3,1},{4,6},{5,7},{6,4},{7,5},{8,10},{9,11},{10,... | collective-permute-start | bytes 1179656 | tf_op jit(solution)/shard_map/ppermute | solution.py:57
  88.7 8.2 %collective-permute-start.19 = (bf16[4,2,24,768]{3,2,1,0:T(8,128)(2,1)S(1)}, bf16[4,2,24,768]{3,2,1,0:T(8,128)(2,1)S(1)}, u32[]{:S(2)}, u32[]{:S(2)}) collective-permute-start(bf16[4,2,24,768]{3,2,1,0:T(8,128)(2,1)S(1)} %get-tuple-element.135), channel_id=1, source_target_pairs={{0,4},{4,0},{8,12},{12,8},{16,20},{20,16},{24,28},{28,24},{1,5},{5... | collective-permute-start | bytes 884744 | tf_op jit(solution)/shard_map/ppermute | solution.py:57
  89.3 16.9 %collective-permute-start.17 = (bf16[256,768]{1,0:T(8,128)(2,1)S(1)}, bf16[256,768]{1,0:T(8,128)(2,1)S(1)}, u32[]{:S(2)}, u32[]{:S(2)}) collective-permute-start(bf16[256,768]{1,0:T(8,128)(2,1)S(1)} %get-tuple-element.129.refs_4_.refs_0_), channel_id=1, source_target_pairs={{0,2},{1,3},{2,0},{3,1},{4,6},{5,7},{6,4},{7,5},{8,10},{9,11},{10,... | collective-permute-start | bytes 1179656 | tf_op jit(solution)/shard_map/ppermute | solution.py:57
  90.2 43.6 %collective-permute-start.12 = (bf16[512,768]{1,0:T(8,128)(2,1)S(1)}, bf16[512,768]{1,0:T(8,128)(2,1)S(1)}, u32[]{:S(2)}, u32[]{:S(2)}) collective-permute-start(bf16[512,768]{1,0:T(8,128)(2,1)S(1)} %pair_out.1.refs_5_.refs_1_), channel_id=1, source_target_pairs={{0,2},{1,3},{2,0},{3,1},{4,6},{5,7},{6,4},{7,5},{8,10},{9,11},{10,... | collective-permute-start | bytes 2359304 | tf_op jit(solution)/shard_map/ppermute | solution.py:57
  97.0 11.1 %collective-permute-start.21 = (bf16[2,2,24,768]{3,2,1,0:T(8,128)(2,1)S(1)}, bf16[2,2,24,768]{3,2,1,0:T(8,128)(2,1)S(1)}, u32[]{:S(2)}, u32[]{:S(2)}) collective-permute-start(bf16[2,2,24,768]{3,2,1,0:T(8,128)(2,1)S(1)} %get-tuple-element.142), channel_id=1, source_target_pairs={{0,8},{4,12},{8,0},{12,4},{16,24},{20,28},{24,16},{28,20},{1,9},{5... | collective-permute-start | bytes 442376 | tf_op jit(solution)/shard_map/ppermute | solution.py:57
  97.8 10.3 %collective-permute-start.22 = (bf16[2,2,24,768]{3,2,1,0:T(8,128)(2,1)S(1)}, bf16[2,2,24,768]{3,2,1,0:T(8,128)(2,1)S(1)}, u32[]{:S(2)}, u32[]{:S(2)}) collective-permute-start(bf16[2,2,24,768]{3,2,1,0:T(8,128)(2,1)S(1)} %get-tuple-element.144), channel_id=1, source_target_pairs={{0,4},{4,0},{8,12},{12,8},{16,20},{20,16},{24,28},{28,24},{1,5},{5... | collective-permute-start | bytes 442376 | tf_op jit(solution)/shard_map/ppermute | solution.py:57
  108.2 11.8 %collective-permute-start.24 = (bf16[2,2,2,24,768]{4,3,2,1,0:T(8,128)(2,1)S(1)}, bf16[2,2,2,24,768]{4,3,2,1,0:T(8,128)(2,1)S(1)}, u32[]{:S(2)}, u32[]{:S(2)}) collective-permute-start(bf16[2,2,2,24,768]{4,3,2,1,0:T(8,128)(2,1)S(1)} %exchange.11.refs_5_.refs_0_), channel_id=1, source_target_pairs={{0,24},{4,28},{8,16},{12,20},{16,8},{20,12},{24,0},{28,4},{1,25},{... | collective-permute-start | bytes 884744 | tf_op jit(solution)/shard_map/ppermute | solution.py:57
  112.0 12.5 %collective-permute-start.31 = (bf16[2,96,768]{2,1,0:T(8,128)(2,1)S(1)}, bf16[2,96,768]{2,1,0:T(8,128)(2,1)S(1)}, u32[]{:S(2)}, u32[]{:S(2)}) collective-permute-start(bf16[2,96,768]{2,1,0:T(8,128)(2,1)S(1)} %get-tuple-element.149.refs_2_), channel_id=1, source_target_pairs={{0,4},{4,0},{8,12},{12,8},{16,20},{20,16},{24,28},{28,24},{1,5},{5... | collective-permute-start | bytes 884744 | tf_op jit(solution)/shard_map/ppermute | solution.py:57
  113.0 13.3 %collective-permute-start.30 = (bf16[2,96,768]{2,1,0:T(8,128)(2,1)S(1)}, bf16[2,96,768]{2,1,0:T(8,128)(2,1)S(1)}, u32[]{:S(2)}, u32[]{:S(2)}) collective-permute-start(bf16[2,96,768]{2,1,0:T(8,128)(2,1)S(1)} %get-tuple-element.146.refs_2_.refs_0_), channel_id=1, source_target_pairs={{0,8},{4,12},{8,0},{12,4},{16,24},{20,28},{24,16},{28,20},{1,9},{5... | collective-permute-start | bytes 884744 | tf_op jit(solution)/shard_map/ppermute | solution.py:57
  126.3 10.1 %collective-permute-start.33 = (bf16[512,768]{1,0:T(8,128)(2,1)S(1)}, bf16[512,768]{1,0:T(8,128)(2,1)S(1)}, u32[]{:S(2)}, u32[]{:S(2)}) collective-permute-start(bf16[512,768]{1,0:T(8,128)(2,1)S(1)} %get-tuple-element.145.refs_4_.own_ref), channel_id=1, source_target_pairs={{0,1},{1,0},{2,3},{3,2},{4,5},{5,4},{6,7},{7,6},{8,9},{9,8},{10,11... | collective-permute-start | bytes 2359304 | tf_op jit(solution)/shard_map/ppermute | solution.py:57
  126.3 7.5 %collective-permute-start.27 = (f32[24,768]{1,0:T(8,128)S(1)}, f32[24,768]{1,0:T(8,128)S(1)}, u32[]{:S(2)}, u32[]{:S(2)}) collective-permute-start(f32[24,768]{1,0:T(8,128)S(1)} %join_sums.4.refs_4_.refs_0_), channel_id=1, source_target_pairs={{0,16},{4,20},{8,24},{12,28},{16,0},{20,4},{24,8},{28,12},{1,17},{... | collective-permute-start | bytes 221192 | tf_op jit(solution)/shard_map/ppermute | solution.py:57
  134.2 16.2 %collective-permute-start.38 = (bf16[4,96,768]{2,1,0:T(8,128)(2,1)S(1)}, bf16[4,96,768]{2,1,0:T(8,128)(2,1)S(1)}, u32[]{:S(2)}, u32[]{:S(2)}) collective-permute-start(bf16[4,96,768]{2,1,0:T(8,128)(2,1)S(1)} %get-tuple-element.154.value_ref), channel_id=1, source_target_pairs={{0,8},{4,12},{8,0},{12,4},{16,24},{20,28},{24,16},{28,20},{1,9},{5... | collective-permute-start | bytes 1769480 | tf_op jit(solution)/shard_map/ppermute | solution.py:57
  134.3 17.7 %collective-permute-start.37 = (bf16[4,96,768]{2,1,0:T(8,128)(2,1)S(1)}, bf16[4,96,768]{2,1,0:T(8,128)(2,1)S(1)}, u32[]{:S(2)}, u32[]{:S(2)}) collective-permute-start(bf16[4,96,768]{2,1,0:T(8,128)(2,1)S(1)} %get-tuple-element.150.refs_4_.value_ref), channel_id=1, source_target_pairs={{0,4},{4,0},{8,12},{12,8},{16,20},{20,16},{24,28},{28,24},{1,5},{5... | collective-permute-start | bytes 1769480 | tf_op jit(solution)/shard_map/ppermute | solution.py:57
  135.4 20.9 %collective-permute-start.35 = (bf16[4,2,24,768]{3,2,1,0:T(8,128)(2,1)S(1)}, bf16[4,2,24,768]{3,2,1,0:T(8,128)(2,1)S(1)}, u32[]{:S(2)}, u32[]{:S(2)}) collective-permute-start(bf16[4,2,24,768]{3,2,1,0:T(8,128)(2,1)S(1)} %get-tuple-element.151.a_ref.refs_0_), channel_id=1, source_target_pairs={{0,4},{4,0},{8,12},{12,8},{16,20},{20,16},{24,28},{28,24},{1,5},{5... | collective-permute-start | bytes 884744 | tf_op jit(solution)/shard_map/ppermute | solution.py:57
  136.4 19.9 %collective-permute-start.36 = (bf16[4,2,24,768]{3,2,1,0:T(8,128)(2,1)S(1)}, bf16[4,2,24,768]{3,2,1,0:T(8,128)(2,1)S(1)}, u32[]{:S(2)}, u32[]{:S(2)}) collective-permute-start(bf16[4,2,24,768]{3,2,1,0:T(8,128)(2,1)S(1)} %get-tuple-element.152.b_ref), channel_id=1, source_target_pairs={{0,8},{4,12},{8,0},{12,4},{16,24},{20,28},{24,16},{28,20},{1,9},{5... | collective-permute-start | bytes 884744 | tf_op jit(solution)/shard_map/ppermute | solution.py:57
  (22 other events, 136.7 us)

commit v6 on v5

--- a/solution.py
+++ b/solution.py
@@ -101,8 +101,8 @@
         hit = (row_group(r) == group) & (row_length(r) <= SHORT)
         return pos + jnp.where(hit, 1, 0)
 
-    long_slots = lax.fori_loop(0, rows, long_row, 0)
-    lax.fori_loop(0, rows, short_row, long_slots)
+    long_slots = lax.fori_loop(0, rows, long_row, 0, unroll=8)
+    lax.fori_loop(0, rows, short_row, long_slots, unroll=8)
     return long_slots
 
 
@@ -681,11 +681,31 @@
     )
 
 
-def mid_back_kernel(pair, other, residual, cot, gain, grad_out, *refs):
+def units(values, after):
+    rows, width = values.shape
+    row = pl.BlockSpec((PAIR, width), lambda i: (i, 0))
+
+    def kernel(value_ref, *refs):
+        unit_out, scale_out = refs[len(after) :]
+        unit_out[...], scale_out[...] = norm_stats(value_ref[...])
+
+    return pl.pallas_call(
+        kernel,
+        grid=(rows // PAIR,),
+        in_specs=[row] + [ANY] * len(after),
+        out_specs=[row, pl.BlockSpec((PAIR, 1), lambda i: (i, 0))],
+        out_shape=[shape((rows, width), F32), shape((rows, 1), F32)],
+        compiler_params=params(),
+        cost_estimate=cost("units"),
+        name="units",
+    )(values, *after)
+
+
+def mid_back_kernel(pair, other, unit_ref, scale_ref, cot, gain, grad_out, *refs):
     low_out, sums = refs[:-1], refs[-1]
     i = pl.program_id(0)
     err = pair[...].astype(F32) + other[...].astype(F32)
-    unit, scale = norm_stats(residual[...])
+    unit, scale = unit_ref[...], scale_ref[...]
     top = cot[...].astype(F32)
     f = err * row_vector(gain)
     f_mean = jnp.mean(f, axis=-1, keepdims=True)
@@ -710,17 +730,17 @@
     sums[2:3] += jnp.sum(top, axis=0, keepdims=True)
 
 
-def mid_back(chunk, chunks, ids, pair, other, residual, cot, gain, pieces, after):
-    rows, width = residual.shape
+def mid_back(chunk, chunks, ids, pair, other, unit, scale, cot, gain, pieces, after):
+    rows, width = unit.shape
     half = rows // PAIR
     row = pl.BlockSpec((PAIR, width), lambda i, ids: (i, 0))
     return pl.pallas_call(
-        lambda ids, *refs: mid_back_kernel(*refs[:5], *refs[5 + len(after) :]),
+        lambda ids, *refs: mid_back_kernel(*refs[:6], *refs[6 + len(after) :]),
         grid_spec=pltpu.PrefetchScalarGridSpec(
             num_scalar_prefetch=1,
             grid=(half,),
             in_specs=[
-                row, row, row,
+                row, row, row, pl.BlockSpec((PAIR, 1), lambda i, ids: (i, 0)),
                 pl.BlockSpec((PAIR, width), lambda i, ids: (block_of(i + half, ids, chunk, half, chunks), 0)),
                 whole(gain),
             ]
@@ -731,7 +751,7 @@
         compiler_params=params(),
         cost_estimate=cost("mid_back"),
         name="mid_back",
-    )(ids, pair, other, residual, cot, gain, *after)
+    )(ids, pair, other, unit, scale, cot, gain, *after)
 
 
 def attend_back_kernel(count, blocks, *refs):
@@ -820,12 +840,12 @@
 
 def last_kernel(count, *refs):
     pairs, others = refs[:count], refs[count : 2 * count]
-    hidden, grad_residual, gain, low_out, sums, times = refs[2 * count :]
+    unit_ref, scale_ref, grad_residual, gain, low_out, sums, times = refs[2 * count :]
     i = pl.program_id(0)
     pair = jnp.where(i == 0, pairs[0][...], pairs[1][...])
     other = jnp.where(i == 0, others[0][...], others[1][...])
     err = pair.astype(F32) + other.astype(F32)
-    unit, scale = norm_stats(hidden[...])
+    unit, scale = unit_ref[...], scale_ref[...]
     f = err * row_vector(gain)
     f_mean = jnp.mean(f, axis=-1, keepdims=True)
     fx_mean = jnp.mean(f * unit, axis=-1, keepdims=True)
@@ -842,14 +862,14 @@
     times[0, 1:2] = jnp.sum(grad[SHORT:], axis=0, keepdims=True)
 
 
-def last_back(pair, other, hidden, grad_residual, gain, after):
-    rows, width = hidden.shape
+def last_back(pair, other, unit, scale, grad_residual, gain, after):
+    rows, width = unit.shape
     half = rows // PAIR
     row = pl.BlockSpec((PAIR, width), lambda i: (i, 0))
     return pl.pallas_call(
-        lambda *refs: last_kernel(2, *refs[:7], *refs[7 + len(after) :]),
+        lambda *refs: last_kernel(2, *refs[:8], *refs[8 + len(after) :]),
         grid=(half,),
-        in_specs=[VM] * 4 + [row, row, whole(gain)] + [ANY] * len(after),
+        in_specs=[VM] * 4 + [row, pl.BlockSpec((PAIR, 1), lambda i: (i, 0)), row, whole(gain)] + [ANY] * len(after),
         out_specs=[
             row,
             pl.BlockSpec((8, width), lambda i: (0, 0)),
@@ -859,7 +879,7 @@
         compiler_params=params(),
         cost_estimate=cost("last_back"),
         name="last_back",
-    )(*pair, *other, hidden, grad_residual, gain, *after)
+    )(*pair, *other, unit, scale, grad_residual, gain, *after)
 
 
 def pack_sums(vec2, vec1, up_a, up_b, times, after):
@@ -1041,7 +1061,8 @@
     other = chip_swap(pair)
     w_up, w_down, cotangent = stage([far(x) for x in (w_up, w_down, cotangent)], [pair])
     grad_act = act_grad(cotangent, w_down)
-    residual, own2 = mid_forward(hidden, pair, other, norm2_gain, norm2_bias, [grad_act])
+    unit1, scale1 = units(hidden, [grad_act])
+    residual, own2 = mid_forward(hidden, pair, other, norm2_gain, norm2_bias, [unit1])
     peer2 = core_swap(own2)
     keep, act_own, low_rows_own, up_own = expand(ids, True, own2, grad_act, w_up, up_bias, [])
     send, act_peer, low_rows_peer, up_peer = expand(ids, False, peer2, grad_act, w_up, up_bias, [keep])
@@ -1075,11 +1096,12 @@
     def contract(after):
         send, it.keep_e = contract_rows(act_peer, act_own, w_down, after)
         it.got_e = core_swap(send)
-        return it.keep_e
+        it.unit2, it.scale2 = units(residual, [it.keep_e])
+        return it.unit2
 
     def mid(after):
         it.grad_res, *it.low_own, it.vec2 = mid_back(
-            0, 1, ids, it.pair2, it.other2, residual, cotangent, norm2_gain, LOW_PIECES, after
+            0, 1, ids, it.pair2, it.other2, it.unit2, it.scale2, cotangent, norm2_gain, LOW_PIECES, after
         )
         it.low_peer = [core_swap(x) for x in it.low_own]
         return it.low_own[0]
@@ -1114,7 +1136,7 @@
 
     def last(after):
         it.low_in, it.vec1, it.times = last_back(
-            it.pair3, it.other3, hidden, it.grad_res, norm1_gain, after
+            it.pair3, it.other3, unit1, scale1, it.grad_res, norm1_gain, after
         )
         it.low_got = core_swap(it.low_in)
         return it.low_in
@@ -1181,9 +1203,8 @@
     order = (
         down_grad, pair_two, up_grad, contract, mid, sum_step(mlp), attend_grad, sum_step(mlp), vo_grad,
         pair_out, pair_three, qk_grad, sum_step(heads_sum), last, sum_step(heads_sum), pack, sum_step(mlp),
-        sum_step(heads_sum), join(0), join(1), sum_step(mlp), sum_step(heads_sum), place_attn(0), join(2),
-        final, place(0, 0), place(1, 0), input_rows, output_rows, table, place(1, 1), place(0, 1),
-        place_attn(1),
+        sum_step(heads_sum), join(0), join(1), sum_step(mlp), sum_step(heads_sum), place(1, 0), place_attn(0),
+        join(2), final, place(0, 0), input_rows, output_rows, table, place(1, 1), place(0, 1), place_attn(1),
     )
     mark = first_keep
     for step in order:

time: 158 us -> 158 us (level)
    pallas_call x2 -> x4, Pallas kernels: 3.86 us -> 4.73 us  [the longest x1 2.05 us: mid_back(): pl.pallas_call(lambda ids, *refs: mid_back_kernel(*refs[:6], *refs[6 + le...]
  transfers between devices with their start and end apart: 39 -> 39, of which waited for: 14 -> 14; matrix products, arithmetic and copies ran while one was open for 0% -> 0% of each run, Pallas kernels for 29% -> 30%
where the time goes in v6:
time: 158 us
  Pallas kernels  62.6 us (40%)
  waiting for transfers between devices  50.4 us (32%)
  starting transfers between devices  43 us (27%)
    ppermute x39, waiting for transfers between devices, swap(): lax.ppermute(value, axis, [(i, i ^ bit) for i in range(lax.axis_size(axis...  50.4 us
    ppermute x39, starting transfers between devices, swap(): lax.ppermute(value, axis, [(i, i ^ bit) for i in range(lax.axis_size(axis...  43 us
    pallas_call x1, Pallas kernels, attend(): pl.pallas_call(lambda *refs: attend_kernel(chunk, half, chunks, slots, *r...  9.79 us
    pallas_call x1, Pallas kernels, attend_back(): pl.pallas_call(lambda *refs: attend_back_kernel(count, blocks, *refs[:ins...  7.19 us
    pallas_call x4, Pallas kernels, place_half(): pl.pallas_call(kernel, grid_spec=pltpu.PrefetchScalarGridSpec(num_scalar_...  6.43 us
    pallas_call x2, Pallas kernels, expand(): pl.pallas_call(lambda *refs: expand_kernel(*refs[:5], *refs[5 + len(after...  6.42 us
    pallas_call x2, Pallas kernels, weight_grad(): pl.pallas_call(lambda ids, *refs: kernel(ids, *refs[:2 * total], *refs[2...  5.1 us
    pallas_call x1, Pallas kernels, table_grad(): pl.pallas_call(lambda *refs: table_kernel(slots, steps, *refs[:3], *refs[...  3.98 us
  transfers between devices with their start and end apart: 39, of which 14 were waited for; matrix products, arithmetic and copies ran while one was open for 0% of the time, Pallas kernels for 30%

profile of v6, /device:TPU:0, one launch (start us, length us, event | category | flops | bytes accessed | tf_op | source)
XLA Modules:
  0.0 158.1 jit_solution(5655544792752078915)
XLA Ops:
  1.4 9.8 %attend.1 = (bf16[512,768]{1,0:T(8,128)(2,1)S(1)}, bf16[512,768]{1,0:T(8,128)(2,1)S(1)}, f32[512,768]{1,0:T(8,128)S(1)}, bf16[1024,768]{1,0:T(8,128)(2,1)S(1)}, ...) custom-call(s32[152]{0:T(256)S(1)} %concatenate.3.refs_0_.ids.ids_re, ...), custom_call_target="tpu_custom_call" | custom-call | bytes 1 | tf_op jit(solution)/shard_map/attend/pallas_call | solution.py:255
  13.8 3.0 %collective-permute-start.1 = (bf16[512,768]{1,0:T(8,128)(2,1)S(1)}, bf16[512,768]{1,0:T(8,128)(2,1)S(1)}, u32[]{:S(2)}, u32[]{:S(2)}) collective-permute-start(bf16[512,768]{1,0:T(8,128)(2,1)S(1)} %pair_one.1.refs_3_.refs_1_), channel_id=1, source_target_pairs={{0,2},{1,3},{2,0},{3,1},{4,6},{5,7},{6,4},{7,5},{8,10},{9,11},{10,... | collective-permute-start | bytes 2359304 | tf_op jit(solution)/shard_map/ppermute | solution.py:57
  16.8 2.1 %stage.1 = (bf16[768,768]{1,0:T(8,128)(2,1)S(1)}, bf16[768,768]{1,0:T(8,128)(2,1)S(1)}, bf16[1024,768]{1,0:T(8,128)(2,1)S(1)}) custom-call(bf16[768,768]{1,0:T(8,128)(2,1)} %refs_0_.1, bf16[768,768]{1,0:T(8,128)(2,1)} %refs_1_.3, bf16[1024,768]{1,0:T(8,128)(2,1)} %refs_2_.3, bf16[512,768]{1,0:T(8,128)(2,1)S(1)} %pair_one.1.refs_3_.refs_1_), custom_call_target="tpu_custom_call" | custom-call | bytes 1 | tf_op jit(solution)/shard_map/stage/pallas_call | solution.py:150
  18.9 2.1 %act_grad.1.refs_0_.refs_2_ = f32[1024,768]{1,0:T(8,128)S(1)} custom-call(bf16[1024,768]{1,0:T(8,128)(2,1)S(1)} %get-tuple-element.96.cot_ref.refs_2_.refs_3_.refs_4_, bf16[768,768]{1,0:T(8,128)(2,1)S(1)} %get-tuple-element.97.w_ref.refs_2_), custom_call_target="tpu_custom_call" | custom-call | bytes 1 | tf_op jit(solution)/shard_map/act_grad/pallas_call | solution.py:322
  21.6 13.0 %collective-permute-done.1.refs_2_ = bf16[512,768]{1,0:T(8,128)(2,1)S(1)} collective-permute-done((bf16[512,768]{1,0:T(8,128)(2,1)S(1)}, bf16[512,768]{1,0:T(8,128)(2,1)S(1)}, u32[]{:S(2)}, u32[]{:S(2)}) %collective-permute-start.1) | collective-permute-done | bytes 786464 | tf_op jit(solution)/shard_map/ppermute | solution.py:57
  35.5 3.2 %expand.2 = (bf16[512,768]{1,0:T(8,128)(2,1)S(1)}, bf16[512,768]{1,0:T(8,128)(2,1)S(1)}, bf16[512,768]{1,0:T(8,128)(2,1)S(1)}, f32[1,768]{1,0:T(1,128)S(1)}) custom-call(s32[152]{0:T(256)S(1)} %concatenate.3.refs_0_.ids.ids_ref, bf16[512,768]{1,0:T(8,128)(2,1)S(1)} %get-tuple-element.100.refs_1_, f32[1024,768]{1,0:T(8,128)S(1)} %act_grad.1.refs_0_.refs_2_, ...), custom_call_target="tpu_custom_call" | custom-call | bytes 1 | tf_op jit(solution)/shard_map/expand/pallas_call | solution.py:358
  38.7 3.2 %expand.3 = (bf16[512,768]{1,0:T(8,128)(2,1)S(1)}, bf16[512,768]{1,0:T(8,128)(2,1)S(1)}, bf16[512,768]{1,0:T(8,128)(2,1)S(1)}, f32[1,768]{1,0:T(1,128)S(1)}) custom-call(s32[152]{0:T(256)S(1)} %concatenate.3.refs_0_.ids.ids_ref, bf16[512,768]{1,0:T(8,128)(2,1)S(1)} %collective-permute-done.2.refs_1_.refs_0_, f32[1024,768]{1,0:T(8,128)S(1)} %act_grad.1.refs_0_.refs_2_, ...), custom_call_target="tpu_custom_call" | custom-call | bytes 1 | tf_op jit(solution)/shard_map/expand/pallas_call | solution.py:358
  42.5 2.5 %down_grad.1 = (bf16[4,96,768]{2,1,0:T(8,128)(2,1)S(1)}, bf16[4,96,768]{2,1,0:T(8,128)(2,1)S(1)}) custom-call(s32[152]{0:T(256)S(1)} %concatenate.3.refs_0_.ids.ids_ref, bf16[512,768]{1,0:T(8,128)(2,1)S(1)} %get-tuple-element.103.refs_0_, bf16[512,768]{1,0:T(8,128)(2,1)S(1)} %get-tuple-element.104.refs_1_, ...), custom_call_target="tpu_custom_call" | custom-call | bytes 1 | tf_op jit(solution)/shard_map/down_grad/pallas_call | solution.py:464
  48.5 2.6 %up_grad.1 = (bf16[4,96,768]{2,1,0:T(8,128)(2,1)S(1)}, bf16[4,96,768]{2,1,0:T(8,128)(2,1)S(1)}) custom-call(s32[152]{0:T(256)S(1)} %concatenate.3.refs_0_.ids.ids_ref, bf16[512,768]{1,0:T(8,128)(2,1)S(1)} %collective-permute-done.2.refs_1_.refs_0_, bf16[512,768]{1,0:T(8,128)(2,1)S(1)} %get-tuple-element.100.refs_1_, ...), custom_call_target="tpu_custom_call" | custom-call | flops 1000000000 | bytes 1 | tf_op jit(solution)/shard_map/up_grad/pallas_call | solution.py:464
  52.8 2.2 %contract_rows.1 = (bf16[512,768]{1,0:T(8,128)(2,1)S(1)}, bf16[512,768]{1,0:T(8,128)(2,1)S(1)}) custom-call(bf16[512,768]{1,0:T(8,128)(2,1)S(1)} %get-tuple-element.103.refs_0_, bf16[512,768]{1,0:T(8,128)(2,1)S(1)} %get-tuple-element.104.refs_1_, bf16[768,768]{1,0:T(8,128)(2,1)S(1)} %get-tuple-element.97.w_ref.refs_2_, ...), custom_call_target="tpu_custom_call" | custom-call | bytes 1 | tf_op jit(solution)/shard_map/contract_rows/pallas_call | solution.py:400
  55.6 9.2 %collective-permute-done.5.refs_1_ = bf16[512,768]{1,0:T(8,128)(2,1)S(1)} collective-permute-done((bf16[512,768]{1,0:T(8,128)(2,1)S(1)}, bf16[512,768]{1,0:T(8,128)(2,1)S(1)}, u32[]{:S(2)}, u32[]{:S(2)}) %collective-permute-start.5) | collective-permute-done | bytes 786464 | tf_op jit(solution)/shard_map/ppermute | solution.py:57
  64.8 2.0 %mid_back.1 = (f32[512,768]{1,0:T(8,128)S(1)}, bf16[256,768]{1,0:T(8,128)(2,1)S(1)}, bf16[256,768]{1,0:T(8,128)(2,1)S(1)}, f32[8,768]{1,0:T(8,128)S(1)}) custom-call(s32[152]{0:T(256)S(1)} %concatenate.3.refs_0_.ids.ids_ref, bf16[512,768]{1,0:T(8,128)(2,1)S(1)} %pair_two.1.refs_4_.refs_0_, bf16[512,768]{1,0:T(8,128)(2,1)S(1)} %collective-permute-done.5.refs_1_, ...), custom_call_target="tpu_custom_call" | custom-call | bytes 1 | tf_op jit(solution)/shard_map/mid_back/pallas_call | solution.py:737
  71.1 7.2 %attend_back.1 = (bf16[128,768]{1,0:T(8,128)(2,1)S(1)}, bf16[128,768]{1,0:T(8,128)(2,1)S(1)}, bf16[128,768]{1,0:T(8,128)(2,1)S(1)}, bf16[128,768]{1,0:T(8,128)(2...) custom-call(bf16[256,768]{1,0:T(8,128)(2,1)S(1)} %collective-permute, ...), custom_call_target="tpu_custom_call" | custom-call | bytes 1 | tf_op jit(solution)/shard_map/attend_back/pallas_call | solution.py:820
  81.5 3.6 %collective-permute-start.25 = (bf16[2,2,96,768]{3,2,1,0:T(8,128)(2,1)S(1)}, bf16[2,2,96,768]{3,2,1,0:T(8,128)(2,1)S(1)}, u32[]{:S(2)}, u32[]{:S(2)}) collective-permute-start(bf16[2,2,96,768]{3,2,1,0:T(8,128)(2,1)S(1)} %exchange.9.refs_7_.refs_0_), channel_id=1, source_target_pairs={{0,24},{4,28},{8,16},{12,20},{16,8},{20,12},{24,0},{28,4},{1,25},{... | collective-permute-start | bytes 1769480 | tf_op jit(solution)/shard_map/ppermute | solution.py:57
  91.6 5.2 %collective-permute-done.19.refs_1_ = bf16[4,2,24,768]{3,2,1,0:T(8,128)(2,1)S(1)} collective-permute-done((bf16[4,2,24,768]{3,2,1,0:T(8,128)(2,1)S(1)}, bf16[4,2,24,768]{3,2,1,0:T(8,128)(2,1)S(1)}, u32[]{:S(2)}, u32[]{:S(2)}) %collective-permute-start.19) | collective-permute-done | bytes 294944 | tf_op jit(solution)/shard_map/ppermute | solution.py:57
  98.2 7.9 %collective-permute-done.17.refs_2_ = bf16[256,768]{1,0:T(8,128)(2,1)S(1)} collective-permute-done((bf16[256,768]{1,0:T(8,128)(2,1)S(1)}, bf16[256,768]{1,0:T(8,128)(2,1)S(1)}, u32[]{:S(2)}, u32[]{:S(2)}) %collective-permute-start.17) | collective-permute-done | bytes 393248 | tf_op jit(solution)/shard_map/ppermute | solution.py:57
  108.1 3.5 %collective-permute-start.24 = (bf16[2,2,2,24,768]{4,3,2,1,0:T(8,128)(2,1)S(1)}, bf16[2,2,2,24,768]{4,3,2,1,0:T(8,128)(2,1)S(1)}, u32[]{:S(2)}, u32[]{:S(2)}) collective-permute-start(bf16[2,2,2,24,768]{4,3,2,1,0:T(8,128)(2,1)S(1)} %exchange.11.refs_5_.refs_0_), channel_id=1, source_target_pairs={{0,24},{4,28},{8,16},{12,20},{16,8},{20,12},{24,0},{28,4},{1,25},{... | collective-permute-start | bytes 884744 | tf_op jit(solution)/shard_map/ppermute | solution.py:57
  112.9 2.4 %collective-permute-start.30 = (bf16[2,96,768]{2,1,0:T(8,128)(2,1)S(1)}, bf16[2,96,768]{2,1,0:T(8,128)(2,1)S(1)}, u32[]{:S(2)}, u32[]{:S(2)}) collective-permute-start(bf16[2,96,768]{2,1,0:T(8,128)(2,1)S(1)} %get-tuple-element.154.refs_2_.refs_0_), channel_id=1, source_target_pairs={{0,8},{4,12},{8,0},{12,4},{16,24},{20,28},{24,16},{28,20},{1,9},{5... | collective-permute-start | bytes 884744 | tf_op jit(solution)/shard_map/ppermute | solution.py:57
  116.5 3.4 %collective-permute-done.24.refs_1_ = bf16[2,2,2,24,768]{4,3,2,1,0:T(8,128)(2,1)S(1)} collective-permute-done((bf16[2,2,2,24,768]{4,3,2,1,0:T(8,128)(2,1)S(1)}, bf16[2,2,2,24,768]{4,3,2,1,0:T(8,128)(2,1)S(1)}, u32[]{:S(2)}, u32[]{:S(2)}) %collective-permute-start.24) | collective-permute-done | bytes 294944 | tf_op jit(solution)/shard_map/ppermute | solution.py:57
  119.9 3.6 %collective-permute-start.26 = (f32[16,768]{1,0:T(8,128)S(1)}, f32[16,768]{1,0:T(8,128)S(1)}, u32[]{:S(2)}, u32[]{:S(2)}) collective-permute-start(f32[16,768]{1,0:T(8,128)S(1)} %join_sums.3.refs_0_.refs_2_), channel_id=1, source_target_pairs={{0,8},{4,12},{8,0},{12,4},{16,24},{20,28},{24,16},{28,20},{1,9},{5... | collective-permute-start | bytes 147464 | tf_op jit(solution)/shard_map/ppermute | solution.py:57
  126.2 3.0 %collective-permute-start.27 = (f32[24,768]{1,0:T(8,128)S(1)}, f32[24,768]{1,0:T(8,128)S(1)}, u32[]{:S(2)}, u32[]{:S(2)}) collective-permute-start(f32[24,768]{1,0:T(8,128)S(1)} %join_sums.4.refs_4_.refs_0_), channel_id=1, source_target_pairs={{0,16},{4,20},{8,24},{12,28},{16,0},{20,4},{24,8},{28,12},{1,17},{... | collective-permute-start | bytes 221192 | tf_op jit(solution)/shard_map/ppermute | solution.py:57
  143.3 4.0 %table_grad.1 = (f32[768]{0:T(1024)}, f32[768]{0:T(1024)}, f32[768]{0:T(1024)}, f32[768]{0:T(1024)}, f32[768]{0:T(1024)}, /*index=5*/f32[768]{0:T(1024)}, f32[192,1000]{1,0:T(8,128)}) custom-call(s32[152]{0:T(256)S(1)} %concatenate.3.refs_0_.ids.ids_ref, f32[40,768]{1,0:T(8,128)S(1)} %join_sums.5.refs_4_.refs_1_, ...), custom_call_target="tpu_custom_call" | custom-call | bytes 1 | tf_op jit(solution)/shard_map/table_grad/pallas_call | solution.py:962
  147.3 3.0 %collective-permute-done.38.value_ref = bf16[4,96,768]{2,1,0:T(8,128)(2,1)S(1)} collective-permute-done((bf16[4,96,768]{2,1,0:T(8,128)(2,1)S(1)}, bf16[4,96,768]{2,1,0:T(8,128)(2,1)S(1)}, u32[]{:S(2)}, u32[]{:S(2)}) %collective-permute-start.38) | collective-permute-done | bytes 589856 | tf_op jit(solution)/shard_map/ppermute | solution.py:57
  153.6 2.6 %collective-permute-done.36.b_ref = bf16[4,2,24,768]{3,2,1,0:T(8,128)(2,1)S(1)} collective-permute-done((bf16[4,2,24,768]{3,2,1,0:T(8,128)(2,1)S(1)}, bf16[4,2,24,768]{3,2,1,0:T(8,128)(2,1)S(1)}, u32[]{:S(2)}, u32[]{:S(2)}) %collective-permute-start.36) | collective-permute-done | bytes 294944 | tf_op jit(solution)/shard_map/ppermute | solution.py:57
  (111 shorter events, 52.4 us)
Async XLA Ops:
  13.8 20.8 %collective-permute-start.1 = (bf16[512,768]{1,0:T(8,128)(2,1)S(1)}, bf16[512,768]{1,0:T(8,128)(2,1)S(1)}, u32[]{:S(2)}, u32[]{:S(2)}) collective-permute-start(bf16[512,768]{1,0:T(8,128)(2,1)S(1)} %pair_one.1.refs_3_.refs_1_), channel_id=1, source_target_pairs={{0,2},{1,3},{2,0},{3,1},{4,6},{5,7},{6,4},{7,5},{8,10},{9,11},{10,... | collective-permute-start | bytes 2359304 | tf_op jit(solution)/shard_map/ppermute | solution.py:57
  45.3 19.5 %collective-permute-start.5 = (bf16[512,768]{1,0:T(8,128)(2,1)S(1)}, bf16[512,768]{1,0:T(8,128)(2,1)S(1)}, u32[]{:S(2)}, u32[]{:S(2)}) collective-permute-start(bf16[512,768]{1,0:T(8,128)(2,1)S(1)} %pair_two.1.refs_4_.refs_0_), channel_id=1, source_target_pairs={{0,2},{1,3},{2,0},{3,1},{4,6},{5,7},{6,4},{7,5},{8,10},{9,11},{10,... | collective-permute-start | bytes 2359304 | tf_op jit(solution)/shard_map/ppermute | solution.py:57
  47.1 20.4 %collective-permute-start.8 = (bf16[4,96,768]{2,1,0:T(8,128)(2,1)S(1)}, bf16[4,96,768]{2,1,0:T(8,128)(2,1)S(1)}, u32[]{:S(2)}, u32[]{:S(2)}) collective-permute-start(bf16[4,96,768]{2,1,0:T(8,128)(2,1)S(1)} %get-tuple-element.120), channel_id=1, source_target_pairs={{0,4},{4,0},{8,12},{12,8},{16,20},{20,16},{24,28},{28,24},{1,5},{5... | collective-permute-start | bytes 1769480 | tf_op jit(solution)/shard_map/ppermute | solution.py:57
  51.1 16.3 %collective-permute-start.9 = (bf16[4,96,768]{2,1,0:T(8,128)(2,1)S(1)}, bf16[4,96,768]{2,1,0:T(8,128)(2,1)S(1)}, u32[]{:S(2)}, u32[]{:S(2)}) collective-permute-start(bf16[4,96,768]{2,1,0:T(8,128)(2,1)S(1)} %get-tuple-element.121), channel_id=1, source_target_pairs={{0,8},{4,12},{8,0},{12,4},{16,24},{20,28},{24,16},{28,20},{1,9},{5... | collective-permute-start | bytes 1769480 | tf_op jit(solution)/shard_map/ppermute | solution.py:57
  54.9 26.1 %collective-permute-start.4 = (bf16[512,768]{1,0:T(8,128)(2,1)S(1)}, bf16[512,768]{1,0:T(8,128)(2,1)S(1)}, u32[]{:S(2)}, u32[]{:S(2)}) collective-permute-start(bf16[512,768]{1,0:T(8,128)(2,1)S(1)} %get-tuple-element.111), channel_id=1, source_target_pairs={{0,1},{1,0},{2,3},{3,2},{4,5},{5,4},{6,7},{7,6},{8,9},{9,8},{10,11... | collective-permute-start | bytes 2359304 | tf_op jit(solution)/shard_map/ppermute | solution.py:57
  67.7 11.2 %collective-permute-start.10 = (bf16[2,96,768]{2,1,0:T(8,128)(2,1)S(1)}, bf16[2,96,768]{2,1,0:T(8,128)(2,1)S(1)}, u32[]{:S(2)}, u32[]{:S(2)}) collective-permute-start(bf16[2,96,768]{2,1,0:T(8,128)(2,1)S(1)} %get-tuple-element.126), channel_id=1, source_target_pairs={{0,8},{4,12},{8,0},{12,4},{16,24},{20,28},{24,16},{28,20},{1,9},{5... | collective-permute-start | bytes 884744 | tf_op jit(solution)/shard_map/ppermute | solution.py:57
  69.6 9.4 %collective-permute-start.11 = (bf16[2,96,768]{2,1,0:T(8,128)(2,1)S(1)}, bf16[2,96,768]{2,1,0:T(8,128)(2,1)S(1)}, u32[]{:S(2)}, u32[]{:S(2)}) collective-permute-start(bf16[2,96,768]{2,1,0:T(8,128)(2,1)S(1)} %get-tuple-element.128), channel_id=1, source_target_pairs={{0,4},{4,0},{8,12},{12,8},{16,20},{20,16},{24,28},{28,24},{1,5},{5... | collective-permute-start | bytes 884744 | tf_op jit(solution)/shard_map/ppermute | solution.py:57
  81.0 9.1 %collective-permute-start.20 = (bf16[4,2,24,768]{3,2,1,0:T(8,128)(2,1)S(1)}, bf16[4,2,24,768]{3,2,1,0:T(8,128)(2,1)S(1)}, u32[]{:S(2)}, u32[]{:S(2)}) collective-permute-start(bf16[4,2,24,768]{3,2,1,0:T(8,128)(2,1)S(1)} %get-tuple-element.144), channel_id=1, source_target_pairs={{0,8},{4,12},{8,0},{12,4},{16,24},{20,28},{24,16},{28,20},{1,9},{5... | collective-permute-start | bytes 884744 | tf_op jit(solution)/shard_map/ppermute | solution.py:57
  81.5 30.1 %collective-permute-start.25 = (bf16[2,2,96,768]{3,2,1,0:T(8,128)(2,1)S(1)}, bf16[2,2,96,768]{3,2,1,0:T(8,128)(2,1)S(1)}, u32[]{:S(2)}, u32[]{:S(2)}) collective-permute-start(bf16[2,2,96,768]{3,2,1,0:T(8,128)(2,1)S(1)} %exchange.9.refs_7_.refs_0_), channel_id=1, source_target_pairs={{0,24},{4,28},{8,16},{12,20},{16,8},{20,12},{24,0},{28,4},{1,25},{... | collective-permute-start | bytes 1769480 | tf_op jit(solution)/shard_map/ppermute | solution.py:57
  85.6 12.1 %collective-permute-start.18 = (bf16[256,768]{1,0:T(8,128)(2,1)S(1)}, bf16[256,768]{1,0:T(8,128)(2,1)S(1)}, u32[]{:S(2)}, u32[]{:S(2)}) collective-permute-start(bf16[256,768]{1,0:T(8,128)(2,1)S(1)} %get-tuple-element.137.refs_1_), channel_id=1, source_target_pairs={{0,2},{1,3},{2,0},{3,1},{4,6},{5,7},{6,4},{7,5},{8,10},{9,11},{10,... | collective-permute-start | bytes 1179656 | tf_op jit(solution)/shard_map/ppermute | solution.py:57
  88.6 8.2 %collective-permute-start.19 = (bf16[4,2,24,768]{3,2,1,0:T(8,128)(2,1)S(1)}, bf16[4,2,24,768]{3,2,1,0:T(8,128)(2,1)S(1)}, u32[]{:S(2)}, u32[]{:S(2)}) collective-permute-start(bf16[4,2,24,768]{3,2,1,0:T(8,128)(2,1)S(1)} %get-tuple-element.143), channel_id=1, source_target_pairs={{0,4},{4,0},{8,12},{12,8},{16,20},{20,16},{24,28},{28,24},{1,5},{5... | collective-permute-start | bytes 884744 | tf_op jit(solution)/shard_map/ppermute | solution.py:57
  89.2 16.9 %collective-permute-start.17 = (bf16[256,768]{1,0:T(8,128)(2,1)S(1)}, bf16[256,768]{1,0:T(8,128)(2,1)S(1)}, u32[]{:S(2)}, u32[]{:S(2)}) collective-permute-start(bf16[256,768]{1,0:T(8,128)(2,1)S(1)} %get-tuple-element.136.refs_4_.refs_0_), channel_id=1, source_target_pairs={{0,2},{1,3},{2,0},{3,1},{4,6},{5,7},{6,4},{7,5},{8,10},{9,11},{10,... | collective-permute-start | bytes 1179656 | tf_op jit(solution)/shard_map/ppermute | solution.py:57
  90.1 43.6 %collective-permute-start.12 = (bf16[512,768]{1,0:T(8,128)(2,1)S(1)}, bf16[512,768]{1,0:T(8,128)(2,1)S(1)}, u32[]{:S(2)}, u32[]{:S(2)}) collective-permute-start(bf16[512,768]{1,0:T(8,128)(2,1)S(1)} %pair_out.1.refs_5_.refs_1_), channel_id=1, source_target_pairs={{0,2},{1,3},{2,0},{3,1},{4,6},{5,7},{6,4},{7,5},{8,10},{9,11},{10,... | collective-permute-start | bytes 2359304 | tf_op jit(solution)/shard_map/ppermute | solution.py:57
  96.9 11.0 %collective-permute-start.21 = (bf16[2,2,24,768]{3,2,1,0:T(8,128)(2,1)S(1)}, bf16[2,2,24,768]{3,2,1,0:T(8,128)(2,1)S(1)}, u32[]{:S(2)}, u32[]{:S(2)}) collective-permute-start(bf16[2,2,24,768]{3,2,1,0:T(8,128)(2,1)S(1)} %get-tuple-element.150), channel_id=1, source_target_pairs={{0,8},{4,12},{8,0},{12,4},{16,24},{20,28},{24,16},{28,20},{1,9},{5... | collective-permute-start | bytes 442376 | tf_op jit(solution)/shard_map/ppermute | solution.py:57
  97.7 10.3 %collective-permute-start.22 = (bf16[2,2,24,768]{3,2,1,0:T(8,128)(2,1)S(1)}, bf16[2,2,24,768]{3,2,1,0:T(8,128)(2,1)S(1)}, u32[]{:S(2)}, u32[]{:S(2)}) collective-permute-start(bf16[2,2,24,768]{3,2,1,0:T(8,128)(2,1)S(1)} %get-tuple-element.152), channel_id=1, source_target_pairs={{0,4},{4,0},{8,12},{12,8},{16,20},{20,16},{24,28},{28,24},{1,5},{5... | collective-permute-start | bytes 442376 | tf_op jit(solution)/shard_map/ppermute | solution.py:57
  108.1 11.8 %collective-permute-start.24 = (bf16[2,2,2,24,768]{4,3,2,1,0:T(8,128)(2,1)S(1)}, bf16[2,2,2,24,768]{4,3,2,1,0:T(8,128)(2,1)S(1)}, u32[]{:S(2)}, u32[]{:S(2)}) collective-permute-start(bf16[2,2,2,24,768]{4,3,2,1,0:T(8,128)(2,1)S(1)} %exchange.11.refs_5_.refs_0_), channel_id=1, source_target_pairs={{0,24},{4,28},{8,16},{12,20},{16,8},{20,12},{24,0},{28,4},{1,25},{... | collective-permute-start | bytes 884744 | tf_op jit(solution)/shard_map/ppermute | solution.py:57
  111.8 12.6 %collective-permute-start.31 = (bf16[2,96,768]{2,1,0:T(8,128)(2,1)S(1)}, bf16[2,96,768]{2,1,0:T(8,128)(2,1)S(1)}, u32[]{:S(2)}, u32[]{:S(2)}) collective-permute-start(bf16[2,96,768]{2,1,0:T(8,128)(2,1)S(1)} %get-tuple-element.157.refs_2_), channel_id=1, source_target_pairs={{0,4},{4,0},{8,12},{12,8},{16,20},{20,16},{24,28},{28,24},{1,5},{5... | collective-permute-start | bytes 884744 | tf_op jit(solution)/shard_map/ppermute | solution.py:57
  112.9 13.3 %collective-permute-start.30 = (bf16[2,96,768]{2,1,0:T(8,128)(2,1)S(1)}, bf16[2,96,768]{2,1,0:T(8,128)(2,1)S(1)}, u32[]{:S(2)}, u32[]{:S(2)}) collective-permute-start(bf16[2,96,768]{2,1,0:T(8,128)(2,1)S(1)} %get-tuple-element.154.refs_2_.refs_0_), channel_id=1, source_target_pairs={{0,8},{4,12},{8,0},{12,4},{16,24},{20,28},{24,16},{28,20},{1,9},{5... | collective-permute-start | bytes 884744 | tf_op jit(solution)/shard_map/ppermute | solution.py:57
  126.2 11.1 %collective-permute-start.33 = (bf16[512,768]{1,0:T(8,128)(2,1)S(1)}, bf16[512,768]{1,0:T(8,128)(2,1)S(1)}, u32[]{:S(2)}, u32[]{:S(2)}) collective-permute-start(bf16[512,768]{1,0:T(8,128)(2,1)S(1)} %get-tuple-element.153.refs_4_.own_ref), channel_id=1, source_target_pairs={{0,1},{1,0},{2,3},{3,2},{4,5},{5,4},{6,7},{7,6},{8,9},{9,8},{10,11... | collective-permute-start | bytes 2359304 | tf_op jit(solution)/shard_map/ppermute | solution.py:57
  126.2 7.5 %collective-permute-start.27 = (f32[24,768]{1,0:T(8,128)S(1)}, f32[24,768]{1,0:T(8,128)S(1)}, u32[]{:S(2)}, u32[]{:S(2)}) collective-permute-start(f32[24,768]{1,0:T(8,128)S(1)} %join_sums.4.refs_4_.refs_0_), channel_id=1, source_target_pairs={{0,16},{4,20},{8,24},{12,28},{16,0},{20,4},{24,8},{28,12},{1,17},{... | collective-permute-start | bytes 221192 | tf_op jit(solution)/shard_map/ppermute | solution.py:57
  134.1 16.2 %collective-permute-start.38 = (bf16[4,96,768]{2,1,0:T(8,128)(2,1)S(1)}, bf16[4,96,768]{2,1,0:T(8,128)(2,1)S(1)}, u32[]{:S(2)}, u32[]{:S(2)}) collective-permute-start(bf16[4,96,768]{2,1,0:T(8,128)(2,1)S(1)} %get-tuple-element.161.value_ref), channel_id=1, source_target_pairs={{0,8},{4,12},{8,0},{12,4},{16,24},{20,28},{24,16},{28,20},{1,9},{5... | collective-permute-start | bytes 1769480 | tf_op jit(solution)/shard_map/ppermute | solution.py:57
  134.2 17.7 %collective-permute-start.37 = (bf16[4,96,768]{2,1,0:T(8,128)(2,1)S(1)}, bf16[4,96,768]{2,1,0:T(8,128)(2,1)S(1)}, u32[]{:S(2)}, u32[]{:S(2)}) collective-permute-start(bf16[4,96,768]{2,1,0:T(8,128)(2,1)S(1)} %get-tuple-element.158.refs_4_.value_ref), channel_id=1, source_target_pairs={{0,4},{4,0},{8,12},{12,8},{16,20},{20,16},{24,28},{28,24},{1,5},{5... | collective-permute-start | bytes 1769480 | tf_op jit(solution)/shard_map/ppermute | solution.py:57
  135.3 20.9 %collective-permute-start.36 = (bf16[4,2,24,768]{3,2,1,0:T(8,128)(2,1)S(1)}, bf16[4,2,24,768]{3,2,1,0:T(8,128)(2,1)S(1)}, u32[]{:S(2)}, u32[]{:S(2)}) collective-permute-start(bf16[4,2,24,768]{3,2,1,0:T(8,128)(2,1)S(1)} %get-tuple-element.160.b_ref), channel_id=1, source_target_pairs={{0,8},{4,12},{8,0},{12,4},{16,24},{20,28},{24,16},{28,20},{1,9},{5... | collective-permute-start | bytes 884744 | tf_op jit(solution)/shard_map/ppermute | solution.py:57
  137.2 19.0 %collective-permute-start.35 = (bf16[4,2,24,768]{3,2,1,0:T(8,128)(2,1)S(1)}, bf16[4,2,24,768]{3,2,1,0:T(8,128)(2,1)S(1)}, u32[]{:S(2)}, u32[]{:S(2)}) collective-permute-start(bf16[4,2,24,768]{3,2,1,0:T(8,128)(2,1)S(1)} %get-tuple-element.159.refs_0_.a_ref), channel_id=1, source_target_pairs={{0,4},{4,0},{8,12},{12,8},{16,20},{20,16},{24,28},{28,24},{1,5},{5... | collective-permute-start | bytes 884744 | tf_op jit(solution)/shard_map/ppermute | solution.py:57
  (22 other events, 129.1 us)
